TPU v7x, 32 devices: a whole 2x2x4 slice. The times are simulated.
32 devices in a mesh: grp: 2 (over y), tile: 16 (over z, x, core).
Axes of the slice: x: 2, y: 2, z: 4, core: 2. Of those that a mesh axis runs over, the one named last changes fastest.
Arguments:
- rhs: float32 [256, 28672], P('grp', 'tile'), parts along dimension 0, may hold values from -4.5 to 4.5
- mass_diag: float32 [28672], P('tile'), may hold values from 0.1 to 2
- edge_heads: int32 [114688], P('tile'), may hold values from 128 to 1919
- edge_tails: int32 [114688], P('tile'), may hold values from 0 to 2047
- edge_weight: float32 [114688], P('tile'), may hold values from 0.5 to 2
- local_inverse: bfloat16 [32768, 2048], P('tile'), may hold values from -0.5 to 1
- coarse_vec: float32 [28672], P('tile'), may hold values from 0.25 to 1.75
- coarse_inv: float32 [16, 16], replicated, may hold values from -0.000558035714 to 0.002232143
Outputs:
- solution: float32 [256, 28672], P('grp', 'tile'), parts along dimension 0
- residual: float32 [256, 28672], P('grp', 'tile'), parts along dimension 0
There are 2 independent parts, one for each index of `grp`. A program takes and returns all parts, laid end to end along the dimension named above; an argument that names none is the same for every part. Nothing has to cross between parts.
All inputs are finite; a program needn't handle non-finite values.
Results may differ from a plain program's by a relative error of at most 0.015.
Values may be sent and summed in bfloat16 or wider, within the bound.
No kernel may reach another device: no remote copies, remote signals or barrier semaphores. Data moves between devices by JAX's collectives and lax.ppermute only.
A program may use at most 128 MiB of HBM per device.

v0:
```python
import jax
import jax.numpy as jnp
from jax import lax
from jax.sharding import PartitionSpec as P

SUB = 2048
STRIP = 128
ITERS = 2


def with_halo(block, sides, width):
    for axis, dim in sides:
        count = lax.axis_size(axis)
        forward = [(i, i + 1) for i in range(count - 1)]
        backward = [(target, source) for source, target in forward]
        low = lax.ppermute(
            lax.slice_in_dim(block, block.shape[dim] - width, None, axis=dim), axis, forward
        )
        high = lax.ppermute(lax.slice_in_dim(block, 0, width, axis=dim), axis, backward)
        block = jnp.concatenate([low, block, high], axis=dim)
    return block


def send_back(contrib):
    rims = jnp.concatenate([contrib[:, :STRIP], contrib[:, -STRIP:]], axis=1)
    arrived = with_halo(rims.astype(jnp.bfloat16), (("tile", 1),), STRIP).astype(rims.dtype)
    owned = contrib[:, STRIP:-STRIP]
    lower = owned[:, :STRIP] + arrived[:, :STRIP]
    upper = owned[:, -STRIP:] + arrived[:, -STRIP:]
    return jnp.concatenate([lower, owned[:, STRIP:-STRIP], upper], axis=1)


def build_stiffness(edge_heads, edge_tails, edge_weight):
    rows_idx = jnp.concatenate([edge_heads, edge_tails, edge_heads, edge_tails])
    cols_idx = jnp.concatenate([edge_heads, edge_tails, edge_tails, edge_heads])
    values = jnp.concatenate([edge_weight, edge_weight, -edge_weight, -edge_weight])
    return jnp.zeros((SUB, SUB), jnp.float32).at[rows_idx, cols_idx].add(values)


def operate(vector, mass_diag, stiffness):
    widened = with_halo(vector, (("tile", 1),), STRIP)
    contrib = jnp.dot(widened, stiffness, precision=lax.Precision.HIGHEST)
    return mass_diag * vector + send_back(contrib)


def precondition(resid, local_inverse, coarse_vec, coarse_inv):
    widened = with_halo(resid.astype(jnp.bfloat16), (("tile", 1),), STRIP)
    local = jnp.dot(widened, local_inverse, preferred_element_type=jnp.float32)
    schwarz = send_back(local)
    restricted = jnp.sum(resid * coarse_vec, axis=1)
    mine_index = lax.axis_index("tile")
    every = lax.all_gather(restricted[:, None], "tile", axis=1, tiled=True)
    column = lax.dynamic_slice_in_dim(coarse_inv, mine_index, 1, 1)
    mine = jnp.dot(every, column, precision=lax.Precision.HIGHEST)
    return schwarz + mine * coarse_vec


def inner(left, right):
    return jnp.sum(left * right, axis=1)


def both_dots(resid, zvec, image):
    return lax.psum((inner(resid, zvec), inner(image, zvec)), "tile")


def shards(
    rhs, mass_diag, edge_heads, edge_tails, edge_weight, local_inverse, coarse_vec, coarse_inv
):
    stiffness = build_stiffness(edge_heads, edge_tails, edge_weight)
    solution = jnp.zeros_like(rhs)
    resid = rhs
    zvec = precondition(resid, local_inverse, coarse_vec, coarse_inv)
    image = operate(zvec, mass_diag, stiffness)
    gamma, delta = both_dots(resid, zvec, image)
    alpha = gamma / delta
    direction, along = (zvec, image)
    for step in range(ITERS):
        solution = solution + alpha[:, None] * direction
        resid = resid - alpha[:, None] * along
        if step + 1 < ITERS:
            zvec = precondition(resid, local_inverse, coarse_vec, coarse_inv)
            image = operate(zvec, mass_diag, stiffness)
            gamma_next, delta = both_dots(resid, zvec, image)
            ratio = gamma_next / gamma
            alpha = gamma_next / (delta - ratio * gamma_next / alpha)
            direction = zvec + ratio[:, None] * direction
            along = image + ratio[:, None] * along
            gamma = gamma_next
    return (solution, resid)


def solution(mesh):
    return jax.shard_map(
        shards,
        mesh=mesh,
        in_specs=(
            P("grp", "tile"),
            P("tile"),
            P("tile"),
            P("tile"),
            P("tile"),
            P("tile", None),
            P("tile"),
            P(),
        ),
        out_specs=(P("grp", "tile"), P("grp", "tile")),
        check_vma=False,
    )
```

profile of v0, /device:TPU:0, one launch (start us, length us, event | category | flops | bytes accessed | tf_op | source)
XLA Modules:
  0.0 372.3 jit_solution(4083867110889075399)
XLA Ops:
  0.7 1.7 multiply_reduce_fusion.5
  2.4 1.3 collective-permute-start.1
  3.7 3.0 collective-permute-start
  6.7 1.1 compare_select_fusion.1
  8.3 1.1 multiply_reduce_fusion.6
  9.6 23.1 %all-gather = f32[16,1,128]{2,1,0:T(1,128)S(1)} all-gather(f32[1,1,128]{2,1,0:T(1,128)S(1)} %bitcast.29), channel_id=1, replica_groups=mesh['grp'=2,'tile'=16] {'tile'}, dimensions={0}, use_global_device_ids=true | all-gather | bytes 8704 | tf_op jit(solution)/shard_map/all_gather | solution.py:52
  32.7 4.7 %fusion.40 = (bf16[128,2048]{1,0:T(8,128)(2,1)S(1)}, f32[128,2048]{1,0:T(8,128)S(1)}) fusion(bf16[2048,2048]{1,0:T(8,128)(2,1)} %param.13, bf16[128,128]{1,0:T(8,128)(2,1)S(1)} %collective-permute-done.1, bf16[128,1792]{1,0:T(8,128)(2,1)S(1)} %get-tuple-element.29, bf16[128,128]{1,0:T(8,128)(2,1)S(1)} %collective-permute-done), kind=kOutput, calls=%fused_computation.86 | convolution fusion | flops 1075576832 | bytes 10485760 | tf_op jit(solution)/shard_map/dot_general | solution.py:48
  37.5 1.3 collective-permute-start.3
  38.8 3.0 collective-permute-start.2
  42.9 1.3 collective-permute-start.5
  44.2 4.3 %collective-permute-start.4 = (f32[128,128]{1,0:T(8,128)S(1)}, f32[128,128]{1,0:T(8,128)S(1)}, u32[]{:S(2)}, u32[]{:S(2)}) collective-permute-start(f32[128,128]{1,0:T(8,128)S(1)} %get-tuple-element.26), channel_id=1, source_target_pairs={{0,1},{1,2},{2,3},{3,4},{4,5},{5,6},{6,7},{7,8},{8,9},{9,10},{10,1... | collective-permute-start | bytes 196616 | tf_op jit(solution)/shard_map/ppermute | solution.py:16
  48.5 156.5 %scatter_custom_fusion = f32[4194304]{0:T(1024)} fusion(s32[28672]{0:T(1024)S(1)} %broadcast_select_fusion, f32[28672]{0:T(1024)S(1)} %pad_maximum_fusion, f32[]{:T(128)} %constant.5.clone.1), kind=kCustom, calls=%fused_computation.1 | custom fusion | flops 28672 | bytes 16777220
  205.0 18.0 %reshape.335 = f32[2048,2048]{1,0:T(8,128)} reshape(f32[4194304]{0:T(1024)} %scatter_custom_fusion) | data formatting | bytes 33554432 | tf_op jit(solution)/shard_map/scatter-add | solution.py:37
  223.0 12.8 %fusion.41 = (bf16[128,2048]{1,0:T(8,128)(2,1)S(1)}, f32[128,2048]{1,0:T(8,128)S(1)}) fusion(f32[2048,2048]{1,0:T(8,128)} %reshape.335, f32[128,128]{1,0:T(8,128)S(1)} %collective-permute-done.5, f32[128,1792]{1,0:T(8,128)S(1)} %maximum_add_fusion, f32[128,128]{1,0:T(8,128)S(1)} %collective-permute-done.4), kind=kOutput, calls=%fused_computation.87 | convolution fusion | flops 6443237376 | bytes 19398656 | tf_op jit(solution)/shard_map/dot_general | solution.py:42
  235.8 1.3 collective-permute-start.7
  237.1 5.0 %collective-permute-start.6 = (bf16[128,128]{1,0:T(8,128)(2,1)S(1)}, bf16[128,128]{1,0:T(8,128)(2,1)S(1)}, u32[]{:S(2)}, u32[]{:S(2)}) collective-permute-start(bf16[128,128]{1,0:T(8,128)(2,1)S(1)} %get-tuple-element.34), channel_id=1, source_target_pairs={{0,1},{1,2},{2,3},{3,4},{4,5},{5,6},{6,7},{7,8},{8,9},{9,10},{10,1... | collective-permute-start | bytes 98312 | tf_op jit(solution)/shard_map/ppermute | solution.py:16
  243.2 31.4 %all-reduce.1 = (f32[128]{0:T(128)S(1)}, f32[128]{0:T(128)S(1)}) all-reduce(f32[128]{0:T(128)S(1)} %get-tuple-element.5, f32[128]{0:T(128)S(1)} %get-tuple-element.4), channel_id=1, replica_groups=mesh['grp'=2,'tile'=16] {'tile'}, use_global_device_ids=true, to_apply=%region_2.0 | all-reduce | flops 256 | bytes 2048 | tf_op jit(solution)/shard_map/psum | solution.py:63
  275.1 1.2 multiply_reduce_fusion.2
  276.4 1.3 collective-permute-start.9
  277.7 3.0 collective-permute-start.8
  280.7 17.1 %all-gather.1 = f32[16,1,128]{2,1,0:T(1,128)S(1)} all-gather(f32[1,1,128]{2,1,0:T(1,128)S(1)} %bitcast.30), channel_id=1, replica_groups=mesh['grp'=2,'tile'=16] {'tile'}, dimensions={0}, use_global_device_ids=true | all-gather | bytes 8704 | tf_op jit(solution)/shard_map/all_gather | solution.py:52
  297.9 4.7 %fusion.42 = (bf16[128,2048]{1,0:T(8,128)(2,1)S(1)}, f32[128,2048]{1,0:T(8,128)S(1)}) fusion(bf16[2048,2048]{1,0:T(8,128)(2,1)} %param.13, bf16[128,128]{1,0:T(8,128)(2,1)S(1)} %collective-permute-done.9, bf16[128,1792]{1,0:T(8,128)(2,1)S(1)} %convert_element_type.25, bf16[128,128]{1,0:T(8,128)(2,1)S(1)} %collective-permute-done.8), kind=kOutput, calls=%fused_computation.88 | convolution fusion | flops 1075576832 | bytes 10485760 | tf_op jit(solution)/shard_map/dot_general | solution.py:48
  302.6 1.3 collective-permute-start.11
  303.9 3.0 collective-permute-start.10
  308.0 1.3 collective-permute-start.13
  309.3 4.3 %collective-permute-start.12 = (f32[128,128]{1,0:T(8,128)S(1)}, f32[128,128]{1,0:T(8,128)S(1)}, u32[]{:S(2)}, u32[]{:S(2)}) collective-permute-start(f32[128,128]{1,0:T(8,128)S(1)} %get-tuple-element.24), channel_id=1, source_target_pairs={{0,1},{1,2},{2,3},{3,4},{4,5},{5,6},{6,7},{7,8},{8,9},{9,10},{10,1... | collective-permute-start | bytes 196616 | tf_op jit(solution)/shard_map/ppermute | solution.py:16
  313.6 0.9 collective-permute-done.12
  314.5 12.7 %fusion.43 = (bf16[128,2048]{1,0:T(8,128)(2,1)S(1)}, f32[128,2048]{1,0:T(8,128)S(1)}) fusion(f32[2048,2048]{1,0:T(8,128)} %reshape.335, f32[128,128]{1,0:T(8,128)S(1)} %collective-permute-done.13, f32[128,1792]{1,0:T(8,128)S(1)} %maximum_add_fusion.2, f32[128,128]{1,0:T(8,128)S(1)} %collective-permute-done.12), kind=kOutput, calls=%fused_computation.89 | convolution fusion | flops 6443237376 | bytes 19398656 | tf_op jit(solution)/shard_map/dot_general | solution.py:42
  327.2 1.3 collective-permute-start.15
  328.5 5.9 %collective-permute-start.14 = (bf16[128,128]{1,0:T(8,128)(2,1)S(1)}, bf16[128,128]{1,0:T(8,128)(2,1)S(1)}, u32[]{:S(2)}, u32[]{:S(2)}) collective-permute-start(bf16[128,128]{1,0:T(8,128)(2,1)S(1)} %get-tuple-element.30), channel_id=1, source_target_pairs={{0,1},{1,2},{2,3},{3,4},{4,5},{5,6},{6,7},{7,8},{8,9},{9,10},{10,1... | collective-permute-start | bytes 98312 | tf_op jit(solution)/shard_map/ppermute | solution.py:16
  335.9 32.6 %all-reduce = (f32[128]{0:T(128)}, f32[128]{0:T(128)}) all-reduce(f32[128]{0:T(128)S(1)} %get-tuple-element.3, f32[128]{0:T(128)S(1)} %get-tuple-element.2), channel_id=1, replica_groups=mesh['grp'=2,'tile'=16] {'tile'}, use_global_device_ids=true, to_apply=%region_8.0 | all-reduce | flops 256 | bytes 2048 | tf_op jit(solution)/shard_map/psum | solution.py:63
  369.2 3.1 multiply_subtract_fusion
  (75 shorter events, 6.5 us)
Async XLA Ops:
  0.6 8.8 %copy-start = (f32[16,16]{1,0:T(8,128)S(1)}, f32[16,16]{1,0:T(8,128)}, u32[]{:S(2)}) copy-start(f32[16,16]{1,0:T(8,128)} %param.15) | copy-start | bytes 3076
  0.6 42.1 %copy-start.7 = (f32[1792]{0:T(1024)S(1)}, f32[1792]{0:T(1024)}, u32[]{:S(2)}) copy-start(f32[1792]{0:T(1024)} %param.14) | copy-start | bytes 21508
  0.7 41.3 %copy-start.10 = (f32[7168]{0:T(1024)S(1)}, f32[7168]{0:T(1024)}, u32[]{:S(2)}) copy-start(f32[7168]{0:T(1024)} %param.12) | copy-start | bytes 86020
  2.4 30.4 %collective-permute-start.1 = (bf16[128,128]{1,0:T(8,128)(2,1)S(1)}, bf16[128,128]{1,0:T(8,128)(2,1)S(1)}, u32[]{:S(2)}, u32[]{:S(2)}) collective-permute-start(bf16[128,128]{1,0:T(8,128)(2,1)S(1)} %get-tuple-element.41), channel_id=1, source_target_pairs={{1,0},{2,1},{3,2},{4,3},{5,4},{6,5},{7,6},{8,7},{9,8},{10,9},{11,1... | collective-permute-start | bytes 98312 | tf_op jit(solution)/shard_map/ppermute | solution.py:19
  3.7 29.1 %collective-permute-start = (bf16[128,128]{1,0:T(8,128)(2,1)S(1)}, bf16[128,128]{1,0:T(8,128)(2,1)S(1)}, u32[]{:S(2)}, u32[]{:S(2)}) collective-permute-start(bf16[128,128]{1,0:T(8,128)(2,1)S(1)} %get-tuple-element.40), channel_id=1, source_target_pairs={{0,1},{1,2},{2,3},{3,4},{4,5},{5,6},{6,7},{7,8},{8,9},{9,10},{10,1... | collective-permute-start | bytes 98312 | tf_op jit(solution)/shard_map/ppermute | solution.py:16
  9.6 33.1 %copy-start.11 = (f32[16]{0:T(128)}, f32[16]{0:T(128)S(1)}, u32[]{:S(2)}) copy-start(f32[16]{0:T(128)S(1)} %dynamic-slice_reduce_fusion) | copy-start | bytes 196
  37.5 4.6 %collective-permute-start.3 = (bf16[128,128]{1,0:T(8,128)(2,1)S(1)}, bf16[128,128]{1,0:T(8,128)(2,1)S(1)}, u32[]{:S(2)}, u32[]{:S(2)}) collective-permute-start(bf16[128,128]{1,0:T(8,128)(2,1)S(1)} %get-tuple-element.37), channel_id=1, source_target_pairs={{1,0},{2,1},{3,2},{4,3},{5,4},{6,5},{7,6},{8,7},{9,8},{10,9},{11,1... | collective-permute-start | bytes 98312 | tf_op jit(solution)/shard_map/ppermute | solution.py:19
  38.8 3.9 %collective-permute-start.2 = (bf16[128,128]{1,0:T(8,128)(2,1)S(1)}, bf16[128,128]{1,0:T(8,128)(2,1)S(1)}, u32[]{:S(2)}, u32[]{:S(2)}) collective-permute-start(bf16[128,128]{1,0:T(8,128)(2,1)S(1)} %get-tuple-element.36), channel_id=1, source_target_pairs={{0,1},{1,2},{2,3},{3,4},{4,5},{5,6},{6,7},{7,8},{8,9},{9,10},{10,1... | collective-permute-start | bytes 98312 | tf_op jit(solution)/shard_map/ppermute | solution.py:16
  42.9 180.1 %collective-permute-start.5 = (f32[128,128]{1,0:T(8,128)S(1)}, f32[128,128]{1,0:T(8,128)S(1)}, u32[]{:S(2)}, u32[]{:S(2)}) collective-permute-start(f32[128,128]{1,0:T(8,128)S(1)} %get-tuple-element.27), channel_id=1, source_target_pairs={{1,0},{2,1},{3,2},{4,3},{5,4},{6,5},{7,6},{8,7},{9,8},{10,9},{11,1... | collective-permute-start | bytes 196616 | tf_op jit(solution)/shard_map/ppermute | solution.py:19
  44.2 178.8 %collective-permute-start.4 = (f32[128,128]{1,0:T(8,128)S(1)}, f32[128,128]{1,0:T(8,128)S(1)}, u32[]{:S(2)}, u32[]{:S(2)}) collective-permute-start(f32[128,128]{1,0:T(8,128)S(1)} %get-tuple-element.26), channel_id=1, source_target_pairs={{0,1},{1,2},{2,3},{3,4},{4,5},{5,6},{6,7},{7,8},{8,9},{9,10},{10,1... | collective-permute-start | bytes 196616 | tf_op jit(solution)/shard_map/ppermute | solution.py:16
  223.0 19.9 %copy-start.1 = (f32[128,1792]{1,0:T(8,128)S(1)}, f32[128,1792]{1,0:T(8,128)}, u32[]{:S(2)}) copy-start(f32[128,1792]{1,0:T(8,128)} %param.8) | copy-start | bytes 2752516
  223.0 19.9 %copy-start.8 = (f32[1792]{0:T(1024)S(1)}, f32[1792]{0:T(1024)}, u32[]{:S(2)}) copy-start(f32[1792]{0:T(1024)} %param.9) | copy-start | bytes 21508
  235.8 6.4 %collective-permute-start.7 = (bf16[128,128]{1,0:T(8,128)(2,1)S(1)}, bf16[128,128]{1,0:T(8,128)(2,1)S(1)}, u32[]{:S(2)}, u32[]{:S(2)}) collective-permute-start(bf16[128,128]{1,0:T(8,128)(2,1)S(1)} %get-tuple-element.35), channel_id=1, source_target_pairs={{1,0},{2,1},{3,2},{4,3},{5,4},{6,5},{7,6},{8,7},{9,8},{10,9},{11,1... | collective-permute-start | bytes 98312 | tf_op jit(solution)/shard_map/ppermute | solution.py:19
  237.1 5.7 %collective-permute-start.6 = (bf16[128,128]{1,0:T(8,128)(2,1)S(1)}, bf16[128,128]{1,0:T(8,128)(2,1)S(1)}, u32[]{:S(2)}, u32[]{:S(2)}) collective-permute-start(bf16[128,128]{1,0:T(8,128)(2,1)S(1)} %get-tuple-element.34), channel_id=1, source_target_pairs={{0,1},{1,2},{2,3},{3,4},{4,5},{5,6},{6,7},{7,8},{8,9},{9,10},{10,1... | collective-permute-start | bytes 98312 | tf_op jit(solution)/shard_map/ppermute | solution.py:16
  242.8 31.7 %copy-start.3 = (f32[128,128]{1,0:T(8,128)}, f32[128,128]{1,0:T(8,128)S(1)}, u32[]{:S(2)}) copy-start(f32[128,128]{1,0:T(8,128)S(1)} %get-tuple-element.20) | copy-start | bytes 196612
  242.8 31.7 %copy-start.4 = (f32[128,128]{1,0:T(8,128)}, f32[128,128]{1,0:T(8,128)S(1)}, u32[]{:S(2)}) copy-start(f32[128,128]{1,0:T(8,128)S(1)} %get-tuple-element.21) | copy-start | bytes 196612
  274.5 0.5 copy-start.13
  274.5 0.5 copy-start.14
  275.1 22.8 %copy-start.12 = (f32[128]{0:T(128)}, f32[128]{0:T(128)S(1)}, u32[]{:S(2)}) copy-start(f32[128]{0:T(128)S(1)} %div.12) | copy-start | bytes 1540
  276.4 21.5 %collective-permute-start.9 = (bf16[128,128]{1,0:T(8,128)(2,1)S(1)}, bf16[128,128]{1,0:T(8,128)(2,1)S(1)}, u32[]{:S(2)}, u32[]{:S(2)}) collective-permute-start(bf16[128,128]{1,0:T(8,128)(2,1)S(1)} %get-tuple-element.39), channel_id=1, source_target_pairs={{1,0},{2,1},{3,2},{4,3},{5,4},{6,5},{7,6},{8,7},{9,8},{10,9},{11,1... | collective-permute-start | bytes 98312 | tf_op jit(solution)/shard_map/ppermute | solution.py:19
  277.7 20.2 %collective-permute-start.8 = (bf16[128,128]{1,0:T(8,128)(2,1)S(1)}, bf16[128,128]{1,0:T(8,128)(2,1)S(1)}, u32[]{:S(2)}, u32[]{:S(2)}) collective-permute-start(bf16[128,128]{1,0:T(8,128)(2,1)S(1)} %get-tuple-element.38), channel_id=1, source_target_pairs={{0,1},{1,2},{2,3},{3,4},{4,5},{5,6},{6,7},{7,8},{8,9},{9,10},{10,1... | collective-permute-start | bytes 98312 | tf_op jit(solution)/shard_map/ppermute | solution.py:16
  302.6 32.8 %copy-start.9 = (f32[1792]{0:T(1024)S(1)}, f32[1792]{0:T(1024)}, u32[]{:S(2)}) copy-start(f32[1792]{0:T(1024)} %param.9) | copy-start | bytes 21508
  302.6 5.2 %collective-permute-start.11 = (bf16[128,128]{1,0:T(8,128)(2,1)S(1)}, bf16[128,128]{1,0:T(8,128)(2,1)S(1)}, u32[]{:S(2)}, u32[]{:S(2)}) collective-permute-start(bf16[128,128]{1,0:T(8,128)(2,1)S(1)} %get-tuple-element.33), channel_id=1, source_target_pairs={{1,0},{2,1},{3,2},{4,3},{5,4},{6,5},{7,6},{8,7},{9,8},{10,9},{11,1... | collective-permute-start | bytes 98312 | tf_op jit(solution)/shard_map/ppermute | solution.py:19
  303.9 3.9 %collective-permute-start.10 = (bf16[128,128]{1,0:T(8,128)(2,1)S(1)}, bf16[128,128]{1,0:T(8,128)(2,1)S(1)}, u32[]{:S(2)}, u32[]{:S(2)}) collective-permute-start(bf16[128,128]{1,0:T(8,128)(2,1)S(1)} %get-tuple-element.32), channel_id=1, source_target_pairs={{0,1},{1,2},{2,3},{3,4},{4,5},{5,6},{6,7},{7,8},{8,9},{9,10},{10,1... | collective-permute-start | bytes 98312 | tf_op jit(solution)/shard_map/ppermute | solution.py:16
  308.0 5.6 %collective-permute-start.13 = (f32[128,128]{1,0:T(8,128)S(1)}, f32[128,128]{1,0:T(8,128)S(1)}, u32[]{:S(2)}, u32[]{:S(2)}) collective-permute-start(f32[128,128]{1,0:T(8,128)S(1)} %get-tuple-element.25), channel_id=1, source_target_pairs={{1,0},{2,1},{3,2},{4,3},{5,4},{6,5},{7,6},{8,7},{9,8},{10,9},{11,1... | collective-permute-start | bytes 196616 | tf_op jit(solution)/shard_map/ppermute | solution.py:19
  309.3 5.2 %collective-permute-start.12 = (f32[128,128]{1,0:T(8,128)S(1)}, f32[128,128]{1,0:T(8,128)S(1)}, u32[]{:S(2)}, u32[]{:S(2)}) collective-permute-start(f32[128,128]{1,0:T(8,128)S(1)} %get-tuple-element.24), channel_id=1, source_target_pairs={{0,1},{1,2},{2,3},{3,4},{4,5},{5,6},{6,7},{7,8},{8,9},{9,10},{10,1... | collective-permute-start | bytes 196616 | tf_op jit(solution)/shard_map/ppermute | solution.py:16
  327.2 7.2 %collective-permute-start.15 = (bf16[128,128]{1,0:T(8,128)(2,1)S(1)}, bf16[128,128]{1,0:T(8,128)(2,1)S(1)}, u32[]{:S(2)}, u32[]{:S(2)}) collective-permute-start(bf16[128,128]{1,0:T(8,128)(2,1)S(1)} %get-tuple-element.31), channel_id=1, source_target_pairs={{1,0},{2,1},{3,2},{4,3},{5,4},{6,5},{7,6},{8,7},{9,8},{10,9},{11,1... | collective-permute-start | bytes 98312 | tf_op jit(solution)/shard_map/ppermute | solution.py:19
  328.5 6.7 %collective-permute-start.14 = (bf16[128,128]{1,0:T(8,128)(2,1)S(1)}, bf16[128,128]{1,0:T(8,128)(2,1)S(1)}, u32[]{:S(2)}, u32[]{:S(2)}) collective-permute-start(bf16[128,128]{1,0:T(8,128)(2,1)S(1)} %get-tuple-element.30), channel_id=1, source_target_pairs={{0,1},{1,2},{2,3},{3,4},{4,5},{5,6},{6,7},{7,8},{8,9},{9,10},{10,1... | collective-permute-start | bytes 98312 | tf_op jit(solution)/shard_map/ppermute | solution.py:16
  334.4 0.9 copy-start.2
  335.2 0.6 copy-start.5
  335.2 0.7 copy-start.6
where the time goes:
time: 374 us; the launch traced here: 372 us
  other arithmetic  167 us (45%)
  blocking collectives  104 us (28%)
  starting transfers between devices  41.9 us (11%)
  matrix products  35.9 us (10%)
  local copies, waits for them, and re-layouts  19.4 us (5%)
    unnamed x4, other arithmetic  158 us
    psum x2, blocking collectives, both_dots(): return lax.psum((inner(resid, zvec), inner(image, zvec)), 'tile')  64 us
    all_gather x2, blocking collectives, precondition(): every = lax.all_gather(restricted[:, None], 'tile', axis=1, tiled=True)  40.3 us
    ppermute x8, starting transfers between devices, with_halo(): lax.ppermute(lax.slice_in_dim(block, block.shape[dim] - width, None, axis...  31.6 us
    dot_general x2, matrix products, operate(): contrib = jnp.dot(widened, stiffness, precision=lax.Precision.HIGHEST)  25.5 us
    scatter-add x1, local copies, waits for them, and re-layouts, build_stiffness(): return jnp.zeros((SUB, SUB), jnp.float32).at[rows_idx, cols_idx].add(values)  18 us
    ppermute x8, starting transfers between devices, with_halo(): lax.ppermute(lax.slice_in_dim(block, 0, width, axis=dim), axis, backward)  10.3 us
    dot_general x2, matrix products, precondition(): local = jnp.dot(widened, local_inverse, preferred_element_type=jnp.float32)  9.43 us
  transfers between devices with their start and end apart: 16, of which 4 were waited for; matrix products, arithmetic and copies ran while one was open for 48% of the time, Pallas kernels for 0%

commit v1 on v0

v1 whole, which is shorter than its diff:
```python
import functools

import jax
import jax.numpy as jnp
from jax import lax
from jax.experimental import pallas as pl
from jax.experimental.pallas import tpu as pltpu
from jax.sharding import PartitionSpec as P

STRIP = 128
LANES = 128
GROUP = 16
F32 = jnp.float32
BF16 = jnp.bfloat16
NN = (((1,), (0,)), ((), ()))
NT = (((1,), (1,)), ((), ()))
TN = (((0,), (0,)), ((), ()))
HIGHEST = lax.Precision.HIGHEST


def up(value, unit):
    return -(-value // unit) * unit


def iota(shape, dim):
    return lax.broadcasted_iota(jnp.int32, shape, dim)


def place():
    me = lax.axis_index("tile").astype(jnp.int32)
    return me, lax.rem(me, jnp.int32(2)) == 0


def ends(n):
    me, _ = place()
    return (
        jnp.where(me > 0, 1.0, 0.0).astype(F32),
        jnp.where(me < n - 1, 1.0, 0.0).astype(F32),
    )


def put_sides(even_ref, odd_ref, left, right):
    _, even = place()

    @pl.when(even)
    def _():
        even_ref[...] = right
        odd_ref[...] = left

    @pl.when(jnp.logical_not(even))
    def _():
        even_ref[...] = left
        odd_ref[...] = right


def take_sides(even_got, odd_got):
    _, even = place()
    flag = jnp.where(even, 1.0, 0.0).astype(F32)
    a, b = even_got.astype(F32), odd_got.astype(F32)
    return jnp.where(flag > 0, b, a), jnp.where(flag > 0, a, b)


def widen(own_ref, got_left, got_right, n, inner):
    first, last = ends(n)
    w = STRIP
    sub = own_ref.shape[1]
    parts = [
        (own_ref[:, 0:w] + got_left[:, 0:w]) * first,
        own_ref[:, w : 2 * w] + got_left[:, w:],
        own_ref[:, 2 * w : sub - 2 * w],
        own_ref[:, sub - 2 * w : sub - w] + got_right[:, 0:w],
        (own_ref[:, sub - w :] + got_right[:, w:]) * last,
    ]
    return parts


def rows_of(columns, count):
    rhs = columns[0][1].shape[0]
    wide = up(count, LANES)
    lane = iota((rhs, wide), 1)
    total = jnp.zeros((rhs, wide), F32)
    for slot, column in columns:
        total = total + jnp.where(lane == slot, jnp.broadcast_to(column, (rhs, wide)), 0.0)
    return jnp.transpose(total)


def rowsum(x):
    return jnp.sum(x, axis=1, keepdims=True)


def begin_kernel(n, rhs_ref, cvec_ref, mass_ref, even_ref, odd_ref, part_ref):
    me, _ = place()
    own = rhs_ref.shape[1]
    rows = even_ref.shape[0] - rhs_ref.shape[0]

    def side(cols):
        pad = jnp.zeros((rows - 2, STRIP), F32)
        return jnp.concatenate([rhs_ref[:, cols], cvec_ref[:, cols], mass_ref[:, cols], pad], 0)

    put_sides(even_ref, odd_ref, side(slice(0, STRIP)), side(slice(own - STRIP, own)))
    part = rowsum(rhs_ref[...] * cvec_ref[...])
    part_ref[...] = rows_of([(me, part)], n)[: part_ref.shape[0]]


def build_kernel(rows_s, rows_v, lane_v, weight_v, o_ref, deg_ref, acc, merged):
    own, sub = o_ref.shape
    edges = merged.shape[0]
    blocks = edges // LANES
    panels = sub // LANES
    tall = 256

    def clear(i, _):
        acc[pl.ds(pl.multiple_of(i * tall, tall), tall), :] = jnp.zeros((tall, LANES), F32)
        return 0

    lax.fori_loop(0, panels * own // tall, clear, 0)

    fill = up(blocks, LANES) - blocks
    turned = jnp.transpose(
        jnp.concatenate([rows_v[...], jnp.zeros((fill, LANES), jnp.int32)], 0)
    )
    square = (LANES, LANES)
    down, across = iota(square, 0), iota(square, 1)
    same_group = (down // GROUP) == (across // GROUP)
    for k in range(blocks):
        equal = jnp.broadcast_to(turned[:, k : k + 1], square) == jnp.broadcast_to(
            rows_v[k : k + 1, :], square
        )
        equal = jnp.where(equal & same_group, 1.0, 0.0).astype(BF16)
        hit = down == jnp.broadcast_to(lane_v[k : k + 1, :], square)
        weight = weight_v[k : k + 1, :]
        high = weight.astype(BF16).astype(F32)
        total = None
        for part in (high, weight - high):
            spread = jnp.where(hit, jnp.broadcast_to(part, square), 0.0).astype(BF16)
            term = lax.dot_general(equal, spread, NT, preferred_element_type=F32)
            total = term if total is None else total + term
        merged[k * LANES : (k + 1) * LANES, :] = total

    def add(g, _):
        base = g * GROUP
        at = [rows_s[base + i] for i in range(GROUP)]
        new = merged[pl.ds(pl.multiple_of(base, GROUP), GROUP), :]
        old = [acc[pl.ds(r, 1), :] for r in at]
        out = [old[i] + new[i : i + 1, :] for i in range(GROUP)]
        for i in range(GROUP):
            acc[pl.ds(at[i], 1), :] = out[i]
        return 0

    lax.fori_loop(0, edges // GROUP, add, 0)

    def narrow(i, _):
        for p in range(panels):
            o_ref[pl.ds(pl.multiple_of(i * tall, tall), tall), p * LANES : (p + 1) * LANES] = acc[
                pl.ds(pl.multiple_of(p * own + i * tall, tall), tall), :
            ].astype(BF16)
        return 0

    lax.fori_loop(0, own // tall, narrow, 0)
    ones = jnp.ones((16, sub), BF16)
    through(deg_ref, ones, o_ref)


def through(out_ref, v, o_ref):
    own, sub = o_ref.shape
    tall = 256
    mine = v[:, STRIP : STRIP + own]

    for j in range(sub // tall):
        cols = slice(j * tall, (j + 1) * tall)
        out_ref[:, cols] = lax.dot_general(mine, o_ref[:, cols], NN, preferred_element_type=F32)
    for j in range(own // tall):
        cols = slice(STRIP + j * tall, STRIP + (j + 1) * tall)
        out_ref[:, cols] += lax.dot_general(
            v, o_ref[j * tall : (j + 1) * tall, :], NT, preferred_element_type=F32
        )


def local_solve(u_ref, wide, inv_ref):
    sub = u_ref.shape[1]
    tall = 256
    for j in range(sub // tall):
        cols = slice(j * tall, (j + 1) * tall)
        u_ref[:, cols] = jnp.dot(wide, inv_ref[:, cols], preferred_element_type=F32)


def put_strips(even_ref, odd_ref, ref):
    width = even_ref.shape[1]
    sub = ref.shape[1]
    put_sides(
        even_ref, odd_ref, ref[:, 0:width].astype(BF16), ref[:, sub - width :].astype(BF16)
    )


def first_solve_kernel(rhs_ref, even_got, odd_got, inv_ref, u_ref, even_ref, odd_ref):
    rhs = rhs_ref.shape[0]
    left, right = take_sides(even_got[0:rhs, :], odd_got[0:rhs, :])
    wide = jnp.concatenate([left, rhs_ref[...], right], 1).astype(BF16)
    local_solve(u_ref, wide, inv_ref)
    put_strips(even_ref, odd_ref, u_ref)


def next_solve_kernel(n, part_ref, even_got, odd_got, inv_ref, y_ref, u_ref, even_ref, odd_ref):
    left, right = take_sides(even_got[...], odd_got[...])
    wide = jnp.concatenate(widen(part_ref, left, right, n, None), 1)
    sub = wide.shape[1]
    y_ref[...] = wide[:, STRIP : sub - STRIP]
    local_solve(u_ref, wide.astype(BF16), inv_ref)
    put_strips(even_ref, odd_ref, u_ref)


def apply_common(
    n, u_ref, even_got, odd_got, halo_even, halo_odd, o_ref, deg_ref, sums_ref, cinv_ref, cvec_ref,
    mass_ref, wide_ref, out_ref,
):
    me, _ = place()
    rhs, sub = u_ref.shape
    own = sub - 2 * STRIP
    left, right = take_sides(even_got[...], odd_got[...])
    vec_left, vec_right = take_sides(halo_even[rhs : rhs + 1, :], halo_odd[rhs : rhs + 1, :])
    pick = jnp.where(
        (iota((n, LANES), 0) == me - 1 + iota((n, LANES), 1)) & (iota((n, LANES), 1) < 3), 1.0, 0.0
    )
    columns = jnp.dot(cinv_ref[...], pick, precision=HIGHEST, preferred_element_type=F32)
    coarse = lax.dot_general(
        sums_ref[0:n, :], columns, TN, precision=HIGHEST, preferred_element_type=F32
    )
    cvec = jnp.concatenate([vec_left, cvec_ref[...], vec_right], 1)
    parts = jnp.concatenate(widen(u_ref, left, right, n, None), 1)
    for j in range(sub // LANES):
        which = 0 if j == 0 else (2 if j == sub // LANES - 1 else 1)
        cols = slice(j * LANES, (j + 1) * LANES)
        wide_ref[:, cols] = parts[:, cols] + coarse[:, which : which + 1] * cvec[:, cols]
    wide = wide_ref[...]
    through(out_ref, wide.astype(BF16), o_ref)
    out_ref[...] = wide * deg_ref[0:1, :] - out_ref[...]
    out_ref[:, STRIP : STRIP + own] += mass_ref[...] * wide[:, STRIP : STRIP + own]
    return cvec


def first_apply_kernel(
    n, u_ref, even_got, odd_got, halo_even, halo_odd, o_ref, deg_ref, sums_ref, cinv_ref, cvec_ref,
    mass_ref, rhs_ref, z_ref, y_ref, even_ref, odd_ref, part_ref, wide_ref,
):
    me, _ = place()
    cvec = apply_common(
        n, u_ref, even_got, odd_got, halo_even, halo_odd, o_ref, deg_ref, sums_ref, cinv_ref,
        cvec_ref, mass_ref, wide_ref, y_ref,
    )
    sub = u_ref.shape[1]
    z_ref[...] = wide_ref[:, STRIP : sub - STRIP]
    put_strips(even_ref, odd_ref, y_ref)
    scaled = y_ref[...] * cvec
    a = rowsum(rhs_ref[...] * z_ref[...])
    b = rowsum(wide_ref[...] * y_ref[...])
    slots = up(n, 8)
    part_ref[0:slots, :] = rows_of(
        [
            (me - 1, rowsum(scaled[:, 0:STRIP])),
            (me, rowsum(scaled[:, STRIP : sub - STRIP])),
            (me + 1, rowsum(scaled[:, sub - STRIP :])),
        ],
        slots,
    )[0:slots]
    part_ref[slots : slots + 8, :] = rows_of([(0, a), (1, b)], 8)[0:8]


def next_apply_kernel(
    n, u_ref, even_got, odd_got, halo_even, halo_odd, o_ref, deg_ref, sums_ref, cinv_ref, cvec_ref,
    mass_ref, rhs_ref, y_ref, w_ref, q_ref, even_ref, odd_ref, part_ref, wide_ref, out_ref,
):
    apply_common(
        n, u_ref, even_got, odd_got, halo_even, halo_odd, o_ref, deg_ref, sums_ref, cinv_ref,
        cvec_ref, mass_ref, wide_ref, out_ref,
    )
    sub = u_ref.shape[1]
    w_ref[...] = wide_ref[:, STRIP : sub - STRIP]
    q_ref[...] = out_ref[:, STRIP : sub - STRIP]
    put_strips(even_ref, odd_ref, out_ref)
    c = rowsum(rhs_ref[...] * w_ref[...])
    d = rowsum(y_ref[...] * w_ref[...])
    e = rowsum(wide_ref[...] * out_ref[...])
    part_ref[...] = rows_of([(0, c), (1, d), (2, e)], 8)[0:8]


def finish_kernel(
    n, rhs_ref, z_ref, y_ref, w_ref, q_ref, even_got, odd_got, first_ref, second_ref, x_ref, r_ref
):
    slots = up(n, 8)
    a, b = first_ref[slots : slots + 1, :], first_ref[slots + 1 : slots + 2, :]
    c, d, e = second_ref[0:1, :], second_ref[1:2, :], second_ref[2:3, :]
    alpha = a / b
    following = a - alpha * (c + b) + alpha * alpha * d
    beta = following / a
    cross = b - alpha * d
    energy = (b - 2.0 * alpha * d + alpha * alpha * e) + 2.0 * beta * cross + beta * beta * b
    step = following / energy
    rhs, own = rhs_ref.shape
    near = jnp.transpose(jnp.broadcast_to(alpha + step * (1.0 + beta), (LANES, rhs)))[:, 0:1]
    far = jnp.transpose(jnp.broadcast_to(alpha * step, (LANES, rhs)))[:, 0:1]
    x_ref[...] = near * z_ref[...] - far * w_ref[...]
    left, right = take_sides(even_got[...], odd_got[...])
    r_ref[...] = rhs_ref[...] - near * y_ref[...] + far * q_ref[...]
    r_ref[:, 0:STRIP] += far * left
    r_ref[:, own - STRIP :] += far * right


def call(kernel, outs, scratch, limit, in_specs=None, count=None):
    vmem = pl.BlockSpec(memory_space=pltpu.VMEM)
    return pl.pallas_call(
        kernel,
        out_shape=[jax.ShapeDtypeStruct(s, d) for s, d in outs],
        in_specs=in_specs if in_specs is not None else [vmem] * count,
        out_specs=[vmem] * len(outs),
        scratch_shapes=scratch,
        compiler_params=pltpu.CompilerParams(vmem_limit_bytes=limit << 20),
    )


def swap(pair):
    n = lax.axis_size("tile")
    got = []
    for start, payload in zip((0, 1), pair):
        links = []
        for i in range(start, n - 1, 2):
            links += [(i, i + 1), (i + 1, i)]
        got.append(lax.ppermute(payload, "tile", links))
    return got


def total(part):
    n = lax.axis_size("tile")
    if n & (n - 1):
        return lax.psum(part, "tile")
    hop = 1
    while hop < n:
        part = part + lax.ppermute(part, "tile", [(i, i ^ hop) for i in range(n)])
        hop *= 2
    return part


def shards(
    rhs, mass_diag, edge_heads, edge_tails, edge_weight, local_inverse, coarse_vec, coarse_inv
):
    n = lax.axis_size("tile")
    rows, own = rhs.shape
    sub = local_inverse.shape[1]
    edges = edge_heads.shape[0]
    slots = up(n, 8)
    cvec, mass = coarse_vec[None, :], mass_diag[None, :]
    vmem = pl.BlockSpec(memory_space=pltpu.VMEM)
    smem = pl.BlockSpec(memory_space=pltpu.SMEM)

    side = ((rows + 8, STRIP), F32)
    even, odd, part = call(
        functools.partial(begin_kernel, n), [side, side, ((slots, rows), F32)], [], 4, count=3
    )(rhs, cvec, mass)
    halo = swap((even, odd))
    sums = total(part)

    at = (edge_tails >> 7) * own + (edge_heads - STRIP)
    shape = (edges // LANES, LANES)
    stiff, degree = call(
        build_kernel,
        [((own, sub), BF16), ((16, sub), F32)],
        [pltpu.VMEM((sub // LANES * own, LANES), F32), pltpu.VMEM((edges, LANES), F32)],
        32,
        in_specs=[smem, vmem, vmem, vmem],
    )(at, at.reshape(shape), (edge_tails & 127).reshape(shape), edge_weight.reshape(shape))

    whole, owned = ((rows, sub), F32), ((rows, own), F32)
    strip = ((rows, 2 * STRIP), BF16)
    u, even, odd = call(first_solve_kernel, [whole, strip, strip], [], 12, count=4)(
        rhs, *halo, local_inverse
    )
    got = swap((even, odd))
    z, y_part, even, odd, part = call(
        functools.partial(first_apply_kernel, n),
        [owned, whole, strip, strip, ((slots + 8, rows), F32)],
        [pltpu.VMEM((rows, sub), F32)],
        12,
        count=12,
    )(u, *got, *halo, stiff, degree, sums, coarse_inv, cvec, mass, rhs)
    got = swap((even, odd))
    first = total(part)
    y, u, even, odd = call(
        functools.partial(next_solve_kernel, n), [owned, whole, strip, strip], [], 12, count=4
    )(y_part, *got, local_inverse)
    got = swap((even, odd))
    strip = ((rows, STRIP), BF16)
    w, q, even, odd, part = call(
        functools.partial(next_apply_kernel, n),
        [owned, owned, strip, strip, ((8, rows), F32)],
        [pltpu.VMEM((rows, sub), F32), pltpu.VMEM((rows, sub), F32)],
        12,
        count=13,
    )(u, *got, *halo, stiff, degree, first, coarse_inv, cvec, mass, rhs, y)
    got = swap((even, odd))
    second = total(part)
    return tuple(
        call(functools.partial(finish_kernel, n), [owned, owned], [], 16, count=9)(
            rhs, z, y, w, q, *got, first, second
        )
    )


def solution(mesh):
    return jax.shard_map(
        shards,
        mesh=mesh,
        in_specs=(
            P("grp", "tile"),
            P("tile"),
            P("tile"),
            P("tile"),
            P("tile"),
            P("tile", None),
            P("tile"),
            P(),
        ),
        out_specs=(P("grp", "tile"), P("grp", "tile")),
        check_vma=False,
    )
```

time: 374 us -> 103 us (0.28)
  other arithmetic: 167 us -> 0.08 us
  blocking collectives: 104 us -> 0 us
  matrix products: 35.9 us -> 0 us
  Pallas kernels: 0 us -> 35.1 us
  waiting for transfers between devices: 2.86 us -> 20.9 us
  local copies, waits for them, and re-layouts: 19.4 us -> 7.18 us
    unnamed x4 -> x1, other arithmetic: 158 us -> 0.01 us
    psum x2 -> x0, blocking collectives: 64 us -> none  [both_dots(): return lax.psum((inner(resid, zvec), inner(image, zvec)), 'tile')]
    all_gather x2 -> x0, blocking collectives: 40.3 us -> none  [precondition(): every = lax.all_gather(restricted[:, None], 'tile', axis=1, tiled=True)]
    dot_general x6 -> x0, matrix products: 35.9 us -> none  [the longest x2 25.5 us: operate(): contrib = jnp.dot(widened, stiffness, precision=lax.Precision.HIGHEST)]
    pallas_call x0 -> x7, Pallas kernels: none -> 35.1 us  [the longest x1 21.6 us: shards(): call(build_kernel, [((own, sub), BF16), ((16, sub), F32)], [pltpu.VMEM((s...]
    ppermute x16 -> x22, waiting for transfers between devices: 2.86 us -> 20.9 us  [the longest x12 20.7 us: total(): part = part + lax.ppermute(part, 'tile', [(i, i ^ hop) for i in range(n)])]
    scatter-add x1 -> x0, local copies, waits for them, and re-layouts: 18 us -> none  [build_stiffness(): return jnp.zeros((SUB, SUB), jnp.float32).at[rows_idx, cols_idx].add(values)]
    unnamed x30 -> x20, local copies, waits for them, and re-layouts: 0.93 us -> 5.77 us
  transfers between devices with their start and end apart: 16 -> 22, of which waited for: 4 -> 12; matrix products, arithmetic and copies ran while one was open for 48% -> 0% of each run, Pallas kernels for 0% -> 22%
where the time goes in v1:
time: 103 us; the launch traced here: 102 us
  starting transfers between devices  38.2 us (37%)
  Pallas kernels  35.1 us (34%)
  waiting for transfers between devices  20.9 us (20%)
  local copies, waits for them, and re-layouts  7.18 us (7%)
    ppermute x12, starting transfers between devices, total(): part = part + lax.ppermute(part, 'tile', [(i, i ^ hop) for i in range(n)])  26.5 us
    pallas_call x1, Pallas kernels, shards(): call(build_kernel, [((own, sub), BF16), ((16, sub), F32)], [pltpu.VMEM((s...  21.6 us
    ppermute x12, waiting for transfers between devices, total(): part = part + lax.ppermute(part, 'tile', [(i, i ^ hop) for i in range(n)])  20.7 us
    ppermute x10, starting transfers between devices, swap(): got.append(lax.ppermute(payload, 'tile', links))  11.7 us
    unnamed x20, local copies, waits for them, and re-layouts  5.77 us
    pallas_call x1, Pallas kernels, shards(): call(functools.partial(first_apply_kernel, n), [owned, whole, strip, stri...  4.54 us
    pallas_call x1, Pallas kernels, shards(): call(functools.partial(next_apply_kernel, n), [owned, owned, strip, strip...  4.44 us
  transfers between devices with their start and end apart: 22, of which 12 were waited for; matrix products, arithmetic and copies ran while one was open for 0% of the time, Pallas kernels for 22%

profile of v1, /device:TPU:0, one launch (start us, length us, event | category | flops | bytes accessed | tf_op | source)
XLA Modules:
  0.0 102.4 jit_solution(11685889315028968456)
XLA Ops:
  2.1 1.2 %copy-done.1 = f32[128,1792]{1,0:T(8,128)S(1)} copy-done((f32[128,1792]{1,0:T(8,128)S(1)}, f32[128,1792]{1,0:T(8,128)}, u32[]{:S(2)}) %copy-start.1) | copy-done | bytes 917528
  4.6 4.1 %collective-permute-start.4 = (f32[16,128]{1,0:T(8,128)S(1)}, f32[16,128]{1,0:T(8,128)S(1)}, u32[]{:S(2)}, u32[]{:S(2)}) collective-permute-start(f32[16,128]{1,0:T(8,128)S(1)} %get-tuple-element.31), channel_id=1, source_target_pairs={{0,1},{1,0},{2,3},{3,2},{4,5},{5,4},{6,7},{7,6},{8,9},{9,8},{10,11... | collective-permute-start | bytes 24584 | tf_op jit(solution)/shard_map/ppermute | solution.py:337
  9.5 1.5 %collective-permute-start.5 = (f32[16,128]{1,0:T(8,128)S(1)}, f32[16,128]{1,0:T(8,128)S(1)}, u32[]{:S(2)}, u32[]{:S(2)}) collective-permute-start(f32[16,128]{1,0:T(8,128)S(1)} %add.41), channel_id=1, source_target_pairs={{0,2},{1,3},{2,0},{3,1},{4,6},{5,7},{6,4},{7,5},{8,10},{9,11},{10,... | collective-permute-start | bytes 24584 | tf_op jit(solution)/shard_map/ppermute | solution.py:337
  11.1 2.1 %collective-permute-done.5 = f32[16,128]{1,0:T(8,128)S(1)} collective-permute-done((f32[16,128]{1,0:T(8,128)S(1)}, f32[16,128]{1,0:T(8,128)S(1)}, u32[]{:S(2)}, u32[]{:S(2)}) %collective-permute-start.5) | collective-permute-done | bytes 8224 | tf_op jit(solution)/shard_map/ppermute | solution.py:337
  13.2 1.6 %collective-permute-start.6 = (f32[16,128]{1,0:T(8,128)S(1)}, f32[16,128]{1,0:T(8,128)S(1)}, u32[]{:S(2)}, u32[]{:S(2)}) collective-permute-start(f32[16,128]{1,0:T(8,128)S(1)} %add.42), channel_id=1, source_target_pairs={{0,4},{1,5},{2,6},{3,7},{4,0},{5,1},{6,2},{7,3},{8,12},{9,13},{10,... | collective-permute-start | bytes 24584 | tf_op jit(solution)/shard_map/ppermute | solution.py:337
  14.8 2.0 %collective-permute-done.6 = f32[16,128]{1,0:T(8,128)S(1)} collective-permute-done((f32[16,128]{1,0:T(8,128)S(1)}, f32[16,128]{1,0:T(8,128)S(1)}, u32[]{:S(2)}, u32[]{:S(2)}) %collective-permute-start.6) | collective-permute-done | bytes 8224 | tf_op jit(solution)/shard_map/ppermute | solution.py:337
  16.8 2.7 %collective-permute-start.7 = (f32[16,128]{1,0:T(8,128)S(1)}, f32[16,128]{1,0:T(8,128)S(1)}, u32[]{:S(2)}, u32[]{:S(2)}) collective-permute-start(f32[16,128]{1,0:T(8,128)S(1)} %add.43), channel_id=1, source_target_pairs={{0,8},{1,9},{2,10},{3,11},{4,12},{5,13},{6,14},{7,15},{8,0},{9,1},... | collective-permute-start | bytes 24584 | tf_op jit(solution)/shard_map/ppermute | solution.py:337
  19.5 3.4 %copy-done = bf16[2048,2048]{1,0:T(8,128)(2,1)S(1)} copy-done((bf16[2048,2048]{1,0:T(8,128)(2,1)S(1)}, bf16[2048,2048]{1,0:T(8,128)(2,1)}, u32[]{:S(2)}) %copy-start) | copy-done | bytes 8388632
  22.9 1.2 %copy-done.2 = f32[128,1792]{1,0:T(8,128)S(1)} copy-done((f32[128,1792]{1,0:T(8,128)S(1)}, f32[128,1792]{1,0:T(8,128)}, u32[]{:S(2)}) %copy-start.2) | copy-done | bytes 917528
  24.1 1.4 %shard_map.96 = (f32[128,2048]{1,0:T(8,128)S(1)}, bf16[128,256]{1,0:T(8,128)(2,1)S(1)}, bf16[128,256]{1,0:T(8,128)(2,1)S(1)}) custom-call(f32[128,1792]{1,0:T(8,128)S(1)} %copy-done.2, f32[136,128]{1,0:T(8,128)S(1)} %collective-permute-done.even_got.halo_even, f32[136,128]{1,0:T(8,128)S(1)} %collective-permute-done.1.odd_got.halo_odd, ...), custom_call_target="tpu_custom_call" | custom-call | tf_op jit(solution)/shard_map/pallas_call | solution.py:373
  26.2 21.6 %shard_map.97 = (bf16[1792,2048]{1,0:T(8,128)(2,1)S(1)}, f32[16,2048]{1,0:T(8,128)S(1)}) custom-call(s32[7168]{0:T(1024)S(1)} %get-tuple-element.47.rows_s, s32[56,128]{1,0:T(8,128)S(1)} %bitcast.6, s32[56,128]{1,0:T(8,128)S(1)} %get-tuple-element.46.lane_v, f32[56,128]{1,0:T(8,128)S(1)} %bitcast.7), custom_call_target="tpu_custom_call" | custom-call | tf_op jit(solution)/shard_map/pallas_call | solution.py:363
  48.0 4.5 %shard_map.98 = (f32[128,1792]{1,0:T(8,128)S(1)}, f32[128,2048]{1,0:T(8,128)S(1)}, bf16[128,256]{1,0:T(8,128)(2,1)S(1)}, bf16[128,256]{1,0:T(8,128)(2,1)S(1)}, f32[24,128]{1,0:T(8,128)S(1)}) custom-call(f32[128,2048]{1,0:T(8,128)S(1)} %get-tuple-element.26.u_ref, bf16[128,256]{1,0:T(8,128)(2,1)S(1)} %collective-permute-done.2.even_got, ...), custom_call_target="tpu_custom_call" | custom-call | tf_op jit(solution)/shard_map/pallas_call | solution.py:377
  52.5 2.9 %collective-permute-start.8 = (bf16[128,256]{1,0:T(8,128)(2,1)S(1)}, bf16[128,256]{1,0:T(8,128)(2,1)S(1)}, u32[]{:S(2)}, u32[]{:S(2)}) collective-permute-start(bf16[128,256]{1,0:T(8,128)(2,1)S(1)} %get-tuple-element.34), channel_id=1, source_target_pairs={{0,1},{1,0},{2,3},{3,2},{4,5},{5,4},{6,7},{7,6},{8,9},{9,8},{10,11... | collective-permute-start | bytes 196616 | tf_op jit(solution)/shard_map/ppermute | solution.py:327
  56.3 1.3 %shard_map.99 = (f32[128,1792]{1,0:T(8,128)S(1)}, f32[128,2048]{1,0:T(8,128)S(1)}, bf16[128,256]{1,0:T(8,128)(2,1)S(1)}, bf16[128,256]{1,0:T(8,128)(2,1)S(1)}) custom-call(f32[128,2048]{1,0:T(8,128)S(1)} %get-tuple-element.33.part_ref, bf16[128,256]{1,0:T(8,128)(2,1)S(1)} %collective-permute-done.8.even_got, ...), custom_call_target="tpu_custom_call" | custom-call | tf_op jit(solution)/shard_map/pallas_call | solution.py:386
  57.6 4.8 %collective-permute-start.10 = (bf16[128,256]{1,0:T(8,128)(2,1)S(1)}, bf16[128,256]{1,0:T(8,128)(2,1)S(1)}, u32[]{:S(2)}, u32[]{:S(2)}) collective-permute-start(bf16[128,256]{1,0:T(8,128)(2,1)S(1)} %get-tuple-element.38), channel_id=1, source_target_pairs={{0,1},{1,0},{2,3},{3,2},{4,5},{5,4},{6,7},{7,6},{8,9},{9,8},{10,11... | collective-permute-start | bytes 196616 | tf_op jit(solution)/shard_map/ppermute | solution.py:327
  63.2 3.9 %collective-permute-start.12 = (f32[24,128]{1,0:T(8,128)S(1)}, f32[24,128]{1,0:T(8,128)S(1)}, u32[]{:S(2)}, u32[]{:S(2)}) collective-permute-start(f32[24,128]{1,0:T(8,128)S(1)} %get-tuple-element.40), channel_id=1, source_target_pairs={{0,1},{1,0},{2,3},{3,2},{4,5},{5,4},{6,7},{7,6},{8,9},{9,8},{10,11... | collective-permute-start | bytes 36872 | tf_op jit(solution)/shard_map/ppermute | solution.py:337
  67.1 0.8 collective-permute-done.12
  67.9 1.6 %collective-permute-start.13 = (f32[24,128]{1,0:T(8,128)S(1)}, f32[24,128]{1,0:T(8,128)S(1)}, u32[]{:S(2)}, u32[]{:S(2)}) collective-permute-start(f32[24,128]{1,0:T(8,128)S(1)} %add.45), channel_id=1, source_target_pairs={{0,2},{1,3},{2,0},{3,1},{4,6},{5,7},{6,4},{7,5},{8,10},{9,11},{10,... | collective-permute-start | bytes 36872 | tf_op jit(solution)/shard_map/ppermute | solution.py:337
  69.6 2.1 %collective-permute-done.13 = f32[24,128]{1,0:T(8,128)S(1)} collective-permute-done((f32[24,128]{1,0:T(8,128)S(1)}, f32[24,128]{1,0:T(8,128)S(1)}, u32[]{:S(2)}, u32[]{:S(2)}) %collective-permute-start.13) | collective-permute-done | bytes 12320 | tf_op jit(solution)/shard_map/ppermute | solution.py:337
  71.6 1.3 %collective-permute-start.14 = (f32[24,128]{1,0:T(8,128)S(1)}, f32[24,128]{1,0:T(8,128)S(1)}, u32[]{:S(2)}, u32[]{:S(2)}) collective-permute-start(f32[24,128]{1,0:T(8,128)S(1)} %add.46), channel_id=1, source_target_pairs={{0,4},{1,5},{2,6},{3,7},{4,0},{5,1},{6,2},{7,3},{8,12},{9,13},{10,... | collective-permute-start | bytes 36872 | tf_op jit(solution)/shard_map/ppermute | solution.py:337
  73.0 2.4 %collective-permute-done.14 = f32[24,128]{1,0:T(8,128)S(1)} collective-permute-done((f32[24,128]{1,0:T(8,128)S(1)}, f32[24,128]{1,0:T(8,128)S(1)}, u32[]{:S(2)}, u32[]{:S(2)}) %collective-permute-start.14) | collective-permute-done | bytes 12320 | tf_op jit(solution)/shard_map/ppermute | solution.py:337
  75.3 1.8 %collective-permute-start.15 = (f32[24,128]{1,0:T(8,128)S(1)}, f32[24,128]{1,0:T(8,128)S(1)}, u32[]{:S(2)}, u32[]{:S(2)}) collective-permute-start(f32[24,128]{1,0:T(8,128)S(1)} %add.47), channel_id=1, source_target_pairs={{0,8},{1,9},{2,10},{3,11},{4,12},{5,13},{6,14},{7,15},{8,0},{9,1},... | collective-permute-start | bytes 36872 | tf_op jit(solution)/shard_map/ppermute | solution.py:337
  77.1 2.8 %collective-permute-done.15 = f32[24,128]{1,0:T(8,128)S(1)} collective-permute-done((f32[24,128]{1,0:T(8,128)S(1)}, f32[24,128]{1,0:T(8,128)S(1)}, u32[]{:S(2)}, u32[]{:S(2)}) %collective-permute-start.15) | collective-permute-done | bytes 12320 | tf_op jit(solution)/shard_map/ppermute | solution.py:337
  79.9 4.4 %shard_map.100 = (f32[128,1792]{1,0:T(8,128)S(1)}, f32[128,1792]{1,0:T(8,128)S(1)}, bf16[128,128]{1,0:T(8,128)(2,1)S(1)}, bf16[128,128]{1,0:T(8,128)(2,1)S(1)}, f32[8,128]{1,0:T(8,128)S(1)}) custom-call(f32[128,2048]{1,0:T(8,128)S(1)} %get-tuple-element.37.u_ref, bf16[128,256]{1,0:T(8,128)(2,1)S(1)} %collective-permute-done.10.even_got, ...), custom_call_target="tpu_custom_call" | custom-call | tf_op jit(solution)/shard_map/pallas_call | solution.py:391
  85.1 3.0 %collective-permute-start.18 = (f32[8,128]{1,0:T(8,128)S(1)}, f32[8,128]{1,0:T(8,128)S(1)}, u32[]{:S(2)}, u32[]{:S(2)}) collective-permute-start(f32[8,128]{1,0:T(8,128)S(1)} %get-tuple-element.45), channel_id=1, source_target_pairs={{0,1},{1,0},{2,3},{3,2},{4,5},{5,4},{6,7},{7,6},{8,9},{9,8},{10,11... | collective-permute-start | bytes 12296 | tf_op jit(solution)/shard_map/ppermute | solution.py:337
  89.0 1.2 %collective-permute-start.19 = (f32[8,128]{1,0:T(8,128)S(1)}, f32[8,128]{1,0:T(8,128)S(1)}, u32[]{:S(2)}, u32[]{:S(2)}) collective-permute-start(f32[8,128]{1,0:T(8,128)S(1)} %add.49), channel_id=1, source_target_pairs={{0,2},{1,3},{2,0},{3,1},{4,6},{5,7},{6,4},{7,5},{8,10},{9,11},{10,... | collective-permute-start | bytes 12296 | tf_op jit(solution)/shard_map/ppermute | solution.py:337
  90.1 2.4 %collective-permute-done.19 = f32[8,128]{1,0:T(8,128)S(1)} collective-permute-done((f32[8,128]{1,0:T(8,128)S(1)}, f32[8,128]{1,0:T(8,128)S(1)}, u32[]{:S(2)}, u32[]{:S(2)}) %collective-permute-start.19) | collective-permute-done | bytes 4128 | tf_op jit(solution)/shard_map/ppermute | solution.py:337
  92.6 1.8 %collective-permute-start.20 = (f32[8,128]{1,0:T(8,128)S(1)}, f32[8,128]{1,0:T(8,128)S(1)}, u32[]{:S(2)}, u32[]{:S(2)}) collective-permute-start(f32[8,128]{1,0:T(8,128)S(1)} %add.50), channel_id=1, source_target_pairs={{0,4},{1,5},{2,6},{3,7},{4,0},{5,1},{6,2},{7,3},{8,12},{9,13},{10,... | collective-permute-start | bytes 12296 | tf_op jit(solution)/shard_map/ppermute | solution.py:337
  94.4 1.8 %collective-permute-done.20 = f32[8,128]{1,0:T(8,128)S(1)} collective-permute-done((f32[8,128]{1,0:T(8,128)S(1)}, f32[8,128]{1,0:T(8,128)S(1)}, u32[]{:S(2)}, u32[]{:S(2)}) %collective-permute-start.20) | collective-permute-done | bytes 4128 | tf_op jit(solution)/shard_map/ppermute | solution.py:337
  96.2 2.0 %collective-permute-start.21 = (f32[8,128]{1,0:T(8,128)S(1)}, f32[8,128]{1,0:T(8,128)S(1)}, u32[]{:S(2)}, u32[]{:S(2)}) collective-permute-start(f32[8,128]{1,0:T(8,128)S(1)} %add.51), channel_id=1, source_target_pairs={{0,8},{1,9},{2,10},{3,11},{4,12},{5,13},{6,14},{7,15},{8,0},{9,1},... | collective-permute-start | bytes 12296 | tf_op jit(solution)/shard_map/ppermute | solution.py:337
  98.2 2.5 %collective-permute-done.21 = f32[8,128]{1,0:T(8,128)S(1)} collective-permute-done((f32[8,128]{1,0:T(8,128)S(1)}, f32[8,128]{1,0:T(8,128)S(1)}, u32[]{:S(2)}, u32[]{:S(2)}) %collective-permute-start.21) | collective-permute-done | bytes 4128 | tf_op jit(solution)/shard_map/ppermute | solution.py:337
  100.7 1.7 %shard_map.101 = (f32[128,1792]{1,0:T(8,128)}, f32[128,1792]{1,0:T(8,128)}) custom-call(f32[128,1792]{1,0:T(8,128)S(1)} %copy-done.3, f32[128,1792]{1,0:T(8,128)S(1)} %get-tuple-element.32.z_ref, f32[128,1792]{1,0:T(8,128)S(1)} %get-tuple-element.36.y_ref, f32[128,1792]{1,0:T(8,128)S(1)} %get-tuple-element.41.w_ref, ...), custom_call_target="tpu_custom_call" | custom-call | tf_op jit(solution)/shard_map/pallas_call | solution.py:401
  (55 shorter events, 7.7 us)
Async XLA Ops:
  0.6 47.3 %copy-start.4 = (f32[16,16]{1,0:T(8,128)S(1)}, f32[16,16]{1,0:T(8,128)}, u32[]{:S(2)}) copy-start(f32[16,16]{1,0:T(8,128)} %cinv_ref.3) | copy-start | bytes 3076
  2.1 1.2 %copy-start.1 = (f32[128,1792]{1,0:T(8,128)S(1)}, f32[128,1792]{1,0:T(8,128)}, u32[]{:S(2)}) copy-start(f32[128,1792]{1,0:T(8,128)} %rhs_ref.9) | copy-start | bytes 2752516
  3.2 23.0 %copy-start.6 = (s32[7168]{0:T(1024)S(1)}, s32[7168]{0:T(1024)}, u32[]{:S(2)}) copy-start(s32[7168]{0:T(1024)} %param.11) | copy-start | bytes 86020
  3.2 23.0 %copy-start.7 = (s32[7168]{0:T(1024)S(1)}, s32[7168]{0:T(1024)}, u32[]{:S(2)}) copy-start(s32[7168]{0:T(1024)} %param.10) | copy-start | bytes 86020
  3.2 23.0 %copy-start.5 = (f32[7168]{0:T(1024)S(1)}, f32[7168]{0:T(1024)}, u32[]{:S(2)}) copy-start(f32[7168]{0:T(1024)} %param.12) | copy-start | bytes 86020
  3.2 44.7 %copy-start.3 = (f32[128,1792]{1,0:T(8,128)S(1)}, f32[128,1792]{1,0:T(8,128)}, u32[]{:S(2)}) copy-start(f32[128,1792]{1,0:T(8,128)} %rhs_ref.9) | copy-start | bytes 2752516
  3.5 16.0 %collective-permute-start = (f32[136,128]{1,0:T(8,128)S(1)}, f32[136,128]{1,0:T(8,128)S(1)}, u32[]{:S(2)}, u32[]{:S(2)}) collective-permute-start(f32[136,128]{1,0:T(8,128)S(1)} %get-tuple-element.24), channel_id=1, source_target_pairs={{0,1},{1,0},{2,3},{3,2},{4,5},{5,4},{6,7},{7,6},{8,9},{9,8},{10,11... | collective-permute-start | bytes 208904 | tf_op jit(solution)/shard_map/ppermute | solution.py:327
  4.0 15.5 %collective-permute-start.1 = (f32[136,128]{1,0:T(8,128)S(1)}, f32[136,128]{1,0:T(8,128)S(1)}, u32[]{:S(2)}, u32[]{:S(2)}) collective-permute-start(f32[136,128]{1,0:T(8,128)S(1)} %get-tuple-element.25), channel_id=1, source_target_pairs={{1,2},{2,1},{3,4},{4,3},{5,6},{6,5},{7,8},{8,7},{9,10},{10,9},{11,... | collective-permute-start | bytes 208904 | tf_op jit(solution)/shard_map/ppermute | solution.py:327
  4.6 4.9 %collective-permute-start.4 = (f32[16,128]{1,0:T(8,128)S(1)}, f32[16,128]{1,0:T(8,128)S(1)}, u32[]{:S(2)}, u32[]{:S(2)}) collective-permute-start(f32[16,128]{1,0:T(8,128)S(1)} %get-tuple-element.31), channel_id=1, source_target_pairs={{0,1},{1,0},{2,3},{3,2},{4,5},{5,4},{6,7},{7,6},{8,9},{9,8},{10,11... | collective-permute-start | bytes 24584 | tf_op jit(solution)/shard_map/ppermute | solution.py:337
  9.5 3.7 %collective-permute-start.5 = (f32[16,128]{1,0:T(8,128)S(1)}, f32[16,128]{1,0:T(8,128)S(1)}, u32[]{:S(2)}, u32[]{:S(2)}) collective-permute-start(f32[16,128]{1,0:T(8,128)S(1)} %add.41), channel_id=1, source_target_pairs={{0,2},{1,3},{2,0},{3,1},{4,6},{5,7},{6,4},{7,5},{8,10},{9,11},{10,... | collective-permute-start | bytes 24584 | tf_op jit(solution)/shard_map/ppermute | solution.py:337
  13.2 3.7 %collective-permute-start.6 = (f32[16,128]{1,0:T(8,128)S(1)}, f32[16,128]{1,0:T(8,128)S(1)}, u32[]{:S(2)}, u32[]{:S(2)}) collective-permute-start(f32[16,128]{1,0:T(8,128)S(1)} %add.42), channel_id=1, source_target_pairs={{0,4},{1,5},{2,6},{3,7},{4,0},{5,1},{6,2},{7,3},{8,12},{9,13},{10,... | collective-permute-start | bytes 24584 | tf_op jit(solution)/shard_map/ppermute | solution.py:337
  16.8 31.0 %collective-permute-start.7 = (f32[16,128]{1,0:T(8,128)S(1)}, f32[16,128]{1,0:T(8,128)S(1)}, u32[]{:S(2)}, u32[]{:S(2)}) collective-permute-start(f32[16,128]{1,0:T(8,128)S(1)} %add.43), channel_id=1, source_target_pairs={{0,8},{1,9},{2,10},{3,11},{4,12},{5,13},{6,14},{7,15},{8,0},{9,1},... | collective-permute-start | bytes 24584 | tf_op jit(solution)/shard_map/ppermute | solution.py:337
  19.5 3.4 %copy-start = (bf16[2048,2048]{1,0:T(8,128)(2,1)S(1)}, bf16[2048,2048]{1,0:T(8,128)(2,1)}, u32[]{:S(2)}) copy-start(bf16[2048,2048]{1,0:T(8,128)(2,1)} %inv_ref.3) | copy-start | bytes 25165828
  22.9 1.2 %copy-start.2 = (f32[128,1792]{1,0:T(8,128)S(1)}, f32[128,1792]{1,0:T(8,128)}, u32[]{:S(2)}) copy-start(f32[128,1792]{1,0:T(8,128)} %rhs_ref.9) | copy-start | bytes 2752516
  24.1 32.2 %slice-start = ((s8[8388608]{0:T(1024)(128)(4,1)}), s8[4194304]{0:T(1024)(128)(4,1)S(1)}, s32[]{:S(2)}) async-start(s8[8388608]{0:T(1024)(128)(4,1)} %bitcast.4), calls=%async_computation | async-start | bytes 8388608
  25.4 22.5 %collective-permute-start.2 = (bf16[128,256]{1,0:T(8,128)(2,1)S(1)}, bf16[128,256]{1,0:T(8,128)(2,1)S(1)}, u32[]{:S(2)}, u32[]{:S(2)}) collective-permute-start(bf16[128,256]{1,0:T(8,128)(2,1)S(1)} %get-tuple-element.27), channel_id=1, source_target_pairs={{0,1},{1,0},{2,3},{3,2},{4,5},{5,4},{6,7},{7,6},{8,9},{9,8},{10,11... | collective-permute-start | bytes 196616 | tf_op jit(solution)/shard_map/ppermute | solution.py:327
  25.5 22.4 %collective-permute-start.3 = (bf16[128,256]{1,0:T(8,128)(2,1)S(1)}, bf16[128,256]{1,0:T(8,128)(2,1)S(1)}, u32[]{:S(2)}, u32[]{:S(2)}) collective-permute-start(bf16[128,256]{1,0:T(8,128)(2,1)S(1)} %get-tuple-element.28), channel_id=1, source_target_pairs={{1,2},{2,1},{3,4},{4,3},{5,6},{6,5},{7,8},{8,7},{9,10},{10,9},{11,... | collective-permute-start | bytes 196616 | tf_op jit(solution)/shard_map/ppermute | solution.py:327
  47.9 8.4 %slice-start.1 = ((s8[8388608]{0:T(1024)(128)(4,1)}), s8[4194304]{0:T(1024)(128)(4,1)S(1)}, s32[]{:S(2)}) async-start(s8[8388608]{0:T(1024)(128)(4,1)} %bitcast.4), calls=%async_computation.1 | async-start | bytes 8388608
  52.5 3.8 %collective-permute-start.8 = (bf16[128,256]{1,0:T(8,128)(2,1)S(1)}, bf16[128,256]{1,0:T(8,128)(2,1)S(1)}, u32[]{:S(2)}, u32[]{:S(2)}) collective-permute-start(bf16[128,256]{1,0:T(8,128)(2,1)S(1)} %get-tuple-element.34), channel_id=1, source_target_pairs={{0,1},{1,0},{2,3},{3,2},{4,5},{5,4},{6,7},{7,6},{8,9},{9,8},{10,11... | collective-permute-start | bytes 196616 | tf_op jit(solution)/shard_map/ppermute | solution.py:327
  55.4 0.9 collective-permute-start.9
  57.6 22.3 %collective-permute-start.10 = (bf16[128,256]{1,0:T(8,128)(2,1)S(1)}, bf16[128,256]{1,0:T(8,128)(2,1)S(1)}, u32[]{:S(2)}, u32[]{:S(2)}) collective-permute-start(bf16[128,256]{1,0:T(8,128)(2,1)S(1)} %get-tuple-element.38), channel_id=1, source_target_pairs={{0,1},{1,0},{2,3},{3,2},{4,5},{5,4},{6,7},{7,6},{8,9},{9,8},{10,11... | collective-permute-start | bytes 196616 | tf_op jit(solution)/shard_map/ppermute | solution.py:327
  62.4 17.6 %collective-permute-start.11 = (bf16[128,256]{1,0:T(8,128)(2,1)S(1)}, bf16[128,256]{1,0:T(8,128)(2,1)S(1)}, u32[]{:S(2)}, u32[]{:S(2)}) collective-permute-start(bf16[128,256]{1,0:T(8,128)(2,1)S(1)} %get-tuple-element.39), channel_id=1, source_target_pairs={{1,2},{2,1},{3,4},{4,3},{5,6},{6,5},{7,8},{8,7},{9,10},{10,9},{11,... | collective-permute-start | bytes 196616 | tf_op jit(solution)/shard_map/ppermute | solution.py:327
  63.2 4.7 %collective-permute-start.12 = (f32[24,128]{1,0:T(8,128)S(1)}, f32[24,128]{1,0:T(8,128)S(1)}, u32[]{:S(2)}, u32[]{:S(2)}) collective-permute-start(f32[24,128]{1,0:T(8,128)S(1)} %get-tuple-element.40), channel_id=1, source_target_pairs={{0,1},{1,0},{2,3},{3,2},{4,5},{5,4},{6,7},{7,6},{8,9},{9,8},{10,11... | collective-permute-start | bytes 36872 | tf_op jit(solution)/shard_map/ppermute | solution.py:337
  67.9 3.7 %collective-permute-start.13 = (f32[24,128]{1,0:T(8,128)S(1)}, f32[24,128]{1,0:T(8,128)S(1)}, u32[]{:S(2)}, u32[]{:S(2)}) collective-permute-start(f32[24,128]{1,0:T(8,128)S(1)} %add.45), channel_id=1, source_target_pairs={{0,2},{1,3},{2,0},{3,1},{4,6},{5,7},{6,4},{7,5},{8,10},{9,11},{10,... | collective-permute-start | bytes 36872 | tf_op jit(solution)/shard_map/ppermute | solution.py:337
  71.6 3.7 %collective-permute-start.14 = (f32[24,128]{1,0:T(8,128)S(1)}, f32[24,128]{1,0:T(8,128)S(1)}, u32[]{:S(2)}, u32[]{:S(2)}) collective-permute-start(f32[24,128]{1,0:T(8,128)S(1)} %add.46), channel_id=1, source_target_pairs={{0,4},{1,5},{2,6},{3,7},{4,0},{5,1},{6,2},{7,3},{8,12},{9,13},{10,... | collective-permute-start | bytes 36872 | tf_op jit(solution)/shard_map/ppermute | solution.py:337
  75.3 4.6 %collective-permute-start.15 = (f32[24,128]{1,0:T(8,128)S(1)}, f32[24,128]{1,0:T(8,128)S(1)}, u32[]{:S(2)}, u32[]{:S(2)}) collective-permute-start(f32[24,128]{1,0:T(8,128)S(1)} %add.47), channel_id=1, source_target_pairs={{0,8},{1,9},{2,10},{3,11},{4,12},{5,13},{6,14},{7,15},{8,0},{9,1},... | collective-permute-start | bytes 36872 | tf_op jit(solution)/shard_map/ppermute | solution.py:337
  84.4 16.3 %collective-permute-start.16 = (bf16[128,128]{1,0:T(8,128)(2,1)S(1)}, bf16[128,128]{1,0:T(8,128)(2,1)S(1)}, u32[]{:S(2)}, u32[]{:S(2)}) collective-permute-start(bf16[128,128]{1,0:T(8,128)(2,1)S(1)} %get-tuple-element.43), channel_id=1, source_target_pairs={{0,1},{1,0},{2,3},{3,2},{4,5},{5,4},{6,7},{7,6},{8,9},{9,8},{10,11... | collective-permute-start | bytes 98312 | tf_op jit(solution)/shard_map/ppermute | solution.py:327
  84.4 16.3 %collective-permute-start.17 = (bf16[128,128]{1,0:T(8,128)(2,1)S(1)}, bf16[128,128]{1,0:T(8,128)(2,1)S(1)}, u32[]{:S(2)}, u32[]{:S(2)}) collective-permute-start(bf16[128,128]{1,0:T(8,128)(2,1)S(1)} %get-tuple-element.44), channel_id=1, source_target_pairs={{1,2},{2,1},{3,4},{4,3},{5,6},{6,5},{7,8},{8,7},{9,10},{10,9},{11,... | collective-permute-start | bytes 98312 | tf_op jit(solution)/shard_map/ppermute | solution.py:327
  85.1 3.9 %collective-permute-start.18 = (f32[8,128]{1,0:T(8,128)S(1)}, f32[8,128]{1,0:T(8,128)S(1)}, u32[]{:S(2)}, u32[]{:S(2)}) collective-permute-start(f32[8,128]{1,0:T(8,128)S(1)} %get-tuple-element.45), channel_id=1, source_target_pairs={{0,1},{1,0},{2,3},{3,2},{4,5},{5,4},{6,7},{7,6},{8,9},{9,8},{10,11... | collective-permute-start | bytes 12296 | tf_op jit(solution)/shard_map/ppermute | solution.py:337
  89.0 3.6 %collective-permute-start.19 = (f32[8,128]{1,0:T(8,128)S(1)}, f32[8,128]{1,0:T(8,128)S(1)}, u32[]{:S(2)}, u32[]{:S(2)}) collective-permute-start(f32[8,128]{1,0:T(8,128)S(1)} %add.49), channel_id=1, source_target_pairs={{0,2},{1,3},{2,0},{3,1},{4,6},{5,7},{6,4},{7,5},{8,10},{9,11},{10,... | collective-permute-start | bytes 12296 | tf_op jit(solution)/shard_map/ppermute | solution.py:337
  92.6 3.6 %collective-permute-start.20 = (f32[8,128]{1,0:T(8,128)S(1)}, f32[8,128]{1,0:T(8,128)S(1)}, u32[]{:S(2)}, u32[]{:S(2)}) collective-permute-start(f32[8,128]{1,0:T(8,128)S(1)} %add.50), channel_id=1, source_target_pairs={{0,4},{1,5},{2,6},{3,7},{4,0},{5,1},{6,2},{7,3},{8,12},{9,13},{10,... | collective-permute-start | bytes 12296 | tf_op jit(solution)/shard_map/ppermute | solution.py:337
  96.2 4.5 %collective-permute-start.21 = (f32[8,128]{1,0:T(8,128)S(1)}, f32[8,128]{1,0:T(8,128)S(1)}, u32[]{:S(2)}, u32[]{:S(2)}) collective-permute-start(f32[8,128]{1,0:T(8,128)S(1)} %add.51), channel_id=1, source_target_pairs={{0,8},{1,9},{2,10},{3,11},{4,12},{5,13},{6,14},{7,15},{8,0},{9,1},... | collective-permute-start | bytes 12296 | tf_op jit(solution)/shard_map/ppermute | solution.py:337

commit v2 on v1

v2 whole, which is shorter than its diff:
```python
import functools

import jax
import jax.numpy as jnp
from jax import lax
from jax.experimental import pallas as pl
from jax.experimental.pallas import tpu as pltpu
from jax.sharding import PartitionSpec as P

STRIP = 128
LANES = 128
GROUP = 8
TURNS = 16
EXTRA = 16
F32 = jnp.float32
BF16 = jnp.bfloat16
NN = (((1,), (0,)), ((), ()))
NT = (((1,), (1,)), ((), ()))
TN = (((0,), (0,)), ((), ()))
HIGHEST = lax.Precision.HIGHEST


def up(value, unit):
    return -(-value // unit) * unit


def iota(shape, dim):
    return lax.broadcasted_iota(jnp.int32, shape, dim)


def place():
    me = lax.axis_index("tile").astype(jnp.int32)
    return me, lax.rem(me, jnp.int32(2)) == 0


def ends(n):
    me, _ = place()
    return (
        jnp.where(me > 0, 1.0, 0.0).astype(F32),
        jnp.where(me < n - 1, 1.0, 0.0).astype(F32),
    )


def put_sides(even_ref, odd_ref, left, right):
    _, even = place()

    @pl.when(even)
    def _():
        even_ref[...] = right
        odd_ref[...] = left

    @pl.when(jnp.logical_not(even))
    def _():
        even_ref[...] = left
        odd_ref[...] = right


def take_sides(even_got, odd_got):
    _, even = place()
    flag = jnp.where(even, 1.0, 0.0).astype(F32)
    a, b = even_got.astype(F32), odd_got.astype(F32)
    return jnp.where(flag > 0, b, a), jnp.where(flag > 0, a, b)


def flat(ref):
    return jnp.concatenate([ref[i : i + 1, :] for i in range(ref.shape[0])], 1)


def widen(own, got_left, got_right, n):
    first, last = ends(n)
    w = STRIP
    sub = own.shape[1]
    return jnp.concatenate(
        [
            (own[:, 0:w] + got_left[:, 0:w]) * first,
            own[:, w : 2 * w] + got_left[:, w:],
            own[:, 2 * w : sub - 2 * w],
            own[:, sub - 2 * w : sub - w] + got_right[:, 0:w],
            (own[:, sub - w :] + got_right[:, w:]) * last,
        ],
        1,
    )


def rows_of(columns, count):
    rhs = columns[0][1].shape[0]
    wide = up(count, LANES)
    lane = iota((rhs, wide), 1)
    total = jnp.zeros((rhs, wide), F32)
    for slot, column in columns:
        total = total + jnp.where(lane == slot, jnp.broadcast_to(column, (rhs, wide)), 0.0)
    return jnp.transpose(total)[0:count]


def rowsum(x):
    return jnp.sum(x, axis=1, keepdims=True)


def coarse_columns(n, sums, cinv_ref, reach):
    me, _ = place()
    shape = (n, LANES)
    lane = iota(shape, 1)
    pick = (iota(shape, 0) == me - reach + lane) & (lane <= 2 * reach)
    columns = jnp.dot(
        cinv_ref[...], jnp.where(pick, 1.0, 0.0), precision=HIGHEST, preferred_element_type=F32
    )
    return lax.dot_general(sums, columns, TN, precision=HIGHEST, preferred_element_type=F32)


def begin_kernel(n, rhs_ref, cvec_ref, even_ref, odd_ref, part_ref):
    me, _ = place()
    rhs, own = rhs_ref.shape
    slots = part_ref.shape[0]
    cvec = flat(cvec_ref)
    part = rows_of([(me, rowsum(rhs_ref[...] * cvec))], slots)
    part_ref[...] = part

    def side(start):
        pad = jnp.zeros((7, STRIP), F32)
        cols = slice(start, start + STRIP)
        return jnp.concatenate([rhs_ref[:, cols], cvec[:, cols], pad, part], 0)

    put_sides(even_ref, odd_ref, side(0), side(own - STRIP))


def build_kernel(rows_s, rows_v, lane_v, weight_v, o_ref, *scratch):
    merged, tables = scratch[0], scratch[1:]
    own, sub = o_ref.shape
    edges = merged.shape[0]
    blocks = edges // LANES
    panels = sub // LANES
    height = panels * own
    chunk = up(-(-height // blocks), 8)

    fill = up(blocks, LANES) - blocks
    turned = jnp.transpose(
        jnp.concatenate([rows_v[...], jnp.zeros((fill, LANES), jnp.int32)], 0)
    )
    square = (LANES, LANES)
    down, across = iota(square, 0), iota(square, 1)
    same_group = (down // GROUP) == (across // GROUP)
    for k in range(blocks):
        low = min(k * chunk, height)
        high = min(low + chunk, height)
        if high > low:
            for acc in tables:
                acc[low:high, :] = jnp.zeros((high - low, LANES), F32)
        equal = jnp.broadcast_to(turned[:, k : k + 1], square) == jnp.broadcast_to(
            rows_v[k : k + 1, :], square
        )
        equal = jnp.where(equal & same_group, 1.0, 0.0).astype(BF16)
        hit = down == jnp.broadcast_to(lane_v[k : k + 1, :], square)
        spread = jnp.where(hit, jnp.broadcast_to(weight_v[k : k + 1, :], square), 0.0)
        merged[k * LANES : (k + 1) * LANES, :] = lax.dot_general(
            equal, spread.astype(BF16), NT, preferred_element_type=F32
        )

    def add(g, _):
        for q in range(TURNS):
            acc = tables[q % len(tables)]
            base = (g * TURNS + q) * GROUP
            at = [rows_s[base + i] for i in range(GROUP)]
            new = merged[pl.ds(pl.multiple_of(base, GROUP), GROUP), :]
            out = [acc[pl.ds(at[i], 1), :] + new[i : i + 1, :] for i in range(GROUP)]
            for i in range(GROUP):
                acc[pl.ds(at[i], 1), :] = out[i]
        return 0

    lax.fori_loop(0, edges // (GROUP * TURNS), add, 0)

    tall = 256

    def narrow(i, _):
        for p in range(panels):
            rows = pl.ds(pl.multiple_of(p * own + i * tall, tall), tall)
            value = tables[0][rows, :]
            for acc in tables[1:]:
                value = value + acc[rows, :]
            o_ref[pl.ds(pl.multiple_of(i * tall, tall), tall), p * LANES : (p + 1) * LANES] = (
                value.astype(BF16)
            )
        return 0

    lax.fori_loop(0, own // tall, narrow, 0)


def local_solve(u_ref, wide, inv_ref):
    tall = 256
    for j in range(u_ref.shape[1] // tall):
        cols = slice(j * tall, (j + 1) * tall)
        u_ref[:, cols] = jnp.dot(wide, inv_ref[:, cols], preferred_element_type=F32)


def put_strips(even_ref, odd_ref, ref):
    width = even_ref.shape[1]
    sub = ref.shape[1]
    put_sides(
        even_ref, odd_ref, ref[:, 0:width].astype(BF16), ref[:, sub - width :].astype(BF16)
    )


def first_solve_kernel(
    rhs_ref, even_got, odd_got, inv_ref, sum_ref, sum_got, u_ref, even_ref, odd_ref, sum_out
):
    rhs = rhs_ref.shape[0]
    left, right = take_sides(even_got[0:rhs, :], odd_got[0:rhs, :])
    wide = jnp.concatenate([left, rhs_ref[...], right], 1).astype(BF16)
    local_solve(u_ref, wide, inv_ref)
    put_strips(even_ref, odd_ref, u_ref)
    sum_out[...] = sum_ref[...] + sum_got[...]


def product(wide_ref, o_ref, deg, mass, out_ref):
    rows, sub = wide_ref.shape
    own = sub - 2 * STRIP
    tall = 256
    high = wide_ref[...].astype(BF16)
    mine = high[:, STRIP : STRIP + own]
    sides = jnp.concatenate([o_ref[:, 0:STRIP], o_ref[:, sub - STRIP :]], 1)
    thru = lax.dot_general(mine, sides, NN, preferred_element_type=F32)
    for part, start in ((thru[:, 0:STRIP], 0), (thru[:, STRIP:], sub - STRIP)):
        cols = slice(start, start + STRIP)
        out_ref[:, cols] = wide_ref[:, cols] * deg(part, cols) - part
    for j in range(own // tall):
        cols = slice(STRIP + j * tall, STRIP + (j + 1) * tall)
        part = lax.dot_general(mine, o_ref[:, cols], NN, preferred_element_type=F32)
        part = part + lax.dot_general(
            high, o_ref[j * tall : (j + 1) * tall, :], NT, preferred_element_type=F32
        )
        diag = deg(part, cols) + mass[:, j * tall : (j + 1) * tall]
        out_ref[:, cols] = wide_ref[:, cols] * diag - part


def first_apply_kernel(
    n, u_ref, even_got, odd_got, halo_even, halo_odd, o_ref, cvec_ref, mass_ref, sum_ref, sum_got,
    s_ref, y_ref, deg_ref, even_ref, odd_ref, sum_out, wide_ref,
):
    rhs, sub = u_ref.shape
    own = sub - 2 * STRIP
    left, right = take_sides(even_got[...], odd_got[...])
    vec_left, vec_right = take_sides(halo_even[rhs : rhs + 1, :], halo_odd[rhs : rhs + 1, :])
    wide_ref[0:rhs, :] = widen(u_ref, left, right, n)
    cvec = jnp.concatenate([vec_left, flat(cvec_ref), vec_right], 1)
    lane = iota((1, sub), 1)
    wide_ref[rhs:, :] = jnp.concatenate(
        [
            jnp.where(lane < STRIP, cvec, 0.0),
            jnp.where((lane >= STRIP) & (lane < STRIP + own), cvec, 0.0),
            jnp.where(lane >= STRIP + own, cvec, 0.0),
            jnp.ones((1, sub), F32),
            jnp.zeros((EXTRA - 4, sub), F32),
        ],
        0,
    )

    def degree(part, cols):
        row = part[rhs + 3 : rhs + 4, :]
        deg_ref[:, cols] = jnp.broadcast_to(row, (8, row.shape[1]))
        return row

    product(wide_ref, o_ref, degree, flat(mass_ref), y_ref)
    s_ref[...] = wide_ref[0:rhs, STRIP : sub - STRIP]
    put_strips(even_ref, odd_ref, y_ref)
    sum_out[...] = sum_ref[...] + sum_got[...]


def add_coarse(value, vectors, coarse, first):
    for k in range(3):
        lane = first + k
        value = value + coarse[:, lane : lane + 1] * vectors[k : k + 1, :]
    return value


def next_solve_kernel(
    n, y_ref, even_got, odd_got, sums_ref, cinv_ref, inv_ref, own_ref, u_ref, even_ref, odd_ref
):
    rhs = u_ref.shape[0]
    sub = u_ref.shape[1]
    coarse = coarse_columns(n, sums_ref[0:n, :], cinv_ref, 2)
    left, right = take_sides(even_got[...], odd_got[...])
    left = add_coarse(left[0:rhs], left[rhs : rhs + 3], coarse, 0)
    right = add_coarse(right[0:rhs], right[rhs : rhs + 3], coarse, 2)
    value = add_coarse(y_ref[0:rhs, :], y_ref[rhs : rhs + 3, :], coarse, 1)
    wide = widen(value, left, right, n)
    own_ref[...] = wide[:, STRIP : sub - STRIP]
    local_solve(u_ref, wide.astype(BF16), inv_ref)
    put_strips(even_ref, odd_ref, u_ref)


def between_kernel(
    n, s_ref, y_ref, coarse_rows, even_got, odd_got, sums_ref, cinv_ref, cvec_ref, rhs_ref,
    z_ref, g_ref, part_ref,
):
    me, _ = place()
    rhs, own = s_ref.shape
    sub = own + 2 * STRIP
    slots = up(n, 8)
    coarse = coarse_columns(n, sums_ref[0:n, :], cinv_ref, 0)
    cvec = flat(cvec_ref)
    z = s_ref[...] + coarse[:, 0:1] * cvec
    z_ref[...] = z
    left, right = take_sides(even_got[rhs:, STRIP:], odd_got[rhs:, STRIP:])
    unused, right = take_sides(even_got[rhs:, 0:STRIP], odd_got[rhs:, 0:STRIP])
    mine = coarse_rows[rhs:, STRIP : sub - STRIP]
    lefts = [left[1:2, :], left[2:3, :], None]
    rights = [None, right[0:1, :], right[1:2, :]]
    rows = []
    for k in range(3):
        head, body, tail = (
            mine[k : k + 1, 0:STRIP],
            mine[k : k + 1, STRIP : own - STRIP],
            mine[k : k + 1, own - STRIP :],
        )
        if lefts[k] is not None:
            head = head + lefts[k]
        if rights[k] is not None:
            tail = tail + rights[k]
        rows.append(jnp.concatenate([head, body, tail], 1))
    g = jnp.concatenate(rows + [jnp.zeros((5, own), F32)], 0)
    g_ref[...] = g
    part_ref[0:slots, :] = rows_of([(me, rowsum(y_ref[...] * cvec))], slots)
    shape = (slots, rhs)
    here = iota(shape, 0) == me
    inner = rowsum(g * cvec)
    total = jnp.zeros(shape, F32)
    for k in range(3):
        take = here & (iota(shape, 1) == k)
        total = total + jnp.where(take, jnp.broadcast_to(inner[k : k + 1, :], shape), 0.0)
    part_ref[slots : 2 * slots, :] = total
    a, b = rowsum(rhs_ref[...] * s_ref[...]), rowsum(z * y_ref[...])
    part_ref[2 * slots :, :] = rows_of([(0, a), (1, b)], 8)


def next_apply_kernel(
    n, u_ref, even_got, odd_got, o_ref, deg_ref, mass_ref, rhs_ref, y_ref, g_ref, part_in,
    w_ref, q_ref, even_ref, odd_ref, part_ref, wide_ref, out_ref,
):
    me, _ = place()
    rhs, sub = u_ref.shape
    own = sub - 2 * STRIP
    slots = up(n, 8)
    left, right = take_sides(even_got[...], odd_got[...])
    wide_ref[...] = widen(u_ref, left, right, n)
    product(wide_ref, o_ref, lambda part, cols: deg_ref[0:1, cols], flat(mass_ref), out_ref)
    w = wide_ref[:, STRIP : sub - STRIP]
    w_ref[...] = w
    q_ref[...] = out_ref[:, STRIP : sub - STRIP]
    c = rowsum(rhs_ref[...] * w)
    d = rowsum(y_ref[...] * w)
    e = rowsum(wide_ref[...] * out_ref[...])
    cross = [(me - 1 + k, rowsum(w * g_ref[k : k + 1, :])) for k in range(3)]
    part_ref[0 : 2 * slots, :] = part_in[0 : 2 * slots, :]
    part_ref[2 * slots : 3 * slots, :] = rows_of(cross, slots)
    part_ref[3 * slots :, :] = part_in[2 * slots :, :] + rows_of([(2, c), (3, d), (4, e)], 8)
    _, even = place()

    @pl.when(even)
    def _():
        even_ref[0:rhs, :] = out_ref[:, sub - STRIP :]
        odd_ref[...] = out_ref[:, 0:STRIP]

    @pl.when(jnp.logical_not(even))
    def _():
        even_ref[0:rhs, :] = out_ref[:, 0:STRIP]
        odd_ref[...] = out_ref[:, sub - STRIP :]

    even_ref[rhs:, :] = part_ref[...]


def finish_kernel(
    n, rhs_ref, z_ref, y_ref, w_ref, q_ref, g_ref, even_got, odd_got, first_ref, part_ref,
    cinv_ref, cvec_ref, x_ref, r_ref,
):
    me, _ = place()
    rhs, own = rhs_ref.shape
    slots = up(n, 8)
    first = first_ref[0:n, :]
    rho, cross = part_ref[0:n, :], part_ref[2 * slots : 2 * slots + n, :]
    gram = part_ref[slots : slots + n, :]
    sums = part_ref[3 * slots :, :]
    exact = dict(precision=HIGHEST, preferred_element_type=F32)

    def over(x):
        return jnp.sum(x, axis=0, keepdims=True)

    start = lax.dot_general(cinv_ref[...], first, TN, **exact)
    level = lax.dot_general(cinv_ref[...], rho, TN, **exact)
    shape = (n, n)
    band = jnp.zeros(shape, F32)
    for k in range(3):
        take = iota(shape, 1) == iota(shape, 0) + (k - 1)
        band = band + jnp.where(take, jnp.broadcast_to(gram[:, k : k + 1], shape), 0.0)
    bent = jnp.dot(band, level, **exact)

    a = sums[0:1, :] + over(start * first)
    b = sums[1:2, :]
    c = sums[2:3, :] + over(level * first)
    d = sums[3:4, :] + over(level * rho)
    e = sums[4:5, :] + over(level * (2.0 * cross + bent))
    alpha = a / b
    following = a - alpha * (c + b) + alpha * alpha * d
    beta = following / a
    between = b - alpha * d
    energy = (b - 2.0 * alpha * d + alpha * alpha * e) + 2.0 * beta * between + beta * beta * b
    step = following / energy
    near = jnp.transpose(jnp.broadcast_to(alpha + step * (1.0 + beta), (LANES, rhs)))[:, 0:1]
    far = jnp.transpose(jnp.broadcast_to(alpha * step, (LANES, rhs)))[:, 0:1]
    coarse = coarse_columns(n, rho, cinv_ref, 1) * far
    x_ref[...] = near * z_ref[...] - far * w_ref[...] - coarse[:, 1:2] * flat(cvec_ref)
    left, right = take_sides(even_got[0:rhs, :], odd_got[...])
    r_ref[...] = add_coarse(
        rhs_ref[...] - near * y_ref[...] + far * q_ref[...], g_ref[...], coarse, 0
    )
    r_ref[:, 0:STRIP] += far * left
    r_ref[:, own - STRIP :] += far * right


def call(kernel, name, outs, scratch, limit, count, in_specs=None, flops=0):
    vmem = pl.BlockSpec(memory_space=pltpu.VMEM)
    return pl.pallas_call(
        kernel,
        out_shape=[jax.ShapeDtypeStruct(s, d) for s, d in outs],
        in_specs=in_specs if in_specs is not None else [vmem] * count,
        out_specs=[vmem] * len(outs),
        scratch_shapes=scratch,
        compiler_params=pltpu.CompilerParams(vmem_limit_bytes=limit << 20),
        cost_estimate=pl.CostEstimate(flops=flops, bytes_accessed=0, transcendentals=0),
        name=name,
    )


def swap(pair):
    n = lax.axis_size("tile")
    got = []
    for start, payload in zip((0, 1), pair):
        links = []
        for i in range(start, n - 1, 2):
            links += [(i, i + 1), (i + 1, i)]
        got.append(lax.ppermute(payload, "tile", links))
    return got


def across(part, hop):
    n = lax.axis_size("tile")
    if hop >= n:
        return jnp.zeros_like(part)
    return lax.ppermute(part, "tile", [(i, i ^ hop) for i in range(n)])


def finish_sum(part, hop):
    while hop < lax.axis_size("tile"):
        part = part + across(part, hop)
        hop *= 2
    return part


def shards(
    rhs, mass_diag, edge_heads, edge_tails, edge_weight, local_inverse, coarse_vec, coarse_inv
):
    n = lax.axis_size("tile")
    if n < 2 or n & (n - 1):
        raise ValueError("tile axis")
    rows, own = rhs.shape
    sub = local_inverse.shape[1]
    edges = edge_heads.shape[0]
    slots = up(n, 8)
    cvec, mass = coarse_vec.reshape(-1, LANES), mass_diag.reshape(-1, LANES)
    vmem = pl.BlockSpec(memory_space=pltpu.VMEM)
    smem = pl.BlockSpec(memory_space=pltpu.SMEM)
    bind = functools.partial

    side = ((rows + 8 + slots, STRIP), F32)
    few = ((slots, rows), F32)
    even, odd, part = call(bind(begin_kernel, n), "begin", [side, side, few], [], 4, 2)(rhs, cvec)
    halo = swap((even, odd))
    part = part + halo[0][rows + 8 :]

    at = (edge_tails >> 7) * own + (edge_heads - STRIP)
    shape = (edges // LANES, LANES)
    (stiff,) = call(
        build_kernel,
        "build",
        [((own, sub), BF16)],
        [pltpu.VMEM((edges, LANES), F32)] + [pltpu.VMEM((sub // LANES * own, LANES), F32)] * 2,
        34,
        4,
        in_specs=[smem, vmem, vmem, vmem],
        flops=10**10,
    )(at, at.reshape(shape), (edge_tails & 127).reshape(shape), edge_weight.reshape(shape))

    whole, owned = ((rows, sub), F32), ((rows, own), F32)
    strip = ((rows, 2 * STRIP), BF16)
    extra = ((rows + EXTRA, sub), F32)
    u, even, odd, part = call(
        first_solve_kernel, "solve", [whole, strip, strip, few], [], 12, 6, flops=10**9
    )(rhs, *halo, local_inverse, part, across(part, 2))
    got = swap((even, odd))
    strips = ((rows + EXTRA, 2 * STRIP), BF16)
    s, y_part, degree, even, odd, part = call(
        bind(first_apply_kernel, n),
        "apply",
        [owned, extra, ((8, sub), F32), strips, strips, few],
        [pltpu.VMEM(*extra)],
        12,
        10,
        flops=2 * 10**9,
    )(u, *got, *halo, stiff, cvec, mass, part, across(part, 4))
    got_y = swap((even, odd))
    sums = finish_sum(part, 8)
    y, u, even, odd = call(
        bind(next_solve_kernel, n), "solve2", [owned, whole, strip, strip], [], 12, 6, flops=10**9
    )(y_part, *got_y, sums, coarse_inv, local_inverse)
    got = swap((even, odd))
    z, g, part = call(
        bind(between_kernel, n),
        "between",
        [owned, ((8, own), F32), ((2 * slots + 8, rows), F32)],
        [],
        8,
        9,
        flops=10**9,
    )(s, y, y_part, *got_y, sums, coarse_inv, cvec, rhs)
    many = 3 * slots + 8
    w, q, even, odd, part = call(
        bind(next_apply_kernel, n),
        "apply2",
        [owned, owned, ((rows + many, STRIP), F32), ((rows, STRIP), F32), ((many, rows), F32)],
        [pltpu.VMEM(*whole), pltpu.VMEM(*whole)],
        12,
        10,
        flops=2 * 10**9,
    )(u, *got, stiff, degree, mass, rhs, y, g, part)
    got = swap((even, odd))
    part = finish_sum(part + got[0][rows:], 2)
    return tuple(
        call(bind(finish_kernel, n), "finish", [owned, owned], [], 16, 12)(
            rhs, z, y, w, q, g, *got, sums, part, coarse_inv, cvec
        )
    )


def solution(mesh):
    return jax.shard_map(
        shards,
        mesh=mesh,
        in_specs=(
            P("grp", "tile"),
            P("tile"),
            P("tile"),
            P("tile"),
            P("tile"),
            P("tile", None),
            P("tile"),
            P(),
        ),
        out_specs=(P("grp", "tile"), P("grp", "tile")),
        check_vma=False,
    )
```

time: 103 us -> 75.9 us (0.74)
  starting transfers between devices: 38.2 us -> 28.7 us
  waiting for transfers between devices: 20.9 us -> 11.7 us
  Pallas kernels: 35.1 us -> 26.9 us
    ppermute x12 -> x6, waiting for transfers between devices: 20.7 us -> 10.5 us  [across(): return lax.ppermute(part, 'tile', [(i, i ^ hop) for i in range(n)])]
    ppermute x12 -> x6, starting transfers between devices: 26.5 us -> 17.7 us  [across(): return lax.ppermute(part, 'tile', [(i, i ^ hop) for i in range(n)])]
    pallas_call x7 -> x8, Pallas kernels: 35.1 us -> 26.9 us  [the longest x1 12.5 us: shards(): call(build_kernel, 'build', [((own, sub), BF16)], [pltpu.VMEM((edges, LAN...]
    broadcast_in_dim x2 -> x0, local copies, waits for them, and re-layouts: 1.41 us -> none  [shards(): cvec, mass = (coarse_vec[None, :], mass_diag[None, :])]
    unnamed x20 -> x22, local copies, waits for them, and re-layouts: 5.77 us -> 6.47 us
  transfers between devices with their start and end apart: 22 -> 16, of which waited for: 12 -> 7; matrix products, arithmetic and copies ran while one was open for 0% -> 1% of each run, Pallas kernels for 22% -> 18%
where the time goes in v2:
time: 75.9 us; the launch traced here: 75.4 us
  starting transfers between devices  28.7 us (38%)
  Pallas kernels  26.9 us (35%)
  waiting for transfers between devices  11.7 us (15%)
  local copies, waits for them, and re-layouts  6.47 us (9%)
  between operations  0.88 us (1%)
  other arithmetic  0.8 us (1%)
    ppermute x6, starting transfers between devices, across(): return lax.ppermute(part, 'tile', [(i, i ^ hop) for i in range(n)])  17.7 us
    pallas_call x1, Pallas kernels, shards(): call(build_kernel, 'build', [((own, sub), BF16)], [pltpu.VMEM((edges, LAN...  12.5 us
    ppermute x10, starting transfers between devices, swap(): got.append(lax.ppermute(payload, 'tile', links))  11 us
    ppermute x6, waiting for transfers between devices, across(): return lax.ppermute(part, 'tile', [(i, i ^ hop) for i in range(n)])  10.5 us
    unnamed x22, local copies, waits for them, and re-layouts  6.47 us
    pallas_call x1, Pallas kernels, shards(): call(bind(next_apply_kernel, n), 'apply2', [owned, owned, ((rows + many,...  4.02 us
    pallas_call x1, Pallas kernels, shards(): call(bind(first_apply_kernel, n), 'apply', [owned, extra, ((8, sub), F32)...  3.76 us
    pallas_call x1, Pallas kernels, shards(): call(bind(finish_kernel, n), 'finish', [owned, owned], [], 16, 12)  2.39 us
  transfers between devices with their start and end apart: 16, of which 7 were waited for; matrix products, arithmetic and copies ran while one was open for 1% of the time, Pallas kernels for 18%

profile of v2, /device:TPU:0, one launch (start us, length us, event | category | flops | bytes accessed | tf_op | source)
XLA Modules:
  0.0 75.4 jit_solution(1227118498816537019)
XLA Ops:
  0.6 1.2 %copy-done.1 = f32[128,1792]{1,0:T(8,128)S(1)} copy-done((f32[128,1792]{1,0:T(8,128)S(1)}, f32[128,1792]{1,0:T(8,128)}, u32[]{:S(2)}) %copy-start.1) | copy-done | bytes 917528
  1.8 0.7 copy-done.4
  2.7 0.6 collective-permute-start
  3.3 0.7 collective-permute-start.1
  4.2 3.5 %collective-permute-start.2 = (f32[16,128]{1,0:T(8,128)S(1)}, f32[16,128]{1,0:T(8,128)S(1)}, u32[]{:S(2)}, u32[]{:S(2)}) collective-permute-start(f32[16,128]{1,0:T(8,128)S(1)} %slice_add_fusion.1.sum_ref), channel_id=1, source_target_pairs={{0,2},{1,3},{2,0},{3,1},{4,6},{5,7},{6,4},{7,5},{8,10},{9,11},{10,... | collective-permute-start | bytes 24584 | tf_op jit(solution)/shard_map/ppermute | solution.py:447
  7.7 0.8 %and_bitcast_fusion = (s32[56,128]{1,0:T(8,128)S(1)}, s32[7168]{0:T(1024)S(1)}) fusion(s32[7168]{0:T(1024)} %param.11, s32[7168]{0:T(1024)} %param.10), kind=kLoop, calls=%fused_computation.1 | loop fusion | flops 35840 | bytes 114688 | tf_op jit(solution)/shard_map/reshape | solution.py:489
  8.5 1.6 %collective-permute-done.2.sum_got = f32[16,128]{1,0:T(8,128)S(1)} collective-permute-done((f32[16,128]{1,0:T(8,128)S(1)}, f32[16,128]{1,0:T(8,128)S(1)}, u32[]{:S(2)}, u32[]{:S(2)}) %collective-permute-start.2) | collective-permute-done | bytes 8224 | tf_op jit(solution)/shard_map/ppermute | solution.py:447
  10.1 3.4 %copy-done = bf16[2048,2048]{1,0:T(8,128)(2,1)S(1)} copy-done((bf16[2048,2048]{1,0:T(8,128)(2,1)S(1)}, bf16[2048,2048]{1,0:T(8,128)(2,1)}, u32[]{:S(2)}) %copy-start) | copy-done | bytes 8388632
  13.5 1.2 %copy-done.2 = f32[128,1792]{1,0:T(8,128)S(1)} copy-done((f32[128,1792]{1,0:T(8,128)S(1)}, f32[128,1792]{1,0:T(8,128)}, u32[]{:S(2)}) %copy-start.2) | copy-done | bytes 917528
  14.6 1.4 %solve.1 = (f32[128,2048]{1,0:T(8,128)S(1)}, bf16[128,256]{1,0:T(8,128)(2,1)S(1)}, bf16[128,256]{1,0:T(8,128)(2,1)S(1)}, f32[16,128]{1,0:T(8,128)S(1)}) custom-call(f32[128,1792]{1,0:T(8,128)S(1)} %copy-done.2, f32[152,128]{1,0:T(8,128)S(1)} %collective-permute-done.even_got.halo_even, f32[152,128]{1,0:T(8,128)S(1)} %collective-permute-done.1.odd_got.halo_odd, ...), custom_call_target="tpu_custom_call" | custom-call | flops 1000000000 | tf_op jit(solution)/shard_map/solve/pallas_call | solution.py:494
  16.0 3.2 %collective-permute-start.5 = (f32[16,128]{1,0:T(8,128)S(1)}, f32[16,128]{1,0:T(8,128)S(1)}, u32[]{:S(2)}, u32[]{:S(2)}) collective-permute-start(f32[16,128]{1,0:T(8,128)S(1)} %get-tuple-element.33.sum_ref), channel_id=1, source_target_pairs={{0,4},{1,5},{2,6},{3,7},{4,0},{5,1},{6,2},{7,3},{8,12},{9,13},{10,... | collective-permute-start | bytes 24584 | tf_op jit(solution)/shard_map/ppermute | solution.py:447
  19.2 0.7 collective-permute-start.4
  19.9 12.5 %build.1.o_ref = bf16[1792,2048]{1,0:T(8,128)(2,1)S(1)} custom-call(s32[7168]{0:T(1024)S(1)} %get-tuple-element.53.rows_s, s32[56,128]{1,0:T(8,128)S(1)} %bitcast.14, s32[56,128]{1,0:T(8,128)S(1)} %get-tuple-element.52.lane_v, f32[56,128]{1,0:T(8,128)S(1)} %bitcast.15), custom_call_target="tpu_custom_call" | custom-call | flops 10000000000 | tf_op jit(solution)/shard_map/build/pallas_call | solution.py:480
  32.5 3.8 %apply.1 = (f32[128,1792]{1,0:T(8,128)S(1)}, f32[144,2048]{1,0:T(8,128)S(1)}, f32[8,2048]{1,0:T(8,128)S(1)}, bf16[144,256]{1,0:T(8,128)(2,1)S(1)}, bf16[144,256]{1,0:T(8,128)(2,1)S(1)}, /*index=5*/f32[16,128]{1,0:T(8,128)S(1)}) custom-call(f32[128,2048]{1,0:T(8,128)S(1)} %get-tuple-element.30.u_ref, bf16[128,256]{1,0:T(8,128)(2,1)S(1)} %collective-permute-done.3.even_got, ...), custom_call_target="tpu_custom_call" | custom-call | flops 2000000000 | tf_op jit(solution)/shard_map/apply/pallas_call | solution.py:499
  36.2 2.4 %collective-permute-start.6 = (bf16[144,256]{1,0:T(8,128)(2,1)S(1)}, bf16[144,256]{1,0:T(8,128)(2,1)S(1)}, u32[]{:S(2)}, u32[]{:S(2)}) collective-permute-start(bf16[144,256]{1,0:T(8,128)(2,1)S(1)} %get-tuple-element.36), channel_id=1, source_target_pairs={{0,1},{1,0},{2,3},{3,2},{4,5},{5,4},{6,7},{7,6},{8,9},{9,8},{10,11... | collective-permute-start | bytes 221192 | tf_op jit(solution)/shard_map/ppermute | solution.py:439
  38.6 0.7 collective-permute-start.7
  39.3 5.5 %collective-permute-start.8 = (f32[16,128]{1,0:T(8,128)S(1)}, f32[16,128]{1,0:T(8,128)S(1)}, u32[]{:S(2)}, u32[]{:S(2)}) collective-permute-start(f32[16,128]{1,0:T(8,128)S(1)} %get-tuple-element.38), channel_id=1, source_target_pairs={{0,8},{1,9},{2,10},{3,11},{4,12},{5,13},{6,14},{7,15},{8,0},{9,1},... | collective-permute-start | bytes 24584 | tf_op jit(solution)/shard_map/ppermute | solution.py:447
  44.8 2.3 %collective-permute-done.8 = f32[16,128]{1,0:T(8,128)S(1)} collective-permute-done((f32[16,128]{1,0:T(8,128)S(1)}, f32[16,128]{1,0:T(8,128)S(1)}, u32[]{:S(2)}, u32[]{:S(2)}) %collective-permute-start.8) | collective-permute-done | bytes 8224 | tf_op jit(solution)/shard_map/ppermute | solution.py:447
  47.2 1.9 %solve2.1 = (f32[128,1792]{1,0:T(8,128)S(1)}, f32[128,2048]{1,0:T(8,128)S(1)}, bf16[128,256]{1,0:T(8,128)(2,1)S(1)}, bf16[128,256]{1,0:T(8,128)(2,1)S(1)}) custom-call(f32[144,2048]{1,0:T(8,128)S(1)} %get-tuple-element.35.y_ref.coarse_rows, bf16[144,256]{1,0:T(8,128)(2,1)S(1)} %collective-permute-done.6.even_got, ...), custom_call_target="tpu_custom_call" | custom-call | flops 1000000000 | tf_op jit(solution)/shard_map/solve2/pallas_call | solution.py:510
  49.2 0.8 %collective-permute-start.10 = (bf16[128,256]{1,0:T(8,128)(2,1)S(1)}, bf16[128,256]{1,0:T(8,128)(2,1)S(1)}, u32[]{:S(2)}, u32[]{:S(2)}) collective-permute-start(bf16[128,256]{1,0:T(8,128)(2,1)S(1)} %get-tuple-element.43), channel_id=1, source_target_pairs={{1,2},{2,1},{3,4},{4,3},{5,6},{6,5},{7,8},{8,7},{9,10},{10,9},{11,... | collective-permute-start | bytes 196616 | tf_op jit(solution)/shard_map/ppermute | solution.py:439
  50.1 0.7 between.1
  50.8 4.0 %apply2.1 = (f32[128,1792]{1,0:T(8,128)S(1)}, f32[128,1792]{1,0:T(8,128)S(1)}, f32[184,128]{1,0:T(8,128)S(1)}, f32[128,128]{1,0:T(8,128)S(1)}, f32[56,128]{1,0:T(8,128)S(1)}) custom-call(f32[128,2048]{1,0:T(8,128)S(1)} %get-tuple-element.41.u_ref, bf16[128,256]{1,0:T(8,128)(2,1)S(1)} %collective-permute-done.9.even_got, ...), custom_call_target="tpu_custom_call" | custom-call | flops 2000000000 | tf_op jit(solution)/shard_map/apply2/pallas_call | solution.py:524
  54.8 4.5 %collective-permute-start.11 = (f32[184,128]{1,0:T(8,128)S(1)}, f32[184,128]{1,0:T(8,128)S(1)}, u32[]{:S(2)}, u32[]{:S(2)}) collective-permute-start(f32[184,128]{1,0:T(8,128)S(1)} %get-tuple-element.49), channel_id=1, source_target_pairs={{0,1},{1,0},{2,3},{3,2},{4,5},{5,4},{6,7},{7,6},{8,9},{9,8},{10,11... | collective-permute-start | bytes 282632 | tf_op jit(solution)/shard_map/ppermute | solution.py:439
  59.4 0.9 %collective-permute-done.11.even_got = f32[184,128]{1,0:T(8,128)S(1)} collective-permute-done((f32[184,128]{1,0:T(8,128)S(1)}, f32[184,128]{1,0:T(8,128)S(1)}, u32[]{:S(2)}, u32[]{:S(2)}) %collective-permute-start.11) | collective-permute-done | bytes 94240 | tf_op jit(solution)/shard_map/ppermute | solution.py:439
  60.3 0.6 collective-permute-start.13
  60.9 0.7 collective-permute-start.12
  61.5 2.6 %collective-permute-done.13 = f32[56,128]{1,0:T(8,128)S(1)} collective-permute-done((f32[56,128]{1,0:T(8,128)S(1)}, f32[56,128]{1,0:T(8,128)S(1)}, u32[]{:S(2)}, u32[]{:S(2)}) %collective-permute-start.13) | collective-permute-done | bytes 28704 | tf_op jit(solution)/shard_map/ppermute | solution.py:447
  64.2 2.0 %collective-permute-start.14 = (f32[56,128]{1,0:T(8,128)S(1)}, f32[56,128]{1,0:T(8,128)S(1)}, u32[]{:S(2)}, u32[]{:S(2)}) collective-permute-start(f32[56,128]{1,0:T(8,128)S(1)} %add.26), channel_id=1, source_target_pairs={{0,4},{1,5},{2,6},{3,7},{4,0},{5,1},{6,2},{7,3},{8,12},{9,13},{10,... | collective-permute-start | bytes 86024 | tf_op jit(solution)/shard_map/ppermute | solution.py:447
  66.1 2.1 %collective-permute-done.14 = f32[56,128]{1,0:T(8,128)S(1)} collective-permute-done((f32[56,128]{1,0:T(8,128)S(1)}, f32[56,128]{1,0:T(8,128)S(1)}, u32[]{:S(2)}, u32[]{:S(2)}) %collective-permute-start.14) | collective-permute-done | bytes 28704 | tf_op jit(solution)/shard_map/ppermute | solution.py:447
  68.2 2.9 %collective-permute-start.15 = (f32[56,128]{1,0:T(8,128)S(1)}, f32[56,128]{1,0:T(8,128)S(1)}, u32[]{:S(2)}, u32[]{:S(2)}) collective-permute-start(f32[56,128]{1,0:T(8,128)S(1)} %add.27), channel_id=1, source_target_pairs={{0,8},{1,9},{2,10},{3,11},{4,12},{5,13},{6,14},{7,15},{8,0},{9,1},... | collective-permute-start | bytes 86024 | tf_op jit(solution)/shard_map/ppermute | solution.py:447
  71.1 1.9 %collective-permute-done.15 = f32[56,128]{1,0:T(8,128)S(1)} collective-permute-done((f32[56,128]{1,0:T(8,128)S(1)}, f32[56,128]{1,0:T(8,128)S(1)}, u32[]{:S(2)}, u32[]{:S(2)}) %collective-permute-start.15) | collective-permute-done | bytes 28704 | tf_op jit(solution)/shard_map/ppermute | solution.py:447
  73.0 2.4 %finish.1 = (f32[128,1792]{1,0:T(8,128)}, f32[128,1792]{1,0:T(8,128)}) custom-call(f32[128,1792]{1,0:T(8,128)S(1)} %copy-done.3, f32[128,1792]{1,0:T(8,128)S(1)} %get-tuple-element.40.z_ref, f32[128,1792]{1,0:T(8,128)S(1)} %get-tuple-element.39.y_ref, f32[128,1792]{1,0:T(8,128)S(1)} %get-tuple-element.47.w_ref, f32[128,1792]{1,0:T(8,128)S(1)} %get-tuple-element.48.q_ref, ...), custom_call_target="tpu_custom_call" | custom-call | tf_op jit(solution)/shard_map/finish/pallas_call | solution.py:536
  (38 shorter events, 0.6 us)
Async XLA Ops:
  0.6 1.2 %copy-start.1 = (f32[128,1792]{1,0:T(8,128)S(1)}, f32[128,1792]{1,0:T(8,128)}, u32[]{:S(2)}) copy-start(f32[128,1792]{1,0:T(8,128)} %rhs_ref.9) | copy-start | bytes 2752516
  1.8 0.7 copy-start.4
  2.5 17.4 %copy-start.8 = (f32[7168]{0:T(1024)S(1)}, f32[7168]{0:T(1024)}, u32[]{:S(2)}) copy-start(f32[7168]{0:T(1024)} %param.12) | copy-start | bytes 86020
  2.7 1.5 %collective-permute-start = (f32[152,128]{1,0:T(8,128)S(1)}, f32[152,128]{1,0:T(8,128)S(1)}, u32[]{:S(2)}, u32[]{:S(2)}) collective-permute-start(f32[152,128]{1,0:T(8,128)S(1)} %get-tuple-element.27), channel_id=1, source_target_pairs={{0,1},{1,0},{2,3},{3,2},{4,5},{5,4},{6,7},{7,6},{8,9},{9,8},{10,11... | collective-permute-start | bytes 233480 | tf_op jit(solution)/shard_map/ppermute | solution.py:439
  3.3 5.2 %collective-permute-start.1 = (f32[152,128]{1,0:T(8,128)S(1)}, f32[152,128]{1,0:T(8,128)S(1)}, u32[]{:S(2)}, u32[]{:S(2)}) collective-permute-start(f32[152,128]{1,0:T(8,128)S(1)} %get-tuple-element.28), channel_id=1, source_target_pairs={{1,2},{2,1},{3,4},{4,3},{5,6},{6,5},{7,8},{8,7},{9,10},{10,9},{11,... | collective-permute-start | bytes 233480 | tf_op jit(solution)/shard_map/ppermute | solution.py:439
  4.2 5.9 %collective-permute-start.2 = (f32[16,128]{1,0:T(8,128)S(1)}, f32[16,128]{1,0:T(8,128)S(1)}, u32[]{:S(2)}, u32[]{:S(2)}) collective-permute-start(f32[16,128]{1,0:T(8,128)S(1)} %slice_add_fusion.1.sum_ref), channel_id=1, source_target_pairs={{0,2},{1,3},{2,0},{3,1},{4,6},{5,7},{6,4},{7,5},{8,10},{9,11},{10,... | collective-permute-start | bytes 24584 | tf_op jit(solution)/shard_map/ppermute | solution.py:447
  10.1 3.4 %copy-start = (bf16[2048,2048]{1,0:T(8,128)(2,1)S(1)}, bf16[2048,2048]{1,0:T(8,128)(2,1)}, u32[]{:S(2)}) copy-start(bf16[2048,2048]{1,0:T(8,128)(2,1)} %inv_ref.3) | copy-start | bytes 25165828
  13.5 1.2 %copy-start.2 = (f32[128,1792]{1,0:T(8,128)S(1)}, f32[128,1792]{1,0:T(8,128)}, u32[]{:S(2)}) copy-start(f32[128,1792]{1,0:T(8,128)} %rhs_ref.9) | copy-start | bytes 2752516
  16.0 16.4 %collective-permute-start.5 = (f32[16,128]{1,0:T(8,128)S(1)}, f32[16,128]{1,0:T(8,128)S(1)}, u32[]{:S(2)}, u32[]{:S(2)}) collective-permute-start(f32[16,128]{1,0:T(8,128)S(1)} %get-tuple-element.33.sum_ref), channel_id=1, source_target_pairs={{0,4},{1,5},{2,6},{3,7},{4,0},{5,1},{6,2},{7,3},{8,12},{9,13},{10,... | collective-permute-start | bytes 24584 | tf_op jit(solution)/shard_map/ppermute | solution.py:447
  19.2 13.2 %collective-permute-start.3 = (bf16[128,256]{1,0:T(8,128)(2,1)S(1)}, bf16[128,256]{1,0:T(8,128)(2,1)S(1)}, u32[]{:S(2)}, u32[]{:S(2)}) collective-permute-start(bf16[128,256]{1,0:T(8,128)(2,1)S(1)} %get-tuple-element.31), channel_id=1, source_target_pairs={{0,1},{1,0},{2,3},{3,2},{4,5},{5,4},{6,7},{7,6},{8,9},{9,8},{10,11... | collective-permute-start | bytes 196616 | tf_op jit(solution)/shard_map/ppermute | solution.py:439
  19.2 13.2 %collective-permute-start.4 = (bf16[128,256]{1,0:T(8,128)(2,1)S(1)}, bf16[128,256]{1,0:T(8,128)(2,1)S(1)}, u32[]{:S(2)}, u32[]{:S(2)}) collective-permute-start(bf16[128,256]{1,0:T(8,128)(2,1)S(1)} %get-tuple-element.32), channel_id=1, source_target_pairs={{1,2},{2,1},{3,4},{4,3},{5,6},{6,5},{7,8},{8,7},{9,10},{10,9},{11,... | collective-permute-start | bytes 196616 | tf_op jit(solution)/shard_map/ppermute | solution.py:439
  19.9 27.3 %slice-start = ((s8[8388608]{0:T(1024)(128)(4,1)}), s8[4194304]{0:T(1024)(128)(4,1)S(1)}, s32[]{:S(2)}) async-start(s8[8388608]{0:T(1024)(128)(4,1)} %bitcast.6), calls=%async_computation | async-start | bytes 8388608
  19.9 12.6 %copy-start.5 = (f32[1792]{0:T(1024)S(1)}, f32[1792]{0:T(1024)}, u32[]{:S(2)}) copy-start(f32[1792]{0:T(1024)} %param.14) | copy-start | bytes 21508
  19.9 12.6 %copy-start.7 = (f32[1792]{0:T(1024)S(1)}, f32[1792]{0:T(1024)}, u32[]{:S(2)}) copy-start(f32[1792]{0:T(1024)} %param.9) | copy-start | bytes 21508
  19.9 27.2 %slice-start.1 = ((s8[8388608]{0:T(1024)(128)(4,1)}), s8[4194304]{0:T(1024)(128)(4,1)S(1)}, s32[]{:S(2)}) async-start(s8[8388608]{0:T(1024)(128)(4,1)} %bitcast.6), calls=%async_computation.1 | async-start | bytes 8388608
  32.4 14.8 %copy-start.6 = (f32[16,16]{1,0:T(8,128)S(1)}, f32[16,16]{1,0:T(8,128)}, u32[]{:S(2)}) copy-start(f32[16,16]{1,0:T(8,128)} %cinv_ref.5) | copy-start | bytes 3076
  32.5 17.6 %copy-start.3 = (f32[128,1792]{1,0:T(8,128)S(1)}, f32[128,1792]{1,0:T(8,128)}, u32[]{:S(2)}) copy-start(f32[128,1792]{1,0:T(8,128)} %rhs_ref.9) | copy-start | bytes 2752516
  36.2 10.9 %collective-permute-start.6 = (bf16[144,256]{1,0:T(8,128)(2,1)S(1)}, bf16[144,256]{1,0:T(8,128)(2,1)S(1)}, u32[]{:S(2)}, u32[]{:S(2)}) collective-permute-start(bf16[144,256]{1,0:T(8,128)(2,1)S(1)} %get-tuple-element.36), channel_id=1, source_target_pairs={{0,1},{1,0},{2,3},{3,2},{4,5},{5,4},{6,7},{7,6},{8,9},{9,8},{10,11... | collective-permute-start | bytes 221192 | tf_op jit(solution)/shard_map/ppermute | solution.py:439
  38.6 8.5 %collective-permute-start.7 = (bf16[144,256]{1,0:T(8,128)(2,1)S(1)}, bf16[144,256]{1,0:T(8,128)(2,1)S(1)}, u32[]{:S(2)}, u32[]{:S(2)}) collective-permute-start(bf16[144,256]{1,0:T(8,128)(2,1)S(1)} %get-tuple-element.37), channel_id=1, source_target_pairs={{1,2},{2,1},{3,4},{4,3},{5,6},{6,5},{7,8},{8,7},{9,10},{10,9},{11,... | collective-permute-start | bytes 221192 | tf_op jit(solution)/shard_map/ppermute | solution.py:439
  39.3 7.9 %collective-permute-start.8 = (f32[16,128]{1,0:T(8,128)S(1)}, f32[16,128]{1,0:T(8,128)S(1)}, u32[]{:S(2)}, u32[]{:S(2)}) collective-permute-start(f32[16,128]{1,0:T(8,128)S(1)} %get-tuple-element.38), channel_id=1, source_target_pairs={{0,8},{1,9},{2,10},{3,11},{4,12},{5,13},{6,14},{7,15},{8,0},{9,1},... | collective-permute-start | bytes 24584 | tf_op jit(solution)/shard_map/ppermute | solution.py:447
  49.1 1.7 %collective-permute-start.9 = (bf16[128,256]{1,0:T(8,128)(2,1)S(1)}, bf16[128,256]{1,0:T(8,128)(2,1)S(1)}, u32[]{:S(2)}, u32[]{:S(2)}) collective-permute-start(bf16[128,256]{1,0:T(8,128)(2,1)S(1)} %get-tuple-element.42), channel_id=1, source_target_pairs={{0,1},{1,0},{2,3},{3,2},{4,5},{5,4},{6,7},{7,6},{8,9},{9,8},{10,11... | collective-permute-start | bytes 196616 | tf_op jit(solution)/shard_map/ppermute | solution.py:439
  49.2 1.6 %collective-permute-start.10 = (bf16[128,256]{1,0:T(8,128)(2,1)S(1)}, bf16[128,256]{1,0:T(8,128)(2,1)S(1)}, u32[]{:S(2)}, u32[]{:S(2)}) collective-permute-start(bf16[128,256]{1,0:T(8,128)(2,1)S(1)} %get-tuple-element.43), channel_id=1, source_target_pairs={{1,2},{2,1},{3,4},{4,3},{5,6},{6,5},{7,8},{8,7},{9,10},{10,9},{11,... | collective-permute-start | bytes 196616 | tf_op jit(solution)/shard_map/ppermute | solution.py:439
  54.8 5.5 %collective-permute-start.11 = (f32[184,128]{1,0:T(8,128)S(1)}, f32[184,128]{1,0:T(8,128)S(1)}, u32[]{:S(2)}, u32[]{:S(2)}) collective-permute-start(f32[184,128]{1,0:T(8,128)S(1)} %get-tuple-element.49), channel_id=1, source_target_pairs={{0,1},{1,0},{2,3},{3,2},{4,5},{5,4},{6,7},{7,6},{8,9},{9,8},{10,11... | collective-permute-start | bytes 282632 | tf_op jit(solution)/shard_map/ppermute | solution.py:439
  60.3 3.9 %collective-permute-start.13 = (f32[56,128]{1,0:T(8,128)S(1)}, f32[56,128]{1,0:T(8,128)S(1)}, u32[]{:S(2)}, u32[]{:S(2)}) collective-permute-start(f32[56,128]{1,0:T(8,128)S(1)} %slice_add_fusion), channel_id=1, source_target_pairs={{0,2},{1,3},{2,0},{3,1},{4,6},{5,7},{6,4},{7,5},{8,10},{9,11},{10,... | collective-permute-start | bytes 86024 | tf_op jit(solution)/shard_map/ppermute | solution.py:447
  60.9 12.1 %collective-permute-start.12 = (f32[128,128]{1,0:T(8,128)S(1)}, f32[128,128]{1,0:T(8,128)S(1)}, u32[]{:S(2)}, u32[]{:S(2)}) collective-permute-start(f32[128,128]{1,0:T(8,128)S(1)} %get-tuple-element.50), channel_id=1, source_target_pairs={{1,2},{2,1},{3,4},{4,3},{5,6},{6,5},{7,8},{8,7},{9,10},{10,9},{11,... | collective-permute-start | bytes 196616 | tf_op jit(solution)/shard_map/ppermute | solution.py:439
  64.2 4.0 %collective-permute-start.14 = (f32[56,128]{1,0:T(8,128)S(1)}, f32[56,128]{1,0:T(8,128)S(1)}, u32[]{:S(2)}, u32[]{:S(2)}) collective-permute-start(f32[56,128]{1,0:T(8,128)S(1)} %add.26), channel_id=1, source_target_pairs={{0,4},{1,5},{2,6},{3,7},{4,0},{5,1},{6,2},{7,3},{8,12},{9,13},{10,... | collective-permute-start | bytes 86024 | tf_op jit(solution)/shard_map/ppermute | solution.py:447
  68.2 4.8 %collective-permute-start.15 = (f32[56,128]{1,0:T(8,128)S(1)}, f32[56,128]{1,0:T(8,128)S(1)}, u32[]{:S(2)}, u32[]{:S(2)}) collective-permute-start(f32[56,128]{1,0:T(8,128)S(1)} %add.27), channel_id=1, source_target_pairs={{0,8},{1,9},{2,10},{3,11},{4,12},{5,13},{6,14},{7,15},{8,0},{9,1},... | collective-permute-start | bytes 86024 | tf_op jit(solution)/shard_map/ppermute | solution.py:447

commit v3 on v2

--- a/solution.py
+++ b/solution.py
@@ -123,7 +123,8 @@
     put_sides(even_ref, odd_ref, side(0), side(own - STRIP))
 
 
-def build_kernel(rows_s, rows_v, lane_v, weight_v, o_ref, *scratch):
+def build_kernel(rows_s, rows_v, lane_v, weight_v, o_ref, token, *scratch):
+    token[...] = jnp.zeros(token.shape, F32)
     merged, tables = scratch[0], scratch[1:]
     own, sub = o_ref.shape
     edges = merged.shape[0]
@@ -199,69 +200,115 @@
     )
 
 
-def first_solve_kernel(
-    rhs_ref, even_got, odd_got, inv_ref, sum_ref, sum_got, u_ref, even_ref, odd_ref, sum_out
-):
+def first_solve_kernel(rhs_ref, even_got, odd_got, inv_ref, token, u_ref, even_ref, odd_ref):
     rhs = rhs_ref.shape[0]
     left, right = take_sides(even_got[0:rhs, :], odd_got[0:rhs, :])
     wide = jnp.concatenate([left, rhs_ref[...], right], 1).astype(BF16)
     local_solve(u_ref, wide, inv_ref)
     put_strips(even_ref, odd_ref, u_ref)
-    sum_out[...] = sum_ref[...] + sum_got[...]
-
-
-def product(wide_ref, o_ref, deg, mass, out_ref):
-    rows, sub = wide_ref.shape
+
+
+def blocks_of(sub):
     own = sub - 2 * STRIP
     tall = 256
-    high = wide_ref[...].astype(BF16)
-    mine = high[:, STRIP : STRIP + own]
-    sides = jnp.concatenate([o_ref[:, 0:STRIP], o_ref[:, sub - STRIP :]], 1)
-    thru = lax.dot_general(mine, sides, NN, preferred_element_type=F32)
-    for part, start in ((thru[:, 0:STRIP], 0), (thru[:, STRIP:], sub - STRIP)):
-        cols = slice(start, start + STRIP)
-        out_ref[:, cols] = wide_ref[:, cols] * deg(part, cols) - part
-    for j in range(own // tall):
-        cols = slice(STRIP + j * tall, STRIP + (j + 1) * tall)
-        part = lax.dot_general(mine, o_ref[:, cols], NN, preferred_element_type=F32)
-        part = part + lax.dot_general(
-            high, o_ref[j * tall : (j + 1) * tall, :], NT, preferred_element_type=F32
+    return [None] + [slice(j * tall, (j + 1) * tall) for j in range(own // tall)]
+
+
+def sides_of(ref, rows):
+    sub = ref.shape[1]
+    return jnp.concatenate([ref[rows, 0:STRIP], ref[rows, sub - STRIP :]], 1)
+
+
+def inner_product(inner, o_ref, out_ref):
+    own, sub = o_ref.shape
+    rows = slice(STRIP, own - STRIP)
+    for block in blocks_of(sub):
+        if block is None:
+            thru = lax.dot_general(inner, sides_of(o_ref, rows), NN, preferred_element_type=F32)
+            out_ref[:, 0:STRIP] = thru[:, 0:STRIP]
+            out_ref[:, sub - STRIP :] = thru[:, STRIP:]
+            continue
+        cols = slice(STRIP + block.start, STRIP + block.stop)
+        part = lax.dot_general(inner, o_ref[rows, cols], NN, preferred_element_type=F32)
+        out_ref[:, cols] = part + lax.dot_general(
+            inner, o_ref[block, 2 * STRIP : sub - 2 * STRIP], NT, preferred_element_type=F32
         )
-        diag = deg(part, cols) + mass[:, j * tall : (j + 1) * tall]
-        out_ref[:, cols] = wide_ref[:, cols] * diag - part
-
-
-def first_apply_kernel(
-    n, u_ref, even_got, odd_got, halo_even, halo_odd, o_ref, cvec_ref, mass_ref, sum_ref, sum_got,
-    s_ref, y_ref, deg_ref, even_ref, odd_ref, sum_out, wide_ref,
+
+
+def outer_product(wide_ref, o_ref, thru_ref, deg, mass, out_ref):
+    own, sub = o_ref.shape
+    w = STRIP
+    low, high = wide_ref[:, 0 : 2 * w].astype(BF16), wide_ref[:, sub - 2 * w :].astype(BF16)
+    both = jnp.concatenate([low, high], 1)
+    mine = jnp.concatenate([low[:, w:], high[:, 0:w]], 1)
+
+    def rows(pick):
+        return jnp.concatenate([pick(slice(0, w)), pick(slice(own - w, own))], 0)
+
+    for block in blocks_of(sub):
+        if block is None:
+            part = lax.dot_general(
+                mine, rows(lambda r: sides_of(o_ref, r)), NN, preferred_element_type=F32
+            )
+            for piece, start in ((part[:, 0:w], 0), (part[:, w:], sub - w)):
+                cols = slice(start, start + w)
+                piece = piece + thru_ref[:, cols]
+                out_ref[:, cols] = wide_ref[:, cols] * deg(piece, cols) - piece
+            continue
+        cols = slice(w + block.start, w + block.stop)
+        part = lax.dot_general(
+            mine, rows(lambda r: o_ref[r, cols]), NN, preferred_element_type=F32
+        )
+        ends_of = jnp.concatenate([o_ref[block, 0 : 2 * w], o_ref[block, sub - 2 * w :]], 1)
+        part = part + lax.dot_general(both, ends_of, NT, preferred_element_type=F32)
+        part = part + thru_ref[:, cols]
+        out_ref[:, cols] = wide_ref[:, cols] * (deg(part, cols) + mass[:, block]) - part
+
+
+def fixed_rows(cvec, start, stop, sub):
+    own = sub - 2 * STRIP
+    lane = start + iota((1, stop - start), 1)
+    return jnp.concatenate(
+        [
+            jnp.where(lane < STRIP, cvec, 0.0),
+            jnp.where((lane >= STRIP) & (lane < STRIP + own), cvec, 0.0),
+            jnp.where(lane >= STRIP + own, cvec, 0.0),
+            jnp.ones(cvec.shape, F32),
+            jnp.zeros((EXTRA - 4, stop - start), F32),
+        ],
+        0,
+    )
+
+
+def first_inner_kernel(u_ref, o_ref, cvec_ref, sum_ref, sum_got, thru_ref, sum_out):
+    rhs, sub = u_ref.shape
+    inner = slice(2 * STRIP, sub - 2 * STRIP)
+    cvec = flat(cvec_ref)[:, STRIP : sub - 3 * STRIP]
+    fixed = fixed_rows(cvec, inner.start, inner.stop, sub)
+    value = jnp.concatenate([u_ref[:, inner], fixed], 0).astype(BF16)
+    inner_product(value, o_ref, thru_ref)
+    sum_out[...] = sum_ref[...] + sum_got[...]
+
+
+def first_outer_kernel(
+    n, u_ref, even_got, odd_got, halo_even, halo_odd, o_ref, thru_ref, cvec_ref, mass_ref,
+    s_ref, y_ref, deg_ref, even_ref, odd_ref, wide_ref,
 ):
     rhs, sub = u_ref.shape
-    own = sub - 2 * STRIP
     left, right = take_sides(even_got[...], odd_got[...])
     vec_left, vec_right = take_sides(halo_even[rhs : rhs + 1, :], halo_odd[rhs : rhs + 1, :])
     wide_ref[0:rhs, :] = widen(u_ref, left, right, n)
     cvec = jnp.concatenate([vec_left, flat(cvec_ref), vec_right], 1)
-    lane = iota((1, sub), 1)
-    wide_ref[rhs:, :] = jnp.concatenate(
-        [
-            jnp.where(lane < STRIP, cvec, 0.0),
-            jnp.where((lane >= STRIP) & (lane < STRIP + own), cvec, 0.0),
-            jnp.where(lane >= STRIP + own, cvec, 0.0),
-            jnp.ones((1, sub), F32),
-            jnp.zeros((EXTRA - 4, sub), F32),
-        ],
-        0,
-    )
+    wide_ref[rhs:, :] = fixed_rows(cvec, 0, sub, sub)
 
     def degree(part, cols):
         row = part[rhs + 3 : rhs + 4, :]
         deg_ref[:, cols] = jnp.broadcast_to(row, (8, row.shape[1]))
         return row
 
-    product(wide_ref, o_ref, degree, flat(mass_ref), y_ref)
+    outer_product(wide_ref, o_ref, thru_ref, degree, flat(mass_ref), y_ref)
     s_ref[...] = wide_ref[0:rhs, STRIP : sub - STRIP]
     put_strips(even_ref, odd_ref, y_ref)
-    sum_out[...] = sum_ref[...] + sum_got[...]
 
 
 def add_coarse(value, vectors, coarse, first):
@@ -271,19 +318,44 @@
     return value
 
 
-def next_solve_kernel(
-    n, y_ref, even_got, odd_got, sums_ref, cinv_ref, inv_ref, own_ref, u_ref, even_ref, odd_ref
+def solve_inner_kernel(n, y_ref, sums_ref, cinv_ref, inv_ref, own_ref, u_ref):
+    rhs, sub = u_ref.shape
+    inner = slice(2 * STRIP, sub - 2 * STRIP)
+    coarse = coarse_columns(n, sums_ref[0:n, :], cinv_ref, 2)
+    value = add_coarse(y_ref[0:rhs, inner], y_ref[rhs : rhs + 3, inner], coarse, 1)
+    own_ref[...] = value
+    high = value.astype(BF16)
+    tall = 256
+    for j in range(sub // tall):
+        cols = slice(j * tall, (j + 1) * tall)
+        u_ref[:, cols] = jnp.dot(high, inv_ref[inner, cols], preferred_element_type=F32)
+
+
+def solve_outer_kernel(
+    n, y_ref, even_got, odd_got, sums_ref, cinv_ref, inv_ref, inner_ref, half_ref,
+    own_ref, u_ref, even_ref, odd_ref,
 ):
-    rhs = u_ref.shape[0]
-    sub = u_ref.shape[1]
+    rhs, sub = u_ref.shape
+    w = STRIP
+    first, last = ends(n)
     coarse = coarse_columns(n, sums_ref[0:n, :], cinv_ref, 2)
     left, right = take_sides(even_got[...], odd_got[...])
     left = add_coarse(left[0:rhs], left[rhs : rhs + 3], coarse, 0)
     right = add_coarse(right[0:rhs], right[rhs : rhs + 3], coarse, 2)
-    value = add_coarse(y_ref[0:rhs, :], y_ref[rhs : rhs + 3, :], coarse, 1)
-    wide = widen(value, left, right, n)
-    own_ref[...] = wide[:, STRIP : sub - STRIP]
-    local_solve(u_ref, wide.astype(BF16), inv_ref)
+    low, high = slice(0, 2 * w), slice(sub - 2 * w, sub)
+    left = left + add_coarse(y_ref[0:rhs, low], y_ref[rhs : rhs + 3, low], coarse, 1)
+    right = right + add_coarse(y_ref[0:rhs, high], y_ref[rhs : rhs + 3, high], coarse, 1)
+    own_ref[:, 0:w] = left[:, w:]
+    own_ref[:, w : sub - 3 * w] = inner_ref[...]
+    own_ref[:, sub - 3 * w :] = right[:, 0:w]
+    both = jnp.concatenate(
+        [left[:, 0:w] * first, left[:, w:], right[:, 0:w], right[:, w:] * last], 1
+    ).astype(BF16)
+    tall = 256
+    for j in range(sub // tall):
+        cols = slice(j * tall, (j + 1) * tall)
+        part = jnp.concatenate([inv_ref[low, cols], inv_ref[high, cols]], 0)
+        u_ref[:, cols] = half_ref[:, cols] + jnp.dot(both, part, preferred_element_type=F32)
     put_strips(even_ref, odd_ref, u_ref)
 
 
@@ -331,28 +403,53 @@
     part_ref[2 * slots :, :] = rows_of([(0, a), (1, b)], 8)
 
 
-def next_apply_kernel(
-    n, u_ref, even_got, odd_got, o_ref, deg_ref, mass_ref, rhs_ref, y_ref, g_ref, part_in,
-    w_ref, q_ref, even_ref, odd_ref, part_ref, wide_ref, out_ref,
+def next_inner_kernel(u_ref, o_ref, rhs_ref, y_ref, g_ref, thru_ref, dots_ref):
+    rhs, sub = u_ref.shape
+    own = sub - 2 * STRIP
+    value = u_ref[:, 2 * STRIP : sub - 2 * STRIP]
+    inner_product(value.astype(BF16), o_ref, thru_ref)
+    inner = slice(STRIP, own - STRIP)
+    columns = [rowsum(value * rhs_ref[:, inner]), rowsum(value * y_ref[:, inner])]
+    columns += [rowsum(value * g_ref[k : k + 1, inner]) for k in range(3)]
+    lane = iota((rhs, LANES), 1)
+    total = jnp.zeros((rhs, LANES), F32)
+    for k, column in enumerate(columns):
+        total = total + jnp.where(lane == k, jnp.broadcast_to(column, (rhs, LANES)), 0.0)
+    dots_ref[...] = total
+
+
+def next_outer_kernel(
+    n, u_ref, even_got, odd_got, o_ref, thru_ref, dots_ref, deg_ref, mass_ref, rhs_ref, y_ref,
+    g_ref, part_in, w_ref, q_ref, even_ref, odd_ref, part_ref, wide_ref, out_ref,
 ):
-    me, _ = place()
+    me, even = place()
     rhs, sub = u_ref.shape
     own = sub - 2 * STRIP
     slots = up(n, 8)
     left, right = take_sides(even_got[...], odd_got[...])
     wide_ref[...] = widen(u_ref, left, right, n)
-    product(wide_ref, o_ref, lambda part, cols: deg_ref[0:1, cols], flat(mass_ref), out_ref)
-    w = wide_ref[:, STRIP : sub - STRIP]
-    w_ref[...] = w
+    outer_product(
+        wide_ref, o_ref, thru_ref, lambda part, cols: deg_ref[0:1, cols], flat(mass_ref), out_ref
+    )
+    w_ref[...] = wide_ref[:, STRIP : sub - STRIP]
     q_ref[...] = out_ref[:, STRIP : sub - STRIP]
-    c = rowsum(rhs_ref[...] * w)
-    d = rowsum(y_ref[...] * w)
     e = rowsum(wide_ref[...] * out_ref[...])
-    cross = [(me - 1 + k, rowsum(w * g_ref[k : k + 1, :])) for k in range(3)]
+
+    def edges_of(ref):
+        return jnp.concatenate([ref[:, 0:STRIP], ref[:, own - STRIP :]], 1)
+
+    w = jnp.concatenate(
+        [wide_ref[:, STRIP : 2 * STRIP], wide_ref[:, sub - 2 * STRIP : sub - STRIP]], 1
+    )
+    g = edges_of(g_ref)
+    c = dots_ref[:, 0:1] + rowsum(w * edges_of(rhs_ref))
+    d = dots_ref[:, 1:2] + rowsum(w * edges_of(y_ref))
+    cross = [
+        (me - 1 + k, dots_ref[:, 2 + k : 3 + k] + rowsum(w * g[k : k + 1, :])) for k in range(3)
+    ]
     part_ref[0 : 2 * slots, :] = part_in[0 : 2 * slots, :]
     part_ref[2 * slots : 3 * slots, :] = rows_of(cross, slots)
     part_ref[3 * slots :, :] = part_in[2 * slots :, :] + rows_of([(2, c), (3, d), (4, e)], 8)
-    _, even = place()
 
     @pl.when(even)
     def _():
@@ -477,39 +574,58 @@
 
     at = (edge_tails >> 7) * own + (edge_heads - STRIP)
     shape = (edges // LANES, LANES)
-    (stiff,) = call(
+    stiff, token = call(
         build_kernel,
         "build",
-        [((own, sub), BF16)],
+        [((own, sub), BF16), ((8, LANES), F32)],
         [pltpu.VMEM((edges, LANES), F32)] + [pltpu.VMEM((sub // LANES * own, LANES), F32)] * 2,
         34,
         4,
         in_specs=[smem, vmem, vmem, vmem],
         flops=10**10,
     )(at, at.reshape(shape), (edge_tails & 127).reshape(shape), edge_weight.reshape(shape))
+    part = part + across(part, 2)
 
     whole, owned = ((rows, sub), F32), ((rows, own), F32)
     strip = ((rows, 2 * STRIP), BF16)
     extra = ((rows + EXTRA, sub), F32)
-    u, even, odd, part = call(
-        first_solve_kernel, "solve", [whole, strip, strip, few], [], 12, 6, flops=10**9
-    )(rhs, *halo, local_inverse, part, across(part, 2))
+    u, even, odd = call(
+        first_solve_kernel, "solve", [whole, strip, strip], [], 12, 5, flops=10**9
+    )(rhs, *halo, local_inverse, token)
     got = swap((even, odd))
+    thru, part = call(first_inner_kernel, "inner", [extra, few], [], 8, 5, flops=2 * 10**9)(
+        u, stiff, cvec, part, across(part, 4)
+    )
+    sums = finish_sum(part, 8)
     strips = ((rows + EXTRA, 2 * STRIP), BF16)
-    s, y_part, degree, even, odd, part = call(
-        bind(first_apply_kernel, n),
-        "apply",
-        [owned, extra, ((8, sub), F32), strips, strips, few],
+    s, y_part, degree, even, odd = call(
+        bind(first_outer_kernel, n),
+        "outer",
+        [owned, extra, ((8, sub), F32), strips, strips],
         [pltpu.VMEM(*extra)],
         12,
-        10,
-        flops=2 * 10**9,
-    )(u, *got, *halo, stiff, cvec, mass, part, across(part, 4))
+        9,
+        flops=10**9,
+    )(u, *got, *halo, stiff, thru, cvec, mass)
     got_y = swap((even, odd))
-    sums = finish_sum(part, 8)
+    inner, half = call(
+        bind(solve_inner_kernel, n),
+        "solve_inner",
+        [((rows, own - 2 * STRIP), F32), whole],
+        [],
+        8,
+        4,
+        flops=10**9,
+    )(y_part, sums, coarse_inv, local_inverse)
     y, u, even, odd = call(
-        bind(next_solve_kernel, n), "solve2", [owned, whole, strip, strip], [], 12, 6, flops=10**9
-    )(y_part, *got_y, sums, coarse_inv, local_inverse)
+        bind(solve_outer_kernel, n),
+        "solve_outer",
+        [owned, whole, strip, strip],
+        [],
+        12,
+        8,
+        flops=10**8,
+    )(y_part, *got_y, sums, coarse_inv, local_inverse, inner, half)
     got = swap((even, odd))
     z, g, part = call(
         bind(between_kernel, n),
@@ -520,16 +636,19 @@
         9,
         flops=10**9,
     )(s, y, y_part, *got_y, sums, coarse_inv, cvec, rhs)
+    thru, dots = call(
+        next_inner_kernel, "inner2", [whole, ((rows, LANES), F32)], [], 8, 5, flops=2 * 10**9
+    )(u, stiff, rhs, y, g)
     many = 3 * slots + 8
     w, q, even, odd, part = call(
-        bind(next_apply_kernel, n),
-        "apply2",
+        bind(next_outer_kernel, n),
+        "outer2",
         [owned, owned, ((rows + many, STRIP), F32), ((rows, STRIP), F32), ((many, rows), F32)],
         [pltpu.VMEM(*whole), pltpu.VMEM(*whole)],
         12,
-        10,
-        flops=2 * 10**9,
-    )(u, *got, stiff, degree, mass, rhs, y, g, part)
+        12,
+        flops=10**9,
+    )(u, *got, stiff, thru, dots, degree, mass, rhs, y, g, part)
     got = swap((even, odd))
     part = finish_sum(part + got[0][rows:], 2)
     return tuple(

time: 75.9 us -> 70.8 us (0.933)
  local copies, waits for them, and re-layouts: 6.47 us -> 2.65 us
  waiting for transfers between devices: 11.7 us -> 8.57 us
  Pallas kernels: 26.9 us -> 28.2 us
    unnamed x22 -> x18, local copies, waits for them, and re-layouts: 6.47 us -> 2.65 us
    ppermute x6, waiting for transfers between devices: 10.5 us -> 7.61 us  [across(): return lax.ppermute(part, 'tile', [(i, i ^ hop) for i in range(n)])]
    ppermute x10, starting transfers between devices: 11 us -> 13.8 us  [swap(): got.append(lax.ppermute(payload, 'tile', links))]
    ppermute x6, starting transfers between devices: 17.7 us -> 15.6 us  [across(): return lax.ppermute(part, 'tile', [(i, i ^ hop) for i in range(n)])]
    pallas_call x5 -> x8, Pallas kernels: 23.6 us -> 24.9 us  [the longest x1 12.5 us: shards(): call(build_kernel, 'build', [((own, sub), BF16), ((8, LANES), F32)], [plt...]
  transfers between devices with their start and end apart: 16 -> 16, of which waited for: 7 -> 5; matrix products, arithmetic and copies ran while one was open for 1% -> 1% of each run, Pallas kernels for 18% -> 31%
where the time goes in v3:
time: 70.8 us; the launch traced here: 70.4 us
  starting transfers between devices  29.3 us (41%)
  Pallas kernels  28.2 us (40%)
  waiting for transfers between devices  8.57 us (12%)
  local copies, waits for them, and re-layouts  2.65 us (4%)
  between operations  0.89 us (1%)
  other arithmetic  0.81 us (1%)
    ppermute x6, starting transfers between devices, across(): return lax.ppermute(part, 'tile', [(i, i ^ hop) for i in range(n)])  15.6 us
    ppermute x10, starting transfers between devices, swap(): got.append(lax.ppermute(payload, 'tile', links))  13.8 us
    pallas_call x1, Pallas kernels, shards(): call(build_kernel, 'build', [((own, sub), BF16), ((8, LANES), F32)], [plt...  12.5 us
    ppermute x6, waiting for transfers between devices, across(): return lax.ppermute(part, 'tile', [(i, i ^ hop) for i in range(n)])  7.61 us
    pallas_call x1, Pallas kernels, shards(): call(next_inner_kernel, 'inner2', [whole, ((rows, LANES), F32)], [], 8, 5...  3.12 us
    pallas_call x1, Pallas kernels, shards(): call(first_inner_kernel, 'inner', [extra, few], [], 8, 5, flops=2 * 10 ** 9)  2.88 us
    unnamed x18, local copies, waits for them, and re-layouts  2.65 us
    pallas_call x1, Pallas kernels, shards(): call(bind(finish_kernel, n), 'finish', [owned, owned], [], 16, 12)  2.4 us
  transfers between devices with their start and end apart: 16, of which 5 were waited for; matrix products, arithmetic and copies ran while one was open for 1% of the time, Pallas kernels for 31%

profile of v3, /device:TPU:0, one launch (start us, length us, event | category | flops | bytes accessed | tf_op | source)
XLA Modules:
  0.0 70.4 jit_solution(10622075057932710027)
XLA Ops:
  0.6 1.2 %copy-done = f32[128,1792]{1,0:T(8,128)S(1)} copy-done((f32[128,1792]{1,0:T(8,128)S(1)}, f32[128,1792]{1,0:T(8,128)}, u32[]{:S(2)}) %copy-start) | copy-done | bytes 917528
  1.8 0.7 copy-done.2
  3.3 0.8 %collective-permute-start.1 = (f32[152,128]{1,0:T(8,128)S(1)}, f32[152,128]{1,0:T(8,128)S(1)}, u32[]{:S(2)}, u32[]{:S(2)}) collective-permute-start(f32[152,128]{1,0:T(8,128)S(1)} %get-tuple-element.34), channel_id=1, source_target_pairs={{1,2},{2,1},{3,4},{4,3},{5,6},{6,5},{7,8},{8,7},{9,10},{10,9},{11,... | collective-permute-start | bytes 233480 | tf_op jit(solution)/shard_map/ppermute | solution.py:536
  4.1 0.8 %and_bitcast_fusion = (s32[56,128]{1,0:T(8,128)S(1)}, s32[7168]{0:T(1024)S(1)}) fusion(s32[7168]{0:T(1024)} %param.11, s32[7168]{0:T(1024)} %param.10), kind=kLoop, calls=%fused_computation.1 | loop fusion | flops 35840 | bytes 114688 | tf_op jit(solution)/shard_map/reshape | solution.py:586
  4.9 3.9 %collective-permute-start.4 = (f32[16,128]{1,0:T(8,128)S(1)}, f32[16,128]{1,0:T(8,128)S(1)}, u32[]{:S(2)}, u32[]{:S(2)}) collective-permute-start(f32[16,128]{1,0:T(8,128)S(1)} %slice_add_fusion.1), channel_id=1, source_target_pairs={{0,2},{1,3},{2,0},{3,1},{4,6},{5,7},{6,4},{7,5},{8,10},{9,11},{10,... | collective-permute-start | bytes 24584 | tf_op jit(solution)/shard_map/ppermute | solution.py:544
  8.8 0.7 %copy-done.6 = f32[7168]{0:T(1024)S(1)} copy-done((f32[7168]{0:T(1024)S(1)}, f32[7168]{0:T(1024)}, u32[]{:S(2)}) %copy-start.6) | copy-done | bytes 28696
  9.5 12.5 %build.1 = (bf16[1792,2048]{1,0:T(8,128)(2,1)S(1)}, f32[8,128]{1,0:T(8,128)S(1)}) custom-call(s32[7168]{0:T(1024)S(1)} %get-tuple-element.65.rows_s, s32[56,128]{1,0:T(8,128)S(1)} %bitcast.15, s32[56,128]{1,0:T(8,128)S(1)} %get-tuple-element.64.lane_v, f32[56,128]{1,0:T(8,128)S(1)} %bitcast.16), custom_call_target="tpu_custom_call" | custom-call | flops 10000000000 | tf_op jit(solution)/shard_map/build/pallas_call | solution.py:577
  22.0 2.1 %collective-permute-start.5 = (f32[16,128]{1,0:T(8,128)S(1)}, f32[16,128]{1,0:T(8,128)S(1)}, u32[]{:S(2)}, u32[]{:S(2)}) collective-permute-start(f32[16,128]{1,0:T(8,128)S(1)} %add.27.sum_ref), channel_id=1, source_target_pairs={{0,4},{1,5},{2,6},{3,7},{4,0},{5,1},{6,2},{7,3},{8,12},{9,13},{10,... | collective-permute-start | bytes 24584 | tf_op jit(solution)/shard_map/ppermute | solution.py:544
  24.2 1.3 %solve.1 = (f32[128,2048]{1,0:T(8,128)S(1)}, bf16[128,256]{1,0:T(8,128)(2,1)S(1)}, bf16[128,256]{1,0:T(8,128)(2,1)S(1)}) custom-call(f32[128,1792]{1,0:T(8,128)S(1)} %copy-done.1, f32[152,128]{1,0:T(8,128)S(1)} %collective-permute-done.even_got.halo_even, f32[152,128]{1,0:T(8,128)S(1)} %collective-permute-done.1.odd_got.halo_odd, ...), custom_call_target="tpu_custom_call" | custom-call | flops 1000000000 | tf_op jit(solution)/shard_map/solve/pallas_call | solution.py:592
  25.5 0.7 collective-permute-start.2
  26.9 2.9 %inner.1 = (f32[144,2048]{1,0:T(8,128)S(1)}, f32[16,128]{1,0:T(8,128)S(1)}) custom-call(f32[128,2048]{1,0:T(8,128)S(1)} %get-tuple-element.36.u_ref, bf16[1792,2048]{1,0:T(8,128)(2,1)S(1)} %get-tuple-element.39.o_ref, f32[14,128]{1,0:T(8,128)S(1)} %bitcast.9, f32[16,128]{1,0:T(8,128)S(1)} %add.27.sum_ref, f32[16,128]{1,0:T(8,128)S(1)} %collective-permute-done.5.sum_got), custom_call_target="tpu_custom_call" | custom-call | flops 2000000000 | tf_op jit(solution)/shard_map/inner/pallas_call | solution.py:596
  29.8 3.3 %collective-permute-start.8 = (f32[16,128]{1,0:T(8,128)S(1)}, f32[16,128]{1,0:T(8,128)S(1)}, u32[]{:S(2)}, u32[]{:S(2)}) collective-permute-start(f32[16,128]{1,0:T(8,128)S(1)} %get-tuple-element.46), channel_id=1, source_target_pairs={{0,8},{1,9},{2,10},{3,11},{4,12},{5,13},{6,14},{7,15},{8,0},{9,1},... | collective-permute-start | bytes 24584 | tf_op jit(solution)/shard_map/ppermute | solution.py:544
  33.1 1.6 %collective-permute-done.8 = f32[16,128]{1,0:T(8,128)S(1)} collective-permute-done((f32[16,128]{1,0:T(8,128)S(1)}, f32[16,128]{1,0:T(8,128)S(1)}, u32[]{:S(2)}, u32[]{:S(2)}) %collective-permute-start.8) | collective-permute-done | bytes 8224 | tf_op jit(solution)/shard_map/ppermute | solution.py:544
  34.8 1.2 %outer.1 = (f32[128,1792]{1,0:T(8,128)S(1)}, f32[144,2048]{1,0:T(8,128)S(1)}, f32[8,2048]{1,0:T(8,128)S(1)}, bf16[144,256]{1,0:T(8,128)(2,1)S(1)}, bf16[144,256]{1,0:T(8,128)(2,1)S(1)}) custom-call(f32[128,2048]{1,0:T(8,128)S(1)} %get-tuple-element.36.u_ref, bf16[128,256]{1,0:T(8,128)(2,1)S(1)} %collective-permute-done.2.even_got, ...), custom_call_target="tpu_custom_call" | custom-call | flops 1000000000 | tf_op jit(solution)/shard_map/outer/pallas_call | solution.py:601
  36.0 0.7 %collective-permute-start.6 = (bf16[144,256]{1,0:T(8,128)(2,1)S(1)}, bf16[144,256]{1,0:T(8,128)(2,1)S(1)}, u32[]{:S(2)}, u32[]{:S(2)}) collective-permute-start(bf16[144,256]{1,0:T(8,128)(2,1)S(1)} %get-tuple-element.44), channel_id=1, source_target_pairs={{0,1},{1,0},{2,3},{3,2},{4,5},{5,4},{6,7},{7,6},{8,9},{9,8},{10,11... | collective-permute-start | bytes 221192 | tf_op jit(solution)/shard_map/ppermute | solution.py:536
  36.7 0.7 collective-permute-start.7
  37.4 1.6 %solve_inner.1 = (f32[128,1536]{1,0:T(8,128)S(1)}, f32[128,2048]{1,0:T(8,128)S(1)}) custom-call(f32[144,2048]{1,0:T(8,128)S(1)} %get-tuple-element.43.y_ref.coarse_rows, f32[16,128]{1,0:T(8,128)S(1)} %add.28.sums_ref.first_ref, f32[16,16]{1,0:T(8,128)S(1)} %copy-done.4, bf16[2048,2048]{1,0:T(8,128)(2,1)S(1)} %bitcast.7), custom_call_target="tpu_custom_call" | custom-call | flops 1000000000 | tf_op jit(solution)/shard_map/solve_inner/pallas_call | solution.py:611
  39.0 1.1 %solve_outer.1 = (f32[128,1792]{1,0:T(8,128)S(1)}, f32[128,2048]{1,0:T(8,128)S(1)}, bf16[128,256]{1,0:T(8,128)(2,1)S(1)}, bf16[128,256]{1,0:T(8,128)(2,1)S(1)}) custom-call(f32[144,2048]{1,0:T(8,128)S(1)} %get-tuple-element.43.y_ref.coarse_rows, bf16[144,256]{1,0:T(8,128)(2,1)S(1)} %collective-permute-done.6.even_got, ...), custom_call_target="tpu_custom_call" | custom-call | flops 100000000 | tf_op jit(solution)/shard_map/solve_outer/pallas_call | solution.py:620
  40.0 3.8 %collective-permute-start.9 = (bf16[128,256]{1,0:T(8,128)(2,1)S(1)}, bf16[128,256]{1,0:T(8,128)(2,1)S(1)}, u32[]{:S(2)}, u32[]{:S(2)}) collective-permute-start(bf16[128,256]{1,0:T(8,128)(2,1)S(1)} %get-tuple-element.52), channel_id=1, source_target_pairs={{0,1},{1,0},{2,3},{3,2},{4,5},{5,4},{6,7},{7,6},{8,9},{9,8},{10,11... | collective-permute-start | bytes 196616 | tf_op jit(solution)/shard_map/ppermute | solution.py:536
  43.8 0.8 %collective-permute-start.10 = (bf16[128,256]{1,0:T(8,128)(2,1)S(1)}, bf16[128,256]{1,0:T(8,128)(2,1)S(1)}, u32[]{:S(2)}, u32[]{:S(2)}) collective-permute-start(bf16[128,256]{1,0:T(8,128)(2,1)S(1)} %get-tuple-element.53), channel_id=1, source_target_pairs={{1,2},{2,1},{3,4},{4,3},{5,6},{6,5},{7,8},{8,7},{9,10},{10,9},{11,... | collective-permute-start | bytes 196616 | tf_op jit(solution)/shard_map/ppermute | solution.py:536
  44.6 0.7 %between.1 = (f32[128,1792]{1,0:T(8,128)S(1)}, f32[8,1792]{1,0:T(8,128)S(1)}, f32[40,128]{1,0:T(8,128)S(1)}) custom-call(f32[128,1792]{1,0:T(8,128)S(1)} %get-tuple-element.42.s_ref, f32[128,1792]{1,0:T(8,128)S(1)} %get-tuple-element.49.y_ref, f32[144,2048]{1,0:T(8,128)S(1)} %get-tuple-element.43.y_ref.coarse_rows, ...), custom_call_target="tpu_custom_call" | custom-call | flops 1000000000 | tf_op jit(solution)/shard_map/between/pallas_call | solution.py:630
  45.3 3.1 %inner2.1 = (f32[128,2048]{1,0:T(8,128)S(1)}, f32[128,128]{1,0:T(8,128)S(1)}) custom-call(f32[128,2048]{1,0:T(8,128)S(1)} %get-tuple-element.51.u_ref, bf16[1792,2048]{1,0:T(8,128)(2,1)S(1)} %get-tuple-element.39.o_ref, f32[128,1792]{1,0:T(8,128)S(1)} %copy-done.1, f32[128,1792]{1,0:T(8,128)S(1)} %get-tuple-element.49.y_ref, ...), custom_call_target="tpu_custom_call" | custom-call | flops 2000000000 | tf_op jit(solution)/shard_map/inner2/pallas_call | solution.py:639
  48.5 1.2 %outer2.1 = (f32[128,1792]{1,0:T(8,128)S(1)}, f32[128,1792]{1,0:T(8,128)S(1)}, f32[184,128]{1,0:T(8,128)S(1)}, f32[128,128]{1,0:T(8,128)S(1)}, f32[56,128]{1,0:T(8,128)S(1)}) custom-call(f32[128,2048]{1,0:T(8,128)S(1)} %get-tuple-element.51.u_ref, bf16[128,256]{1,0:T(8,128)(2,1)S(1)} %collective-permute-done.9.even_got, ...), custom_call_target="tpu_custom_call" | custom-call | flops 1000000000 | tf_op jit(solution)/shard_map/outer2/pallas_call | solution.py:643
  49.7 4.4 %collective-permute-start.11 = (f32[184,128]{1,0:T(8,128)S(1)}, f32[184,128]{1,0:T(8,128)S(1)}, u32[]{:S(2)}, u32[]{:S(2)}) collective-permute-start(f32[184,128]{1,0:T(8,128)S(1)} %get-tuple-element.61), channel_id=1, source_target_pairs={{0,1},{1,0},{2,3},{3,2},{4,5},{5,4},{6,7},{7,6},{8,9},{9,8},{10,11... | collective-permute-start | bytes 282632 | tf_op jit(solution)/shard_map/ppermute | solution.py:536
  54.2 0.9 %collective-permute-done.11.even_got = f32[184,128]{1,0:T(8,128)S(1)} collective-permute-done((f32[184,128]{1,0:T(8,128)S(1)}, f32[184,128]{1,0:T(8,128)S(1)}, u32[]{:S(2)}, u32[]{:S(2)}) %collective-permute-start.11) | collective-permute-done | bytes 94240 | tf_op jit(solution)/shard_map/ppermute | solution.py:536
  55.1 2.0 %collective-permute-start.13 = (f32[56,128]{1,0:T(8,128)S(1)}, f32[56,128]{1,0:T(8,128)S(1)}, u32[]{:S(2)}, u32[]{:S(2)}) collective-permute-start(f32[56,128]{1,0:T(8,128)S(1)} %slice_add_fusion), channel_id=1, source_target_pairs={{0,2},{1,3},{2,0},{3,1},{4,6},{5,7},{6,4},{7,5},{8,10},{9,11},{10,... | collective-permute-start | bytes 86024 | tf_op jit(solution)/shard_map/ppermute | solution.py:544
  57.8 1.2 %collective-permute-done.13 = f32[56,128]{1,0:T(8,128)S(1)} collective-permute-done((f32[56,128]{1,0:T(8,128)S(1)}, f32[56,128]{1,0:T(8,128)S(1)}, u32[]{:S(2)}, u32[]{:S(2)}) %collective-permute-start.13) | collective-permute-done | bytes 28704 | tf_op jit(solution)/shard_map/ppermute | solution.py:544
  59.0 1.6 %collective-permute-start.14 = (f32[56,128]{1,0:T(8,128)S(1)}, f32[56,128]{1,0:T(8,128)S(1)}, u32[]{:S(2)}, u32[]{:S(2)}) collective-permute-start(f32[56,128]{1,0:T(8,128)S(1)} %add.30), channel_id=1, source_target_pairs={{0,4},{1,5},{2,6},{3,7},{4,0},{5,1},{6,2},{7,3},{8,12},{9,13},{10,... | collective-permute-start | bytes 86024 | tf_op jit(solution)/shard_map/ppermute | solution.py:544
  60.6 2.6 %collective-permute-done.14 = f32[56,128]{1,0:T(8,128)S(1)} collective-permute-done((f32[56,128]{1,0:T(8,128)S(1)}, f32[56,128]{1,0:T(8,128)S(1)}, u32[]{:S(2)}, u32[]{:S(2)}) %collective-permute-start.14) | collective-permute-done | bytes 28704 | tf_op jit(solution)/shard_map/ppermute | solution.py:544
  63.2 2.6 %collective-permute-start.15 = (f32[56,128]{1,0:T(8,128)S(1)}, f32[56,128]{1,0:T(8,128)S(1)}, u32[]{:S(2)}, u32[]{:S(2)}) collective-permute-start(f32[56,128]{1,0:T(8,128)S(1)} %add.31), channel_id=1, source_target_pairs={{0,8},{1,9},{2,10},{3,11},{4,12},{5,13},{6,14},{7,15},{8,0},{9,1},... | collective-permute-start | bytes 86024 | tf_op jit(solution)/shard_map/ppermute | solution.py:544
  65.8 2.2 %collective-permute-done.15 = f32[56,128]{1,0:T(8,128)S(1)} collective-permute-done((f32[56,128]{1,0:T(8,128)S(1)}, f32[56,128]{1,0:T(8,128)S(1)}, u32[]{:S(2)}, u32[]{:S(2)}) %collective-permute-start.15) | collective-permute-done | bytes 28704 | tf_op jit(solution)/shard_map/ppermute | solution.py:544
  68.0 2.4 %finish.1 = (f32[128,1792]{1,0:T(8,128)}, f32[128,1792]{1,0:T(8,128)}) custom-call(f32[128,1792]{1,0:T(8,128)S(1)} %copy-done.1, f32[128,1792]{1,0:T(8,128)S(1)} %get-tuple-element.50.z_ref, f32[128,1792]{1,0:T(8,128)S(1)} %get-tuple-element.49.y_ref, f32[128,1792]{1,0:T(8,128)S(1)} %get-tuple-element.59.w_ref, f32[128,1792]{1,0:T(8,128)S(1)} %get-tuple-element.60.q_ref, ...), custom_call_target="tpu_custom_call" | custom-call | tf_op jit(solution)/shard_map/finish/pallas_call | solution.py:655
  (38 shorter events, 2.2 us)
Async XLA Ops:
  0.6 1.2 %copy-start = (f32[128,1792]{1,0:T(8,128)S(1)}, f32[128,1792]{1,0:T(8,128)}, u32[]{:S(2)}) copy-start(f32[128,1792]{1,0:T(8,128)} %rhs_ref.11) | copy-start | bytes 2752516
  1.8 0.7 copy-start.2
  2.5 21.6 %slice-start = ((s8[8388608]{0:T(1024)(128)(4,1)}), s8[4194304]{0:T(1024)(128)(4,1)S(1)}, s32[]{:S(2)}) async-start(s8[8388608]{0:T(1024)(128)(4,1)} %bitcast.6), calls=%async_computation | async-start | bytes 8388608
  2.7 2.1 %collective-permute-start = (f32[152,128]{1,0:T(8,128)S(1)}, f32[152,128]{1,0:T(8,128)S(1)}, u32[]{:S(2)}, u32[]{:S(2)}) collective-permute-start(f32[152,128]{1,0:T(8,128)S(1)} %get-tuple-element.33), channel_id=1, source_target_pairs={{0,1},{1,0},{2,3},{3,2},{4,5},{5,4},{6,7},{7,6},{8,9},{9,8},{10,11... | collective-permute-start | bytes 233480 | tf_op jit(solution)/shard_map/ppermute | solution.py:536
  3.3 20.9 %collective-permute-start.1 = (f32[152,128]{1,0:T(8,128)S(1)}, f32[152,128]{1,0:T(8,128)S(1)}, u32[]{:S(2)}, u32[]{:S(2)}) collective-permute-start(f32[152,128]{1,0:T(8,128)S(1)} %get-tuple-element.34), channel_id=1, source_target_pairs={{1,2},{2,1},{3,4},{4,3},{5,6},{6,5},{7,8},{8,7},{9,10},{10,9},{11,... | collective-permute-start | bytes 233480 | tf_op jit(solution)/shard_map/ppermute | solution.py:536
  4.9 17.2 %collective-permute-start.4 = (f32[16,128]{1,0:T(8,128)S(1)}, f32[16,128]{1,0:T(8,128)S(1)}, u32[]{:S(2)}, u32[]{:S(2)}) collective-permute-start(f32[16,128]{1,0:T(8,128)S(1)} %slice_add_fusion.1), channel_id=1, source_target_pairs={{0,2},{1,3},{2,0},{3,1},{4,6},{5,7},{6,4},{7,5},{8,10},{9,11},{10,... | collective-permute-start | bytes 24584 | tf_op jit(solution)/shard_map/ppermute | solution.py:544
  8.8 0.7 %copy-start.6 = (f32[7168]{0:T(1024)S(1)}, f32[7168]{0:T(1024)}, u32[]{:S(2)}) copy-start(f32[7168]{0:T(1024)} %param.12) | copy-start | bytes 86020
  9.5 14.7 %slice-start.1 = ((s8[8388608]{0:T(1024)(128)(4,1)}), s8[4194304]{0:T(1024)(128)(4,1)S(1)}, s32[]{:S(2)}) async-start(s8[8388608]{0:T(1024)(128)(4,1)} %bitcast.6), calls=%async_computation.1 | async-start | bytes 8388608
  9.5 14.7 %copy-start.1 = (f32[128,1792]{1,0:T(8,128)S(1)}, f32[128,1792]{1,0:T(8,128)}, u32[]{:S(2)}) copy-start(f32[128,1792]{1,0:T(8,128)} %rhs_ref.11) | copy-start | bytes 2752516
  22.0 4.9 %copy-start.3 = (f32[1792]{0:T(1024)S(1)}, f32[1792]{0:T(1024)}, u32[]{:S(2)}) copy-start(f32[1792]{0:T(1024)} %param.14) | copy-start | bytes 21508
  22.0 4.9 %collective-permute-start.5 = (f32[16,128]{1,0:T(8,128)S(1)}, f32[16,128]{1,0:T(8,128)S(1)}, u32[]{:S(2)}, u32[]{:S(2)}) collective-permute-start(f32[16,128]{1,0:T(8,128)S(1)} %add.27.sum_ref), channel_id=1, source_target_pairs={{0,4},{1,5},{2,6},{3,7},{4,0},{5,1},{6,2},{7,3},{8,12},{9,13},{10,... | collective-permute-start | bytes 24584 | tf_op jit(solution)/shard_map/ppermute | solution.py:544
  24.2 10.6 %copy-start.5 = (f32[1792]{0:T(1024)S(1)}, f32[1792]{0:T(1024)}, u32[]{:S(2)}) copy-start(f32[1792]{0:T(1024)} %param.9) | copy-start | bytes 21508
  25.5 9.2 %collective-permute-start.2 = (bf16[128,256]{1,0:T(8,128)(2,1)S(1)}, bf16[128,256]{1,0:T(8,128)(2,1)S(1)}, u32[]{:S(2)}, u32[]{:S(2)}) collective-permute-start(bf16[128,256]{1,0:T(8,128)(2,1)S(1)} %get-tuple-element.37), channel_id=1, source_target_pairs={{0,1},{1,0},{2,3},{3,2},{4,5},{5,4},{6,7},{7,6},{8,9},{9,8},{10,11... | collective-permute-start | bytes 196616 | tf_op jit(solution)/shard_map/ppermute | solution.py:536
  26.2 8.5 %collective-permute-start.3 = (bf16[128,256]{1,0:T(8,128)(2,1)S(1)}, bf16[128,256]{1,0:T(8,128)(2,1)S(1)}, u32[]{:S(2)}, u32[]{:S(2)}) collective-permute-start(bf16[128,256]{1,0:T(8,128)(2,1)S(1)} %get-tuple-element.38), channel_id=1, source_target_pairs={{1,2},{2,1},{3,4},{4,3},{5,6},{6,5},{7,8},{8,7},{9,10},{10,9},{11,... | collective-permute-start | bytes 196616 | tf_op jit(solution)/shard_map/ppermute | solution.py:536
  26.9 10.5 %copy-start.4 = (f32[16,16]{1,0:T(8,128)S(1)}, f32[16,16]{1,0:T(8,128)}, u32[]{:S(2)}) copy-start(f32[16,16]{1,0:T(8,128)} %cinv_ref.7) | copy-start | bytes 3076
  29.8 5.0 %collective-permute-start.8 = (f32[16,128]{1,0:T(8,128)S(1)}, f32[16,128]{1,0:T(8,128)S(1)}, u32[]{:S(2)}, u32[]{:S(2)}) collective-permute-start(f32[16,128]{1,0:T(8,128)S(1)} %get-tuple-element.46), channel_id=1, source_target_pairs={{0,8},{1,9},{2,10},{3,11},{4,12},{5,13},{6,14},{7,15},{8,0},{9,1},... | collective-permute-start | bytes 24584 | tf_op jit(solution)/shard_map/ppermute | solution.py:544
  36.0 3.0 %collective-permute-start.6 = (bf16[144,256]{1,0:T(8,128)(2,1)S(1)}, bf16[144,256]{1,0:T(8,128)(2,1)S(1)}, u32[]{:S(2)}, u32[]{:S(2)}) collective-permute-start(bf16[144,256]{1,0:T(8,128)(2,1)S(1)} %get-tuple-element.44), channel_id=1, source_target_pairs={{0,1},{1,0},{2,3},{3,2},{4,5},{5,4},{6,7},{7,6},{8,9},{9,8},{10,11... | collective-permute-start | bytes 221192 | tf_op jit(solution)/shard_map/ppermute | solution.py:536
  36.7 2.3 %collective-permute-start.7 = (bf16[144,256]{1,0:T(8,128)(2,1)S(1)}, bf16[144,256]{1,0:T(8,128)(2,1)S(1)}, u32[]{:S(2)}, u32[]{:S(2)}) collective-permute-start(bf16[144,256]{1,0:T(8,128)(2,1)S(1)} %get-tuple-element.45), channel_id=1, source_target_pairs={{1,2},{2,1},{3,4},{4,3},{5,6},{6,5},{7,8},{8,7},{9,10},{10,9},{11,... | collective-permute-start | bytes 221192 | tf_op jit(solution)/shard_map/ppermute | solution.py:536
  40.0 8.4 %collective-permute-start.9 = (bf16[128,256]{1,0:T(8,128)(2,1)S(1)}, bf16[128,256]{1,0:T(8,128)(2,1)S(1)}, u32[]{:S(2)}, u32[]{:S(2)}) collective-permute-start(bf16[128,256]{1,0:T(8,128)(2,1)S(1)} %get-tuple-element.52), channel_id=1, source_target_pairs={{0,1},{1,0},{2,3},{3,2},{4,5},{5,4},{6,7},{7,6},{8,9},{9,8},{10,11... | collective-permute-start | bytes 196616 | tf_op jit(solution)/shard_map/ppermute | solution.py:536
  43.8 4.7 %collective-permute-start.10 = (bf16[128,256]{1,0:T(8,128)(2,1)S(1)}, bf16[128,256]{1,0:T(8,128)(2,1)S(1)}, u32[]{:S(2)}, u32[]{:S(2)}) collective-permute-start(bf16[128,256]{1,0:T(8,128)(2,1)S(1)} %get-tuple-element.53), channel_id=1, source_target_pairs={{1,2},{2,1},{3,4},{4,3},{5,6},{6,5},{7,8},{8,7},{9,10},{10,9},{11,... | collective-permute-start | bytes 196616 | tf_op jit(solution)/shard_map/ppermute | solution.py:536
  49.7 5.4 %collective-permute-start.11 = (f32[184,128]{1,0:T(8,128)S(1)}, f32[184,128]{1,0:T(8,128)S(1)}, u32[]{:S(2)}, u32[]{:S(2)}) collective-permute-start(f32[184,128]{1,0:T(8,128)S(1)} %get-tuple-element.61), channel_id=1, source_target_pairs={{0,1},{1,0},{2,3},{3,2},{4,5},{5,4},{6,7},{7,6},{8,9},{9,8},{10,11... | collective-permute-start | bytes 282632 | tf_op jit(solution)/shard_map/ppermute | solution.py:536
  55.1 3.9 %collective-permute-start.13 = (f32[56,128]{1,0:T(8,128)S(1)}, f32[56,128]{1,0:T(8,128)S(1)}, u32[]{:S(2)}, u32[]{:S(2)}) collective-permute-start(f32[56,128]{1,0:T(8,128)S(1)} %slice_add_fusion), channel_id=1, source_target_pairs={{0,2},{1,3},{2,0},{3,1},{4,6},{5,7},{6,4},{7,5},{8,10},{9,11},{10,... | collective-permute-start | bytes 86024 | tf_op jit(solution)/shard_map/ppermute | solution.py:544
  57.2 10.8 %collective-permute-start.12 = (f32[128,128]{1,0:T(8,128)S(1)}, f32[128,128]{1,0:T(8,128)S(1)}, u32[]{:S(2)}, u32[]{:S(2)}) collective-permute-start(f32[128,128]{1,0:T(8,128)S(1)} %get-tuple-element.62), channel_id=1, source_target_pairs={{1,2},{2,1},{3,4},{4,3},{5,6},{6,5},{7,8},{8,7},{9,10},{10,9},{11,... | collective-permute-start | bytes 196616 | tf_op jit(solution)/shard_map/ppermute | solution.py:536
  59.0 4.2 %collective-permute-start.14 = (f32[56,128]{1,0:T(8,128)S(1)}, f32[56,128]{1,0:T(8,128)S(1)}, u32[]{:S(2)}, u32[]{:S(2)}) collective-permute-start(f32[56,128]{1,0:T(8,128)S(1)} %add.30), channel_id=1, source_target_pairs={{0,4},{1,5},{2,6},{3,7},{4,0},{5,1},{6,2},{7,3},{8,12},{9,13},{10,... | collective-permute-start | bytes 86024 | tf_op jit(solution)/shard_map/ppermute | solution.py:544
  63.2 4.8 %collective-permute-start.15 = (f32[56,128]{1,0:T(8,128)S(1)}, f32[56,128]{1,0:T(8,128)S(1)}, u32[]{:S(2)}, u32[]{:S(2)}) collective-permute-start(f32[56,128]{1,0:T(8,128)S(1)} %add.31), channel_id=1, source_target_pairs={{0,8},{1,9},{2,10},{3,11},{4,12},{5,13},{6,14},{7,15},{8,0},{9,1},... | collective-permute-start | bytes 86024 | tf_op jit(solution)/shard_map/ppermute | solution.py:544

commit v4 on v3

--- a/solution.py
+++ b/solution.py
@@ -12,6 +12,7 @@
 GROUP = 8
 TURNS = 16
 EXTRA = 16
+CHUNKS = 4
 F32 = jnp.float32
 BF16 = jnp.bfloat16
 NN = (((1,), (0,)), ((), ()))
@@ -107,10 +108,18 @@
     return lax.dot_general(sums, columns, TN, precision=HIGHEST, preferred_element_type=F32)
 
 
-def begin_kernel(n, rhs_ref, cvec_ref, even_ref, odd_ref, part_ref):
+def begin_kernel(rhs_hbm, cvec_hbm, even_ref, odd_ref, part_ref, rhs_ref, cvec_ref, sem):
     me, _ = place()
-    rhs, own = rhs_ref.shape
+    _, own = rhs_ref.shape
     slots = part_ref.shape[0]
+    copies = [
+        pltpu.make_async_copy(rhs_hbm, rhs_ref, sem.at[0]),
+        pltpu.make_async_copy(cvec_hbm, cvec_ref, sem.at[1]),
+    ]
+    for copy in copies:
+        copy.start()
+    for copy in copies:
+        copy.wait()
     cvec = flat(cvec_ref)
     part = rows_of([(me, rowsum(rhs_ref[...] * cvec))], slots)
     part_ref[...] = part
@@ -123,7 +132,9 @@
     put_sides(even_ref, odd_ref, side(0), side(own - STRIP))
 
 
-def build_kernel(rows_s, rows_v, lane_v, weight_v, o_ref, token, *scratch):
+def build_kernel(rows_s, rows_v, lane_v, weight_hbm, o_ref, token, weight_v, sem, *scratch):
+    copy = pltpu.make_async_copy(weight_hbm, weight_v, sem)
+    copy.start()
     token[...] = jnp.zeros(token.shape, F32)
     merged, tables = scratch[0], scratch[1:]
     own, sub = o_ref.shape
@@ -140,6 +151,7 @@
     square = (LANES, LANES)
     down, across = iota(square, 0), iota(square, 1)
     same_group = (down // GROUP) == (across // GROUP)
+    copy.wait()
     for k in range(blocks):
         low = min(k * chunk, height)
         high = min(low + chunk, height)
@@ -200,12 +212,15 @@
     )
 
 
-def first_solve_kernel(rhs_ref, even_got, odd_got, inv_ref, token, u_ref, even_ref, odd_ref):
+def first_solve_kernel(
+    rhs_ref, even_got, odd_got, inv_ref, token, sum_ref, sum_got, u_ref, even_ref, odd_ref, sum_out
+):
     rhs = rhs_ref.shape[0]
     left, right = take_sides(even_got[0:rhs, :], odd_got[0:rhs, :])
     wide = jnp.concatenate([left, rhs_ref[...], right], 1).astype(BF16)
     local_solve(u_ref, wide, inv_ref)
     put_strips(even_ref, odd_ref, u_ref)
+    sum_out[...] = sum_ref[...] + sum_got[...]
 
 
 def blocks_of(sub):
@@ -280,19 +295,18 @@
     )
 
 
-def first_inner_kernel(u_ref, o_ref, cvec_ref, sum_ref, sum_got, thru_ref, sum_out):
-    rhs, sub = u_ref.shape
+def first_inner_kernel(u_ref, o_ref, cvec_ref, thru_ref):
+    _, sub = u_ref.shape
     inner = slice(2 * STRIP, sub - 2 * STRIP)
     cvec = flat(cvec_ref)[:, STRIP : sub - 3 * STRIP]
     fixed = fixed_rows(cvec, inner.start, inner.stop, sub)
     value = jnp.concatenate([u_ref[:, inner], fixed], 0).astype(BF16)
     inner_product(value, o_ref, thru_ref)
-    sum_out[...] = sum_ref[...] + sum_got[...]
 
 
 def first_outer_kernel(
-    n, u_ref, even_got, odd_got, halo_even, halo_odd, o_ref, thru_ref, cvec_ref, mass_ref,
-    s_ref, y_ref, deg_ref, even_ref, odd_ref, wide_ref,
+    n, u_ref, even_got, odd_got, halo_even, halo_odd, o_ref, thru_ref, cvec_ref, mass_ref, sum_ref,
+    sum_got, s_ref, y_ref, deg_ref, even_ref, odd_ref, sum_out, wide_ref,
 ):
     rhs, sub = u_ref.shape
     left, right = take_sides(even_got[...], odd_got[...])
@@ -309,6 +323,7 @@
     outer_product(wide_ref, o_ref, thru_ref, degree, flat(mass_ref), y_ref)
     s_ref[...] = wide_ref[0:rhs, STRIP : sub - STRIP]
     put_strips(even_ref, odd_ref, y_ref)
+    sum_out[...] = sum_ref[...] + sum_got[...]
 
 
 def add_coarse(value, vectors, coarse, first):
@@ -318,13 +333,10 @@
     return value
 
 
-def solve_inner_kernel(n, y_ref, sums_ref, cinv_ref, inv_ref, own_ref, u_ref):
-    rhs, sub = u_ref.shape
+def solve_inner_kernel(y_ref, inv_ref, u_ref):
+    sub = y_ref.shape[1]
     inner = slice(2 * STRIP, sub - 2 * STRIP)
-    coarse = coarse_columns(n, sums_ref[0:n, :], cinv_ref, 2)
-    value = add_coarse(y_ref[0:rhs, inner], y_ref[rhs : rhs + 3, inner], coarse, 1)
-    own_ref[...] = value
-    high = value.astype(BF16)
+    high = y_ref[:, inner].astype(BF16)
     tall = 256
     for j in range(sub // tall):
         cols = slice(j * tall, (j + 1) * tall)
@@ -332,12 +344,13 @@
 
 
 def solve_outer_kernel(
-    n, y_ref, even_got, odd_got, sums_ref, cinv_ref, inv_ref, inner_ref, half_ref,
-    own_ref, u_ref, even_ref, odd_ref,
+    n, y_ref, even_got, odd_got, sum_ref, sum_got, cinv_ref, inv_ref, half_ref,
+    own_ref, u_ref, even_ref, odd_ref, sums_ref,
 ):
     rhs, sub = u_ref.shape
     w = STRIP
     first, last = ends(n)
+    sums_ref[...] = sum_ref[...] + sum_got[...]
     coarse = coarse_columns(n, sums_ref[0:n, :], cinv_ref, 2)
     left, right = take_sides(even_got[...], odd_got[...])
     left = add_coarse(left[0:rhs], left[rhs : rhs + 3], coarse, 0)
@@ -345,8 +358,11 @@
     low, high = slice(0, 2 * w), slice(sub - 2 * w, sub)
     left = left + add_coarse(y_ref[0:rhs, low], y_ref[rhs : rhs + 3, low], coarse, 1)
     right = right + add_coarse(y_ref[0:rhs, high], y_ref[rhs : rhs + 3, high], coarse, 1)
+    inner = slice(2 * w, sub - 2 * w)
     own_ref[:, 0:w] = left[:, w:]
-    own_ref[:, w : sub - 3 * w] = inner_ref[...]
+    own_ref[:, w : sub - 3 * w] = add_coarse(
+        y_ref[0:rhs, inner], y_ref[rhs : rhs + 3, inner], coarse, 1
+    )
     own_ref[:, sub - 3 * w :] = right[:, 0:w]
     both = jnp.concatenate(
         [left[:, 0:w] * first, left[:, w:], right[:, 0:w], right[:, w:] * last], 1
@@ -355,7 +371,8 @@
     for j in range(sub // tall):
         cols = slice(j * tall, (j + 1) * tall)
         part = jnp.concatenate([inv_ref[low, cols], inv_ref[high, cols]], 0)
-        u_ref[:, cols] = half_ref[:, cols] + jnp.dot(both, part, preferred_element_type=F32)
+        part = jnp.dot(both, part, preferred_element_type=F32) + half_ref[0:rhs, cols]
+        u_ref[:, cols] = add_coarse(part, half_ref[rhs : rhs + 3, cols], coarse, 1)
     put_strips(even_ref, odd_ref, u_ref)
 
 
@@ -372,7 +389,7 @@
     z = s_ref[...] + coarse[:, 0:1] * cvec
     z_ref[...] = z
     left, right = take_sides(even_got[rhs:, STRIP:], odd_got[rhs:, STRIP:])
-    unused, right = take_sides(even_got[rhs:, 0:STRIP], odd_got[rhs:, 0:STRIP])
+    _, right = take_sides(even_got[rhs:, 0:STRIP], odd_got[rhs:, 0:STRIP])
     mine = coarse_rows[rhs:, STRIP : sub - STRIP]
     lefts = [left[1:2, :], left[2:3, :], None]
     rights = [None, right[0:1, :], right[1:2, :]]
@@ -465,13 +482,14 @@
 
 
 def finish_kernel(
-    n, rhs_ref, z_ref, y_ref, w_ref, q_ref, g_ref, even_got, odd_got, first_ref, part_ref,
-    cinv_ref, cvec_ref, x_ref, r_ref,
+    n, rhs_ref, z_ref, y_ref, w_ref, q_ref, g_ref, even_got, odd_got, first_ref, part_in, more_ref,
+    cinv_ref, cvec_ref, x_hbm, r_hbm, x_ref, r_ref, sem,
 ):
-    me, _ = place()
+    _, _ = place()
     rhs, own = rhs_ref.shape
     slots = up(n, 8)
     first = first_ref[0:n, :]
+    part_ref = part_in[...] + more_ref[...]
     rho, cross = part_ref[0:n, :], part_ref[2 * slots : 2 * slots + n, :]
     gram = part_ref[slots : slots + n, :]
     sums = part_ref[3 * slots :, :]
@@ -503,26 +521,39 @@
     near = jnp.transpose(jnp.broadcast_to(alpha + step * (1.0 + beta), (LANES, rhs)))[:, 0:1]
     far = jnp.transpose(jnp.broadcast_to(alpha * step, (LANES, rhs)))[:, 0:1]
     coarse = coarse_columns(n, rho, cinv_ref, 1) * far
-    x_ref[...] = near * z_ref[...] - far * w_ref[...] - coarse[:, 1:2] * flat(cvec_ref)
+    cvec = flat(cvec_ref)
     left, right = take_sides(even_got[0:rhs, :], odd_got[...])
-    r_ref[...] = add_coarse(
-        rhs_ref[...] - near * y_ref[...] + far * q_ref[...], g_ref[...], coarse, 0
-    )
-    r_ref[:, 0:STRIP] += far * left
-    r_ref[:, own - STRIP :] += far * right
-
-
-def call(kernel, name, outs, scratch, limit, count, in_specs=None, flops=0):
+    edge = {0: far * left, own - STRIP: far * right}
+    tall = rhs // CHUNKS
+    copies = []
+    for i in range(CHUNKS):
+        at = slice(i * tall, (i + 1) * tall)
+        p, s, c = near[at], far[at], coarse[at]
+        x_ref[at, :] = p * z_ref[at, :] - s * w_ref[at, :] - c[:, 1:2] * cvec
+        r_ref[at, :] = add_coarse(
+            rhs_ref[at, :] - p * y_ref[at, :] + s * q_ref[at, :], g_ref[...], c, 0
+        )
+        for start, value in edge.items():
+            r_ref[at, start : start + STRIP] += value[at]
+        for k, (source, target) in enumerate(((x_ref, x_hbm), (r_ref, r_hbm))):
+            copy = pltpu.make_async_copy(source.at[at, :], target.at[at, :], sem.at[k, i])
+            copy.start()
+            copies.append(copy)
+    for copy in copies:
+        copy.wait()
+
+
+def call(kernel, outs, scratch, limit, count, in_specs=None, out_space=None, flops=0):
     vmem = pl.BlockSpec(memory_space=pltpu.VMEM)
+    out_spec = vmem if out_space is None else pl.BlockSpec(memory_space=out_space)
     return pl.pallas_call(
         kernel,
         out_shape=[jax.ShapeDtypeStruct(s, d) for s, d in outs],
         in_specs=in_specs if in_specs is not None else [vmem] * count,
-        out_specs=[vmem] * len(outs),
+        out_specs=[out_spec] * len(outs),
         scratch_shapes=scratch,
         compiler_params=pltpu.CompilerParams(vmem_limit_bytes=limit << 20),
         cost_estimate=pl.CostEstimate(flops=flops, bytes_accessed=0, transcendentals=0),
-        name=name,
     )
 
 
@@ -545,10 +576,11 @@
 
 
 def finish_sum(part, hop):
-    while hop < lax.axis_size("tile"):
+    n = lax.axis_size("tile")
+    while 2 * hop < n:
         part = part + across(part, hop)
         hop *= 2
-    return part
+    return part, across(part, hop)
 
 
 def shards(
@@ -568,7 +600,15 @@
 
     side = ((rows + 8 + slots, STRIP), F32)
     few = ((slots, rows), F32)
-    even, odd, part = call(bind(begin_kernel, n), "begin", [side, side, few], [], 4, 2)(rhs, cvec)
+    hbm = pl.BlockSpec(memory_space=pltpu.HBM)
+    even, odd, part = call(
+        begin_kernel,
+        [side, side, few],
+        [pltpu.VMEM(rhs.shape, F32), pltpu.VMEM(cvec.shape, F32), pltpu.SemaphoreType.DMA((2,))],
+        4,
+        2,
+        in_specs=[hbm, hbm],
+    )(rhs, cvec)
     halo = swap((even, odd))
     part = part + halo[0][rows + 8 :]
 
@@ -576,60 +616,42 @@
     shape = (edges // LANES, LANES)
     stiff, token = call(
         build_kernel,
-        "build",
         [((own, sub), BF16), ((8, LANES), F32)],
-        [pltpu.VMEM((edges, LANES), F32)] + [pltpu.VMEM((sub // LANES * own, LANES), F32)] * 2,
+        [pltpu.VMEM(shape, F32), pltpu.SemaphoreType.DMA, pltpu.VMEM((edges, LANES), F32)]
+        + [pltpu.VMEM((sub // LANES * own, LANES), F32)] * 2,
         34,
         4,
-        in_specs=[smem, vmem, vmem, vmem],
+        in_specs=[smem, vmem, vmem, hbm],
         flops=10**10,
     )(at, at.reshape(shape), (edge_tails & 127).reshape(shape), edge_weight.reshape(shape))
-    part = part + across(part, 2)
 
     whole, owned = ((rows, sub), F32), ((rows, own), F32)
     strip = ((rows, 2 * STRIP), BF16)
     extra = ((rows + EXTRA, sub), F32)
-    u, even, odd = call(
-        first_solve_kernel, "solve", [whole, strip, strip], [], 12, 5, flops=10**9
-    )(rhs, *halo, local_inverse, token)
+    u, even, odd, part = call(
+        first_solve_kernel, [whole, strip, strip, few], [], 12, 7, flops=10**9
+    )(rhs, *halo, local_inverse, token, part, across(part, 2))
     got = swap((even, odd))
-    thru, part = call(first_inner_kernel, "inner", [extra, few], [], 8, 5, flops=2 * 10**9)(
-        u, stiff, cvec, part, across(part, 4)
-    )
-    sums = finish_sum(part, 8)
+    (thru,) = call(first_inner_kernel, [extra], [], 8, 3, flops=2 * 10**9)(
+        u, stiff, cvec
+    )
     strips = ((rows + EXTRA, 2 * STRIP), BF16)
-    s, y_part, degree, even, odd = call(
+    s, y_part, degree, even, odd, part = call(
         bind(first_outer_kernel, n),
-        "outer",
-        [owned, extra, ((8, sub), F32), strips, strips],
+        [owned, extra, ((8, sub), F32), strips, strips, few],
         [pltpu.VMEM(*extra)],
         12,
-        9,
+        11,
         flops=10**9,
-    )(u, *got, *halo, stiff, thru, cvec, mass)
+    )(u, *got, *halo, stiff, thru, cvec, mass, part, across(part, 4))
     got_y = swap((even, odd))
-    inner, half = call(
-        bind(solve_inner_kernel, n),
-        "solve_inner",
-        [((rows, own - 2 * STRIP), F32), whole],
-        [],
-        8,
-        4,
-        flops=10**9,
-    )(y_part, sums, coarse_inv, local_inverse)
-    y, u, even, odd = call(
-        bind(solve_outer_kernel, n),
-        "solve_outer",
-        [owned, whole, strip, strip],
-        [],
-        12,
-        8,
-        flops=10**8,
-    )(y_part, *got_y, sums, coarse_inv, local_inverse, inner, half)
+    (half,) = call(solve_inner_kernel, [extra], [], 8, 2, flops=10**9)(y_part, local_inverse)
+    y, u, even, odd, sums = call(
+        bind(solve_outer_kernel, n), [owned, whole, strip, strip, few], [], 12, 8, flops=10**8
+    )(y_part, *got_y, *finish_sum(part, 8), coarse_inv, local_inverse, half)
     got = swap((even, odd))
     z, g, part = call(
         bind(between_kernel, n),
-        "between",
         [owned, ((8, own), F32), ((2 * slots + 8, rows), F32)],
         [],
         8,
@@ -637,12 +659,11 @@
         flops=10**9,
     )(s, y, y_part, *got_y, sums, coarse_inv, cvec, rhs)
     thru, dots = call(
-        next_inner_kernel, "inner2", [whole, ((rows, LANES), F32)], [], 8, 5, flops=2 * 10**9
+        next_inner_kernel, [whole, ((rows, LANES), F32)], [], 8, 5, flops=2 * 10**9
     )(u, stiff, rhs, y, g)
     many = 3 * slots + 8
     w, q, even, odd, part = call(
         bind(next_outer_kernel, n),
-        "outer2",
         [owned, owned, ((rows + many, STRIP), F32), ((rows, STRIP), F32), ((many, rows), F32)],
         [pltpu.VMEM(*whole), pltpu.VMEM(*whole)],
         12,
@@ -650,11 +671,16 @@
         flops=10**9,
     )(u, *got, stiff, thru, dots, degree, mass, rhs, y, g, part)
     got = swap((even, odd))
-    part = finish_sum(part + got[0][rows:], 2)
+    part, more = finish_sum(part + got[0][rows:], 2)
     return tuple(
-        call(bind(finish_kernel, n), "finish", [owned, owned], [], 16, 12)(
-            rhs, z, y, w, q, g, *got, sums, part, coarse_inv, cvec
-        )
+        call(
+            bind(finish_kernel, n),
+            [owned, owned],
+            [pltpu.VMEM(*owned)] * 2 + [pltpu.SemaphoreType.DMA((2, CHUNKS))],
+            16,
+            13,
+            out_space=pltpu.HBM,
+        )(rhs, z, y, w, q, g, *got, sums, part, more, coarse_inv, cvec)
     )
 
 

time: 70.8 us -> 69.5 us (0.982)
  starting transfers between devices: 29.3 us -> 28 us
    ppermute x10, starting transfers between devices: 13.8 us -> 12.2 us  [swap(): got.append(lax.ppermute(payload, 'tile', links))]
  transfers between devices with their start and end apart: 16 -> 16, of which waited for: 5 -> 4; matrix products, arithmetic and copies ran while one was open for 1% -> 1% of each run, Pallas kernels for 31% -> 30%
where the time goes in v4:
time: 69.5 us; the launch traced here: 69.1 us
  Pallas kernels  28.1 us (40%)
  starting transfers between devices  28 us (40%)
  waiting for transfers between devices  8.39 us (12%)
  local copies, waits for them, and re-layouts  2.8 us (4%)
  between operations  1.08 us (2%)
  other arithmetic  0.8 us (1%)
    ppermute x6, starting transfers between devices, across(): return lax.ppermute(part, 'tile', [(i, i ^ hop) for i in range(n)])  15.8 us
    pallas_call x1, Pallas kernels, shards(): call(build_kernel, [((own, sub), BF16), ((8, LANES), F32)], [pltpu.VMEM(s...  12.6 us
    ppermute x10, starting transfers between devices, swap(): got.append(lax.ppermute(payload, 'tile', links))  12.2 us
    ppermute x6, waiting for transfers between devices, across(): return lax.ppermute(part, 'tile', [(i, i ^ hop) for i in range(n)])  7.43 us
    pallas_call x1, Pallas kernels, shards(): call(next_inner_kernel, [whole, ((rows, LANES), F32)], [], 8, 5, flops=2...  3.12 us
    pallas_call x1, Pallas kernels, shards(): call(first_inner_kernel, [extra], [], 8, 3, flops=2 * 10 ** 9)  2.88 us
    unnamed x18, local copies, waits for them, and re-layouts  2.8 us
    pallas_call x1, Pallas kernels, shards(): call(bind(finish_kernel, n), [owned, owned], [pltpu.VMEM(*owned)] * 2 + [...  2.1 us
  transfers between devices with their start and end apart: 16, of which 4 were waited for; matrix products, arithmetic and copies ran while one was open for 1% of the time, Pallas kernels for 30%

profile of v4, /device:TPU:0, one launch (start us, length us, event | category | flops | bytes accessed | tf_op | source)
XLA Modules:
  0.0 69.1 jit_solution(9326851381921181461)
XLA Ops:
  0.6 1.2 %copy-done = f32[128,1792]{1,0:T(8,128)S(1)} copy-done((f32[128,1792]{1,0:T(8,128)S(1)}, f32[128,1792]{1,0:T(8,128)}, u32[]{:S(2)}) %copy-start) | copy-done | bytes 917528
  1.8 0.7 %copy-done.2 = f32[1792]{0:T(1024)S(1)} copy-done((f32[1792]{0:T(1024)S(1)}, f32[1792]{0:T(1024)}, u32[]{:S(2)}) %copy-start.2) | copy-done | bytes 7192
  3.0 0.6 collective-permute-start
  3.5 0.7 collective-permute-start.1
  4.2 0.8 %and_bitcast_fusion = (s32[56,128]{1,0:T(8,128)S(1)}, s32[7168]{0:T(1024)S(1)}) fusion(s32[7168]{0:T(1024)} %param.11, s32[7168]{0:T(1024)} %param.10), kind=kLoop, calls=%fused_computation.1 | loop fusion | flops 35840 | bytes 114688 | tf_op jit(solution)/shard_map/reshape | solution.py:626
  5.0 3.8 %collective-permute-start.2 = (f32[16,128]{1,0:T(8,128)S(1)}, f32[16,128]{1,0:T(8,128)S(1)}, u32[]{:S(2)}, u32[]{:S(2)}) collective-permute-start(f32[16,128]{1,0:T(8,128)S(1)} %slice_add_fusion.1.sum_ref), channel_id=1, source_target_pairs={{0,2},{1,3},{2,0},{3,1},{4,6},{5,7},{6,4},{7,5},{8,10},{9,11},{10,... | collective-permute-start | bytes 24584 | tf_op jit(solution)/shard_map/ppermute | solution.py:575
  8.8 0.9 %copy-done.6 = f32[7168]{0:T(1024)S(1)} copy-done((f32[7168]{0:T(1024)S(1)}, f32[7168]{0:T(1024)}, u32[]{:S(2)}) %copy-start.6) | copy-done | bytes 28696
  9.7 12.6 %shard_map.96 = (bf16[1792,2048]{1,0:T(8,128)(2,1)S(1)}, f32[8,128]{1,0:T(8,128)S(1)}) custom-call(s32[7168]{0:T(1024)S(1)} %get-tuple-element.63.rows_s, s32[56,128]{1,0:T(8,128)S(1)} %bitcast.15, s32[56,128]{1,0:T(8,128)S(1)} %get-tuple-element.62.lane_v, f32[56,128]{1,0:T(8,128)S(1)} %bitcast.16), custom_call_target="tpu_custom_call" | custom-call | flops 10000000000 | tf_op jit(solution)/shard_map/pallas_call | solution.py:617
  22.3 1.3 %shard_map.97 = (f32[128,2048]{1,0:T(8,128)S(1)}, bf16[128,256]{1,0:T(8,128)(2,1)S(1)}, bf16[128,256]{1,0:T(8,128)(2,1)S(1)}, f32[16,128]{1,0:T(8,128)S(1)}) custom-call(f32[128,1792]{1,0:T(8,128)S(1)} %copy-done.1, f32[152,128]{1,0:T(8,128)S(1)} %collective-permute-done.even_got.halo_even, f32[152,128]{1,0:T(8,128)S(1)} %collective-permute-done.1.odd_got.halo_odd, ...), custom_call_target="tpu_custom_call" | custom-call | flops 1000000000 | tf_op jit(solution)/shard_map/pallas_call | solution.py:631
  23.7 2.3 %collective-permute-start.5 = (f32[16,128]{1,0:T(8,128)S(1)}, f32[16,128]{1,0:T(8,128)S(1)}, u32[]{:S(2)}, u32[]{:S(2)}) collective-permute-start(f32[16,128]{1,0:T(8,128)S(1)} %get-tuple-element.40.sum_ref), channel_id=1, source_target_pairs={{0,4},{1,5},{2,6},{3,7},{4,0},{5,1},{6,2},{7,3},{8,12},{9,13},{10,... | collective-permute-start | bytes 24584 | tf_op jit(solution)/shard_map/ppermute | solution.py:575
  26.4 0.7 collective-permute-start.4
  27.1 2.9 %shard_map.98.thru_ref = f32[144,2048]{1,0:T(8,128)S(1)} custom-call(f32[128,2048]{1,0:T(8,128)S(1)} %get-tuple-element.36.u_ref, bf16[1792,2048]{1,0:T(8,128)(2,1)S(1)} %get-tuple-element.39.o_ref, f32[14,128]{1,0:T(8,128)S(1)} %bitcast.9), custom_call_target="tpu_custom_call" | custom-call | flops 2000000000 | tf_op jit(solution)/shard_map/pallas_call | solution.py:635
  30.0 1.2 %shard_map.99 = (f32[128,1792]{1,0:T(8,128)S(1)}, f32[144,2048]{1,0:T(8,128)S(1)}, f32[8,2048]{1,0:T(8,128)S(1)}, bf16[144,256]{1,0:T(8,128)(2,1)S(1)}, bf16[144...) custom-call(f32[128,2048]{1,0:T(8,128)S(1)} %get-tuple-element.36.u_ref, ...), custom_call_target="tpu_custom_call" | custom-call | flops 1000000000 | tf_op jit(solution)/shard_map/pallas_call | solution.py:639
  31.2 5.1 %collective-permute-start.8 = (f32[16,128]{1,0:T(8,128)S(1)}, f32[16,128]{1,0:T(8,128)S(1)}, u32[]{:S(2)}, u32[]{:S(2)}) collective-permute-start(f32[16,128]{1,0:T(8,128)S(1)} %get-tuple-element.45.sum_ref), channel_id=1, source_target_pairs={{0,8},{1,9},{2,10},{3,11},{4,12},{5,13},{6,14},{7,15},{8,0},{9,1},... | collective-permute-start | bytes 24584 | tf_op jit(solution)/shard_map/ppermute | solution.py:575
  36.3 0.7 collective-permute-start.7
  37.0 1.1 %shard_map.100.half_ref = f32[144,2048]{1,0:T(8,128)S(1)} custom-call(f32[144,2048]{1,0:T(8,128)S(1)} %get-tuple-element.42.y_ref.coarse_rows, bf16[2048,2048]{1,0:T(8,128)(2,1)S(1)} %bitcast.7), custom_call_target="tpu_custom_call" | custom-call | flops 1000000000 | tf_op jit(solution)/shard_map/pallas_call | solution.py:648
  38.2 1.4 %shard_map.101 = (f32[128,1792]{1,0:T(8,128)S(1)}, f32[128,2048]{1,0:T(8,128)S(1)}, bf16[128,256]{1,0:T(8,128)(2,1)S(1)}, bf16[128,256]{1,0:T(8,128)(2,1)S(1)}, f32[16,128]{1,0:T(8,128)S(1)}) custom-call(f32[144,2048]{1,0:T(8,128)S(1)} %get-tuple-element.42.y_ref.coarse_rows, bf16[144,256]{1,0:T(8,128)(2,1)S(1)} %collective-permute-done.6.even_got, ...), custom_call_target="tpu_custom_call" | custom-call | flops 100000000 | tf_op jit(solution)/shard_map/pallas_call | solution.py:649
  39.6 4.4 %collective-permute-start.9 = (bf16[128,256]{1,0:T(8,128)(2,1)S(1)}, bf16[128,256]{1,0:T(8,128)(2,1)S(1)}, u32[]{:S(2)}, u32[]{:S(2)}) collective-permute-start(bf16[128,256]{1,0:T(8,128)(2,1)S(1)} %get-tuple-element.50), channel_id=1, source_target_pairs={{0,1},{1,0},{2,3},{3,2},{4,5},{5,4},{6,7},{7,6},{8,9},{9,8},{10,11... | collective-permute-start | bytes 196616 | tf_op jit(solution)/shard_map/ppermute | solution.py:567
  44.0 0.8 %collective-permute-start.10 = (bf16[128,256]{1,0:T(8,128)(2,1)S(1)}, bf16[128,256]{1,0:T(8,128)(2,1)S(1)}, u32[]{:S(2)}, u32[]{:S(2)}) collective-permute-start(bf16[128,256]{1,0:T(8,128)(2,1)S(1)} %get-tuple-element.51), channel_id=1, source_target_pairs={{1,2},{2,1},{3,4},{4,3},{5,6},{6,5},{7,8},{8,7},{9,10},{10,9},{11,... | collective-permute-start | bytes 196616 | tf_op jit(solution)/shard_map/ppermute | solution.py:567
  44.8 0.7 %shard_map.102 = (f32[128,1792]{1,0:T(8,128)S(1)}, f32[8,1792]{1,0:T(8,128)S(1)}, f32[40,128]{1,0:T(8,128)S(1)}) custom-call(f32[128,1792]{1,0:T(8,128)S(1)} %get-tuple-element.41.s_ref, f32[128,1792]{1,0:T(8,128)S(1)} %get-tuple-element.46.y_ref, f32[144,2048]{1,0:T(8,128)S(1)} %get-tuple-element.42.y_ref.coarse_rows, ...), custom_call_target="tpu_custom_call" | custom-call | flops 1000000000 | tf_op jit(solution)/shard_map/pallas_call | solution.py:653
  45.5 3.1 %shard_map.103 = (f32[128,2048]{1,0:T(8,128)S(1)}, f32[128,128]{1,0:T(8,128)S(1)}) custom-call(f32[128,2048]{1,0:T(8,128)S(1)} %get-tuple-element.49.u_ref, bf16[1792,2048]{1,0:T(8,128)(2,1)S(1)} %get-tuple-element.39.o_ref, f32[128,1792]{1,0:T(8,128)S(1)} %copy-done.1, f32[128,1792]{1,0:T(8,128)S(1)} %get-tuple-element.46.y_ref, ...), custom_call_target="tpu_custom_call" | custom-call | flops 2000000000 | tf_op jit(solution)/shard_map/pallas_call | solution.py:661
  48.7 1.2 %shard_map.104 = (f32[128,1792]{1,0:T(8,128)S(1)}, f32[128,1792]{1,0:T(8,128)S(1)}, f32[184,128]{1,0:T(8,128)S(1)}, f32[128,128]{1,0:T(8,128)S(1)}, f32[56,128]{1,0:T(8,128)S(1)}) custom-call(f32[128,2048]{1,0:T(8,128)S(1)} %get-tuple-element.49.u_ref, bf16[128,256]{1,0:T(8,128)(2,1)S(1)} %collective-permute-done.9.even_got, ...), custom_call_target="tpu_custom_call" | custom-call | flops 1000000000 | tf_op jit(solution)/shard_map/pallas_call | solution.py:665
  49.9 3.3 %collective-permute-start.11 = (f32[184,128]{1,0:T(8,128)S(1)}, f32[184,128]{1,0:T(8,128)S(1)}, u32[]{:S(2)}, u32[]{:S(2)}) collective-permute-start(f32[184,128]{1,0:T(8,128)S(1)} %get-tuple-element.59), channel_id=1, source_target_pairs={{0,1},{1,0},{2,3},{3,2},{4,5},{5,4},{6,7},{7,6},{8,9},{9,8},{10,11... | collective-permute-start | bytes 282632 | tf_op jit(solution)/shard_map/ppermute | solution.py:567
  53.2 0.9 %collective-permute-done.11.even_got = f32[184,128]{1,0:T(8,128)S(1)} collective-permute-done((f32[184,128]{1,0:T(8,128)S(1)}, f32[184,128]{1,0:T(8,128)S(1)}, u32[]{:S(2)}, u32[]{:S(2)}) %collective-permute-start.11) | collective-permute-done | bytes 94240 | tf_op jit(solution)/shard_map/ppermute | solution.py:567
  54.2 1.6 %collective-permute-start.13 = (f32[56,128]{1,0:T(8,128)S(1)}, f32[56,128]{1,0:T(8,128)S(1)}, u32[]{:S(2)}, u32[]{:S(2)}) collective-permute-start(f32[56,128]{1,0:T(8,128)S(1)} %slice_add_fusion), channel_id=1, source_target_pairs={{0,2},{1,3},{2,0},{3,1},{4,6},{5,7},{6,4},{7,5},{8,10},{9,11},{10,... | collective-permute-start | bytes 86024 | tf_op jit(solution)/shard_map/ppermute | solution.py:575
  55.8 0.7 collective-permute-start.12
  56.5 1.6 %collective-permute-done.13 = f32[56,128]{1,0:T(8,128)S(1)} collective-permute-done((f32[56,128]{1,0:T(8,128)S(1)}, f32[56,128]{1,0:T(8,128)S(1)}, u32[]{:S(2)}, u32[]{:S(2)}) %collective-permute-start.13) | collective-permute-done | bytes 28704 | tf_op jit(solution)/shard_map/ppermute | solution.py:575
  58.1 1.3 %collective-permute-start.14 = (f32[56,128]{1,0:T(8,128)S(1)}, f32[56,128]{1,0:T(8,128)S(1)}, u32[]{:S(2)}, u32[]{:S(2)}) collective-permute-start(f32[56,128]{1,0:T(8,128)S(1)} %add.19), channel_id=1, source_target_pairs={{0,4},{1,5},{2,6},{3,7},{4,0},{5,1},{6,2},{7,3},{8,12},{9,13},{10,... | collective-permute-start | bytes 86024 | tf_op jit(solution)/shard_map/ppermute | solution.py:575
  59.4 2.7 %collective-permute-done.14 = f32[56,128]{1,0:T(8,128)S(1)} collective-permute-done((f32[56,128]{1,0:T(8,128)S(1)}, f32[56,128]{1,0:T(8,128)S(1)}, u32[]{:S(2)}, u32[]{:S(2)}) %collective-permute-start.14) | collective-permute-done | bytes 28704 | tf_op jit(solution)/shard_map/ppermute | solution.py:575
  62.1 1.7 %collective-permute-start.15 = (f32[56,128]{1,0:T(8,128)S(1)}, f32[56,128]{1,0:T(8,128)S(1)}, u32[]{:S(2)}, u32[]{:S(2)}) collective-permute-start(f32[56,128]{1,0:T(8,128)S(1)} %add.20.part_in), channel_id=1, source_target_pairs={{0,8},{1,9},{2,10},{3,11},{4,12},{5,13},{6,14},{7,15},{8,0},{9,1},... | collective-permute-start | bytes 86024 | tf_op jit(solution)/shard_map/ppermute | solution.py:575
  63.8 3.1 %collective-permute-done.15.more_ref = f32[56,128]{1,0:T(8,128)S(1)} collective-permute-done((f32[56,128]{1,0:T(8,128)S(1)}, f32[56,128]{1,0:T(8,128)S(1)}, u32[]{:S(2)}, u32[]{:S(2)}) %collective-permute-start.15) | collective-permute-done | bytes 28704 | tf_op jit(solution)/shard_map/ppermute | solution.py:575
  66.9 2.1 %shard_map.105 = (f32[128,1792]{1,0:T(8,128)}, f32[128,1792]{1,0:T(8,128)}) custom-call(f32[128,1792]{1,0:T(8,128)S(1)} %copy-done.1, f32[128,1792]{1,0:T(8,128)S(1)} %get-tuple-element.48.z_ref, f32[128,1792]{1,0:T(8,128)S(1)} %get-tuple-element.46.y_ref, f32[128,1792]{1,0:T(8,128)S(1)} %get-tuple-element.57.w_ref, ...), custom_call_target="tpu_custom_call" | custom-call | tf_op jit(solution)/shard_map/pallas_call | solution.py:676
  (35 shorter events, 1.0 us)
Async XLA Ops:
  0.6 1.2 %copy-start = (f32[128,1792]{1,0:T(8,128)S(1)}, f32[128,1792]{1,0:T(8,128)}, u32[]{:S(2)}) copy-start(f32[128,1792]{1,0:T(8,128)} %rhs_ref.9) | copy-start | bytes 2752516
  1.8 0.7 %copy-start.2 = (f32[1792]{0:T(1024)S(1)}, f32[1792]{0:T(1024)}, u32[]{:S(2)}) copy-start(f32[1792]{0:T(1024)} %param.14) | copy-start | bytes 21508
  3.0 2.0 %collective-permute-start = (f32[152,128]{1,0:T(8,128)S(1)}, f32[152,128]{1,0:T(8,128)S(1)}, u32[]{:S(2)}, u32[]{:S(2)}) collective-permute-start(f32[152,128]{1,0:T(8,128)S(1)} %get-tuple-element.32), channel_id=1, source_target_pairs={{0,1},{1,0},{2,3},{3,2},{4,5},{5,4},{6,7},{7,6},{8,9},{9,8},{10,11... | collective-permute-start | bytes 233480 | tf_op jit(solution)/shard_map/ppermute | solution.py:567
  3.5 18.7 %collective-permute-start.1 = (f32[152,128]{1,0:T(8,128)S(1)}, f32[152,128]{1,0:T(8,128)S(1)}, u32[]{:S(2)}, u32[]{:S(2)}) collective-permute-start(f32[152,128]{1,0:T(8,128)S(1)} %get-tuple-element.33), channel_id=1, source_target_pairs={{1,2},{2,1},{3,4},{4,3},{5,6},{6,5},{7,8},{8,7},{9,10},{10,9},{11,... | collective-permute-start | bytes 233480 | tf_op jit(solution)/shard_map/ppermute | solution.py:567
  5.0 17.3 %collective-permute-start.2 = (f32[16,128]{1,0:T(8,128)S(1)}, f32[16,128]{1,0:T(8,128)S(1)}, u32[]{:S(2)}, u32[]{:S(2)}) collective-permute-start(f32[16,128]{1,0:T(8,128)S(1)} %slice_add_fusion.1.sum_ref), channel_id=1, source_target_pairs={{0,2},{1,3},{2,0},{3,1},{4,6},{5,7},{6,4},{7,5},{8,10},{9,11},{10,... | collective-permute-start | bytes 24584 | tf_op jit(solution)/shard_map/ppermute | solution.py:575
  8.8 13.5 %slice-start = ((s8[8388608]{0:T(1024)(128)(4,1)}), s8[4194304]{0:T(1024)(128)(4,1)S(1)}, s32[]{:S(2)}) async-start(s8[8388608]{0:T(1024)(128)(4,1)} %bitcast.6), calls=%async_computation | async-start | bytes 8388608
  8.8 0.9 %copy-start.6 = (f32[7168]{0:T(1024)S(1)}, f32[7168]{0:T(1024)}, u32[]{:S(2)}) copy-start(f32[7168]{0:T(1024)} %param.12) | copy-start | bytes 86020
  9.7 12.6 %slice-start.1 = ((s8[8388608]{0:T(1024)(128)(4,1)}), s8[4194304]{0:T(1024)(128)(4,1)S(1)}, s32[]{:S(2)}) async-start(s8[8388608]{0:T(1024)(128)(4,1)} %bitcast.6), calls=%async_computation.1 | async-start | bytes 8388608
  9.7 12.6 %copy-start.1 = (f32[128,1792]{1,0:T(8,128)S(1)}, f32[128,1792]{1,0:T(8,128)}, u32[]{:S(2)}) copy-start(f32[128,1792]{1,0:T(8,128)} %rhs_ref.9) | copy-start | bytes 2752516
  22.3 4.8 %copy-start.3 = (f32[1792]{0:T(1024)S(1)}, f32[1792]{0:T(1024)}, u32[]{:S(2)}) copy-start(f32[1792]{0:T(1024)} %param.14) | copy-start | bytes 21508
  23.7 6.3 %collective-permute-start.5 = (f32[16,128]{1,0:T(8,128)S(1)}, f32[16,128]{1,0:T(8,128)S(1)}, u32[]{:S(2)}, u32[]{:S(2)}) collective-permute-start(f32[16,128]{1,0:T(8,128)S(1)} %get-tuple-element.40.sum_ref), channel_id=1, source_target_pairs={{0,4},{1,5},{2,6},{3,7},{4,0},{5,1},{6,2},{7,3},{8,12},{9,13},{10,... | collective-permute-start | bytes 24584 | tf_op jit(solution)/shard_map/ppermute | solution.py:575
  25.9 4.1 %collective-permute-start.3 = (bf16[128,256]{1,0:T(8,128)(2,1)S(1)}, bf16[128,256]{1,0:T(8,128)(2,1)S(1)}, u32[]{:S(2)}, u32[]{:S(2)}) collective-permute-start(bf16[128,256]{1,0:T(8,128)(2,1)S(1)} %get-tuple-element.37), channel_id=1, source_target_pairs={{0,1},{1,0},{2,3},{3,2},{4,5},{5,4},{6,7},{7,6},{8,9},{9,8},{10,11... | collective-permute-start | bytes 196616 | tf_op jit(solution)/shard_map/ppermute | solution.py:567
  26.4 3.6 %collective-permute-start.4 = (bf16[128,256]{1,0:T(8,128)(2,1)S(1)}, bf16[128,256]{1,0:T(8,128)(2,1)S(1)}, u32[]{:S(2)}, u32[]{:S(2)}) collective-permute-start(bf16[128,256]{1,0:T(8,128)(2,1)S(1)} %get-tuple-element.38), channel_id=1, source_target_pairs={{1,2},{2,1},{3,4},{4,3},{5,6},{6,5},{7,8},{8,7},{9,10},{10,9},{11,... | collective-permute-start | bytes 196616 | tf_op jit(solution)/shard_map/ppermute | solution.py:567
  27.1 2.9 %copy-start.5 = (f32[1792]{0:T(1024)S(1)}, f32[1792]{0:T(1024)}, u32[]{:S(2)}) copy-start(f32[1792]{0:T(1024)} %param.9) | copy-start | bytes 21508
  31.2 6.9 %collective-permute-start.8 = (f32[16,128]{1,0:T(8,128)S(1)}, f32[16,128]{1,0:T(8,128)S(1)}, u32[]{:S(2)}, u32[]{:S(2)}) collective-permute-start(f32[16,128]{1,0:T(8,128)S(1)} %get-tuple-element.45.sum_ref), channel_id=1, source_target_pairs={{0,8},{1,9},{2,10},{3,11},{4,12},{5,13},{6,14},{7,15},{8,0},{9,1},... | collective-permute-start | bytes 24584 | tf_op jit(solution)/shard_map/ppermute | solution.py:575
  36.3 1.8 %collective-permute-start.6 = (bf16[144,256]{1,0:T(8,128)(2,1)S(1)}, bf16[144,256]{1,0:T(8,128)(2,1)S(1)}, u32[]{:S(2)}, u32[]{:S(2)}) collective-permute-start(bf16[144,256]{1,0:T(8,128)(2,1)S(1)} %get-tuple-element.43), channel_id=1, source_target_pairs={{0,1},{1,0},{2,3},{3,2},{4,5},{5,4},{6,7},{7,6},{8,9},{9,8},{10,11... | collective-permute-start | bytes 221192 | tf_op jit(solution)/shard_map/ppermute | solution.py:567
  36.3 1.8 %collective-permute-start.7 = (bf16[144,256]{1,0:T(8,128)(2,1)S(1)}, bf16[144,256]{1,0:T(8,128)(2,1)S(1)}, u32[]{:S(2)}, u32[]{:S(2)}) collective-permute-start(bf16[144,256]{1,0:T(8,128)(2,1)S(1)} %get-tuple-element.44), channel_id=1, source_target_pairs={{1,2},{2,1},{3,4},{4,3},{5,6},{6,5},{7,8},{8,7},{9,10},{10,9},{11,... | collective-permute-start | bytes 221192 | tf_op jit(solution)/shard_map/ppermute | solution.py:567
  37.0 1.2 %copy-start.4 = (f32[16,16]{1,0:T(8,128)S(1)}, f32[16,16]{1,0:T(8,128)}, u32[]{:S(2)}) copy-start(f32[16,16]{1,0:T(8,128)} %cinv_ref.5) | copy-start | bytes 3076
  39.6 9.1 %collective-permute-start.9 = (bf16[128,256]{1,0:T(8,128)(2,1)S(1)}, bf16[128,256]{1,0:T(8,128)(2,1)S(1)}, u32[]{:S(2)}, u32[]{:S(2)}) collective-permute-start(bf16[128,256]{1,0:T(8,128)(2,1)S(1)} %get-tuple-element.50), channel_id=1, source_target_pairs={{0,1},{1,0},{2,3},{3,2},{4,5},{5,4},{6,7},{7,6},{8,9},{9,8},{10,11... | collective-permute-start | bytes 196616 | tf_op jit(solution)/shard_map/ppermute | solution.py:567
  44.0 4.7 %collective-permute-start.10 = (bf16[128,256]{1,0:T(8,128)(2,1)S(1)}, bf16[128,256]{1,0:T(8,128)(2,1)S(1)}, u32[]{:S(2)}, u32[]{:S(2)}) collective-permute-start(bf16[128,256]{1,0:T(8,128)(2,1)S(1)} %get-tuple-element.51), channel_id=1, source_target_pairs={{1,2},{2,1},{3,4},{4,3},{5,6},{6,5},{7,8},{8,7},{9,10},{10,9},{11,... | collective-permute-start | bytes 196616 | tf_op jit(solution)/shard_map/ppermute | solution.py:567
  49.9 4.3 %collective-permute-start.11 = (f32[184,128]{1,0:T(8,128)S(1)}, f32[184,128]{1,0:T(8,128)S(1)}, u32[]{:S(2)}, u32[]{:S(2)}) collective-permute-start(f32[184,128]{1,0:T(8,128)S(1)} %get-tuple-element.59), channel_id=1, source_target_pairs={{0,1},{1,0},{2,3},{3,2},{4,5},{5,4},{6,7},{7,6},{8,9},{9,8},{10,11... | collective-permute-start | bytes 282632 | tf_op jit(solution)/shard_map/ppermute | solution.py:567
  54.2 3.9 %collective-permute-start.13 = (f32[56,128]{1,0:T(8,128)S(1)}, f32[56,128]{1,0:T(8,128)S(1)}, u32[]{:S(2)}, u32[]{:S(2)}) collective-permute-start(f32[56,128]{1,0:T(8,128)S(1)} %slice_add_fusion), channel_id=1, source_target_pairs={{0,2},{1,3},{2,0},{3,1},{4,6},{5,7},{6,4},{7,5},{8,10},{9,11},{10,... | collective-permute-start | bytes 86024 | tf_op jit(solution)/shard_map/ppermute | solution.py:575
  55.8 8.0 %collective-permute-start.12 = (f32[128,128]{1,0:T(8,128)S(1)}, f32[128,128]{1,0:T(8,128)S(1)}, u32[]{:S(2)}, u32[]{:S(2)}) collective-permute-start(f32[128,128]{1,0:T(8,128)S(1)} %get-tuple-element.60), channel_id=1, source_target_pairs={{1,2},{2,1},{3,4},{4,3},{5,6},{6,5},{7,8},{8,7},{9,10},{10,9},{11,... | collective-permute-start | bytes 196616 | tf_op jit(solution)/shard_map/ppermute | solution.py:567
  58.1 4.0 %collective-permute-start.14 = (f32[56,128]{1,0:T(8,128)S(1)}, f32[56,128]{1,0:T(8,128)S(1)}, u32[]{:S(2)}, u32[]{:S(2)}) collective-permute-start(f32[56,128]{1,0:T(8,128)S(1)} %add.19), channel_id=1, source_target_pairs={{0,4},{1,5},{2,6},{3,7},{4,0},{5,1},{6,2},{7,3},{8,12},{9,13},{10,... | collective-permute-start | bytes 86024 | tf_op jit(solution)/shard_map/ppermute | solution.py:575
  62.1 4.8 %collective-permute-start.15 = (f32[56,128]{1,0:T(8,128)S(1)}, f32[56,128]{1,0:T(8,128)S(1)}, u32[]{:S(2)}, u32[]{:S(2)}) collective-permute-start(f32[56,128]{1,0:T(8,128)S(1)} %add.20.part_in), channel_id=1, source_target_pairs={{0,8},{1,9},{2,10},{3,11},{4,12},{5,13},{6,14},{7,15},{8,0},{9,1},... | collective-permute-start | bytes 86024 | tf_op jit(solution)/shard_map/ppermute | solution.py:575

commit v5 on v4

--- a/solution.py
+++ b/solution.py
@@ -10,7 +10,6 @@
 STRIP = 128
 LANES = 128
 GROUP = 8
-TURNS = 16
 EXTRA = 16
 CHUNKS = 4
 F32 = jnp.float32
@@ -132,63 +131,73 @@
     put_sides(even_ref, odd_ref, side(0), side(own - STRIP))
 
 
-def build_kernel(rows_s, rows_v, lane_v, weight_hbm, o_ref, token, weight_v, sem, *scratch):
-    copy = pltpu.make_async_copy(weight_hbm, weight_v, sem)
-    copy.start()
+def build_kernel(rows_v, lane_v, weight_ref, o_ref, token, *scratch):
     token[...] = jnp.zeros(token.shape, F32)
-    merged, tables = scratch[0], scratch[1:]
+    turned_ref, picked, sem, merged = scratch[:4]
+    tables, lists = scratch[4:6], scratch[6:]
     own, sub = o_ref.shape
     edges = merged.shape[0]
     blocks = edges // LANES
     panels = sub // LANES
     height = panels * own
     chunk = up(-(-height // blocks), 8)
+    group = len(lists) // len(tables)
 
     fill = up(blocks, LANES) - blocks
     turned = jnp.transpose(
         jnp.concatenate([rows_v[...], jnp.zeros((fill, LANES), jnp.int32)], 0)
     )
+    turned_ref[...] = turned
+    turns = LANES // len(lists)
+    copies = []
+    for i, target in enumerate(lists):
+        picked[i] = turned_ref[pl.ds(i, turns, stride=len(lists)), :]
+        copies.append(pltpu.make_async_copy(picked.at[i], target, sem.at[i]))
+        copies[-1].start()
+    weights = weight_ref[...].astype(F32)
     square = (LANES, LANES)
     down, across = iota(square, 0), iota(square, 1)
-    same_group = (down // GROUP) == (across // GROUP)
-    copy.wait()
+    same_group = (down // group) == (across // group)
     for k in range(blocks):
-        low = min(k * chunk, height)
-        high = min(low + chunk, height)
-        if high > low:
-            for acc in tables:
-                acc[low:high, :] = jnp.zeros((high - low, LANES), F32)
         equal = jnp.broadcast_to(turned[:, k : k + 1], square) == jnp.broadcast_to(
             rows_v[k : k + 1, :], square
         )
         equal = jnp.where(equal & same_group, 1.0, 0.0).astype(BF16)
         hit = down == jnp.broadcast_to(lane_v[k : k + 1, :], square)
-        spread = jnp.where(hit, jnp.broadcast_to(weight_v[k : k + 1, :], square), 0.0)
+        spread = jnp.where(hit, jnp.broadcast_to(weights[k : k + 1, :], square), 0.0)
         merged[k * LANES : (k + 1) * LANES, :] = lax.dot_general(
             equal, spread.astype(BF16), NT, preferred_element_type=F32
         )
-
-    def add(g, _):
-        for q in range(TURNS):
-            acc = tables[q % len(tables)]
-            base = (g * TURNS + q) * GROUP
-            at = [rows_s[base + i] for i in range(GROUP)]
-            new = merged[pl.ds(pl.multiple_of(base, GROUP), GROUP), :]
-            out = [acc[pl.ds(at[i], 1), :] + new[i : i + 1, :] for i in range(GROUP)]
-            for i in range(GROUP):
-                acc[pl.ds(at[i], 1), :] = out[i]
+        low = min(k * chunk, height)
+        high = min(low + chunk, height)
+        if high > low:
+            blank = jnp.concatenate([spread[LANES - 8 :, :] * 0.0] * ((high - low) // 8), 0)
+            for acc in tables:
+                acc[low:high, :] = blank
+    for copy in copies:
+        copy.wait()
+
+    def add(k, _):
+        base = k * LANES
+        for j in range(turns):
+            for half, acc in enumerate(tables):
+                first = half * group
+                at = [lists[first + i][j, k] for i in range(group)]
+                start = pl.multiple_of(base + j * len(lists) + first, group)
+                new = merged[pl.ds(start, group), :]
+                out = [acc[pl.ds(at[i], 1), :] + new[i : i + 1, :] for i in range(group)]
+                for i in range(group):
+                    acc[pl.ds(at[i], 1), :] = out[i]
         return 0
 
-    lax.fori_loop(0, edges // (GROUP * TURNS), add, 0)
+    lax.fori_loop(0, blocks, add, 0)
 
     tall = 256
 
     def narrow(i, _):
         for p in range(panels):
             rows = pl.ds(pl.multiple_of(p * own + i * tall, tall), tall)
-            value = tables[0][rows, :]
-            for acc in tables[1:]:
-                value = value + acc[rows, :]
+            value = tables[0][rows, :] + tables[1][rows, :]
             o_ref[pl.ds(pl.multiple_of(i * tall, tall), tall), p * LANES : (p + 1) * LANES] = (
                 value.astype(BF16)
             )
@@ -595,7 +604,6 @@
     slots = up(n, 8)
     cvec, mass = coarse_vec.reshape(-1, LANES), mass_diag.reshape(-1, LANES)
     vmem = pl.BlockSpec(memory_space=pltpu.VMEM)
-    smem = pl.BlockSpec(memory_space=pltpu.SMEM)
     bind = functools.partial
 
     side = ((rows + 8 + slots, STRIP), F32)
@@ -614,16 +622,23 @@
 
     at = (edge_tails >> 7) * own + (edge_heads - STRIP)
     shape = (edges // LANES, LANES)
+    weight = jnp.where(edge_tails >= 0, edge_weight, 0.0).astype(BF16)
+    lists = 2 * GROUP
     stiff, token = call(
         build_kernel,
         [((own, sub), BF16), ((8, LANES), F32)],
-        [pltpu.VMEM(shape, F32), pltpu.SemaphoreType.DMA, pltpu.VMEM((edges, LANES), F32)]
-        + [pltpu.VMEM((sub // LANES * own, LANES), F32)] * 2,
+        [
+            pltpu.VMEM((LANES, LANES), jnp.int32),
+            pltpu.VMEM((lists, LANES // lists, LANES), jnp.int32),
+            pltpu.SemaphoreType.DMA((lists,)),
+            pltpu.VMEM((edges, LANES), F32),
+        ]
+        + [pltpu.VMEM((sub // LANES * own, LANES), F32)] * 2
+        + [pltpu.SMEM((LANES // lists, LANES), jnp.int32)] * lists,
         34,
-        4,
-        in_specs=[smem, vmem, vmem, hbm],
+        3,
         flops=10**10,
-    )(at, at.reshape(shape), (edge_tails & 127).reshape(shape), edge_weight.reshape(shape))
+    )(at.reshape(shape), (edge_tails & 127).reshape(shape), weight.reshape(shape))
 
     whole, owned = ((rows, sub), F32), ((rows, own), F32)
     strip = ((rows, 2 * STRIP), BF16)

time: 69.5 us -> 68.2 us (0.981)
  Pallas kernels: 28.1 us -> 26.9 us
  local copies, waits for them, and re-layouts: 2.8 us -> 1.9 us
  other arithmetic: 0.8 us -> 1.57 us
    pallas_call x1, Pallas kernels: 12.6 us -> 11.4 us  [shards(): call(build_kernel, [((own, sub), BF16), ((8, LANES), F32)], [pltpu.VMEM((...]
    unnamed x18 -> x16, local copies, waits for them, and re-layouts: 2.8 us -> 1.9 us
    reshape x0 -> x1, other arithmetic: none -> 0.77 us  [shards(): weight.reshape(shape)]
  transfers between devices with their start and end apart: 16 -> 16, of which waited for: 4 -> 4; matrix products, arithmetic and copies ran while one was open for 1% -> 2% of each run, Pallas kernels for 30% -> 28%
where the time goes in v5:
time: 68.2 us; the launch traced here: 67.8 us
  starting transfers between devices  28 us (41%)
  Pallas kernels  26.9 us (39%)
  waiting for transfers between devices  8.44 us (12%)
  local copies, waits for them, and re-layouts  1.9 us (3%)
  other arithmetic  1.57 us (2%)
  between operations  1.08 us (2%)
    ppermute x6, starting transfers between devices, across(): return lax.ppermute(part, 'tile', [(i, i ^ hop) for i in range(n)])  15.7 us
    ppermute x10, starting transfers between devices, swap(): got.append(lax.ppermute(payload, 'tile', links))  12.2 us
    pallas_call x1, Pallas kernels, shards(): call(build_kernel, [((own, sub), BF16), ((8, LANES), F32)], [pltpu.VMEM((...  11.4 us
    ppermute x6, waiting for transfers between devices, across(): return lax.ppermute(part, 'tile', [(i, i ^ hop) for i in range(n)])  7.48 us
    pallas_call x1, Pallas kernels, shards(): call(next_inner_kernel, [whole, ((rows, LANES), F32)], [], 8, 5, flops=2...  3.1 us
    pallas_call x1, Pallas kernels, shards(): call(first_inner_kernel, [extra], [], 8, 3, flops=2 * 10 ** 9)  2.87 us
    pallas_call x1, Pallas kernels, shards(): call(bind(finish_kernel, n), [owned, owned], [pltpu.VMEM(*owned)] * 2 + [...  2.1 us
    unnamed x16, local copies, waits for them, and re-layouts  1.9 us
  transfers between devices with their start and end apart: 16, of which 4 were waited for; matrix products, arithmetic and copies ran while one was open for 2% of the time, Pallas kernels for 28%

profile of v5, /device:TPU:0, one launch (start us, length us, event | category | flops | bytes accessed | tf_op | source)
XLA Modules:
  0.0 67.8 jit_solution(6558359947795345688)
XLA Ops:
  0.6 1.2 %copy-done = f32[128,1792]{1,0:T(8,128)S(1)} copy-done((f32[128,1792]{1,0:T(8,128)S(1)}, f32[128,1792]{1,0:T(8,128)}, u32[]{:S(2)}) %copy-start) | copy-done | bytes 917528
  1.8 0.7 %copy-done.2 = f32[1792]{0:T(1024)S(1)} copy-done((f32[1792]{0:T(1024)S(1)}, f32[1792]{0:T(1024)}, u32[]{:S(2)}) %copy-start.2) | copy-done | bytes 7192
  3.0 0.6 collective-permute-start
  3.5 0.7 collective-permute-start.1
  4.2 0.8 %and_bitcast_fusion = (s32[56,128]{1,0:T(8,128)S(1)}, s32[56,128]{1,0:T(8,128)S(1)}) fusion(s32[7168]{0:T(1024)} %param.11, s32[7168]{0:T(1024)} %param.10), kind=kLoop, calls=%fused_computation.2 | loop fusion | flops 35840 | bytes 114688 | tf_op jit(solution)/shard_map/reshape | solution.py:641
  5.0 0.8 %fusion.weight_ref = bf16[56,128]{1,0:T(8,128)(2,1)S(1)} fusion(f32[7168]{0:T(1024)} %param.12, s32[7168]{0:T(1024)} %param.11), kind=kLoop, calls=%fused_computation.4 | loop fusion | flops 14336 | bytes 71680 | tf_op jit(solution)/shard_map/reshape | solution.py:641
  5.7 3.8 %collective-permute-start.2 = (f32[16,128]{1,0:T(8,128)S(1)}, f32[16,128]{1,0:T(8,128)S(1)}, u32[]{:S(2)}, u32[]{:S(2)}) collective-permute-start(f32[16,128]{1,0:T(8,128)S(1)} %slice_add_fusion.1.sum_ref), channel_id=1, source_target_pairs={{0,2},{1,3},{2,0},{3,1},{4,6},{5,7},{6,4},{7,5},{8,10},{9,11},{10,... | collective-permute-start | bytes 24584 | tf_op jit(solution)/shard_map/ppermute | solution.py:584
  9.6 11.4 %shard_map.96 = (bf16[1792,2048]{1,0:T(8,128)(2,1)S(1)}, f32[8,128]{1,0:T(8,128)S(1)}) custom-call(s32[56,128]{1,0:T(8,128)S(1)} %get-tuple-element.63.rows_v, s32[56,128]{1,0:T(8,128)S(1)} %get-tuple-element.62.lane_v, bf16[56,128]{1,0:T(8,128)(2,1)S(1)} %fusion.weight_ref), custom_call_target="tpu_custom_call" | custom-call | flops 10000000000 | tf_op jit(solution)/shard_map/pallas_call | solution.py:627
  21.1 1.3 %shard_map.97 = (f32[128,2048]{1,0:T(8,128)S(1)}, bf16[128,256]{1,0:T(8,128)(2,1)S(1)}, bf16[128,256]{1,0:T(8,128)(2,1)S(1)}, f32[16,128]{1,0:T(8,128)S(1)}) custom-call(f32[128,1792]{1,0:T(8,128)S(1)} %copy-done.1, f32[152,128]{1,0:T(8,128)S(1)} %collective-permute-done.even_got.halo_even, f32[152,128]{1,0:T(8,128)S(1)} %collective-permute-done.1.odd_got.halo_odd, ...), custom_call_target="tpu_custom_call" | custom-call | flops 1000000000 | tf_op jit(solution)/shard_map/pallas_call | solution.py:646
  22.4 2.2 %collective-permute-start.5 = (f32[16,128]{1,0:T(8,128)S(1)}, f32[16,128]{1,0:T(8,128)S(1)}, u32[]{:S(2)}, u32[]{:S(2)}) collective-permute-start(f32[16,128]{1,0:T(8,128)S(1)} %get-tuple-element.40.sum_ref), channel_id=1, source_target_pairs={{0,4},{1,5},{2,6},{3,7},{4,0},{5,1},{6,2},{7,3},{8,12},{9,13},{10,... | collective-permute-start | bytes 24584 | tf_op jit(solution)/shard_map/ppermute | solution.py:584
  25.1 0.7 collective-permute-start.4
  25.8 2.9 %shard_map.98.thru_ref = f32[144,2048]{1,0:T(8,128)S(1)} custom-call(f32[128,2048]{1,0:T(8,128)S(1)} %get-tuple-element.36.u_ref, bf16[1792,2048]{1,0:T(8,128)(2,1)S(1)} %get-tuple-element.39.o_ref, f32[14,128]{1,0:T(8,128)S(1)} %bitcast.11), custom_call_target="tpu_custom_call" | custom-call | flops 2000000000 | tf_op jit(solution)/shard_map/pallas_call | solution.py:650
  28.7 1.1 %shard_map.99 = (f32[128,1792]{1,0:T(8,128)S(1)}, f32[144,2048]{1,0:T(8,128)S(1)}, f32[8,2048]{1,0:T(8,128)S(1)}, bf16[144,256]{1,0:T(8,128)(2,1)S(1)}, bf16[144...) custom-call(f32[128,2048]{1,0:T(8,128)S(1)} %get-tuple-element.36.u_ref, ...), custom_call_target="tpu_custom_call" | custom-call | flops 1000000000 | tf_op jit(solution)/shard_map/pallas_call | solution.py:654
  29.9 5.1 %collective-permute-start.8 = (f32[16,128]{1,0:T(8,128)S(1)}, f32[16,128]{1,0:T(8,128)S(1)}, u32[]{:S(2)}, u32[]{:S(2)}) collective-permute-start(f32[16,128]{1,0:T(8,128)S(1)} %get-tuple-element.45.sum_ref), channel_id=1, source_target_pairs={{0,8},{1,9},{2,10},{3,11},{4,12},{5,13},{6,14},{7,15},{8,0},{9,1},... | collective-permute-start | bytes 24584 | tf_op jit(solution)/shard_map/ppermute | solution.py:584
  35.0 0.7 collective-permute-start.7
  35.7 1.1 %shard_map.100.half_ref = f32[144,2048]{1,0:T(8,128)S(1)} custom-call(f32[144,2048]{1,0:T(8,128)S(1)} %get-tuple-element.42.y_ref.coarse_rows, bf16[2048,2048]{1,0:T(8,128)(2,1)S(1)} %bitcast.9), custom_call_target="tpu_custom_call" | custom-call | flops 1000000000 | tf_op jit(solution)/shard_map/pallas_call | solution.py:663
  36.9 1.4 %shard_map.101 = (f32[128,1792]{1,0:T(8,128)S(1)}, f32[128,2048]{1,0:T(8,128)S(1)}, bf16[128,256]{1,0:T(8,128)(2,1)S(1)}, bf16[128,256]{1,0:T(8,128)(2,1)S(1)}, f32[16,128]{1,0:T(8,128)S(1)}) custom-call(f32[144,2048]{1,0:T(8,128)S(1)} %get-tuple-element.42.y_ref.coarse_rows, bf16[144,256]{1,0:T(8,128)(2,1)S(1)} %collective-permute-done.6.even_got, ...), custom_call_target="tpu_custom_call" | custom-call | flops 100000000 | tf_op jit(solution)/shard_map/pallas_call | solution.py:664
  38.3 4.4 %collective-permute-start.9 = (bf16[128,256]{1,0:T(8,128)(2,1)S(1)}, bf16[128,256]{1,0:T(8,128)(2,1)S(1)}, u32[]{:S(2)}, u32[]{:S(2)}) collective-permute-start(bf16[128,256]{1,0:T(8,128)(2,1)S(1)} %get-tuple-element.50), channel_id=1, source_target_pairs={{0,1},{1,0},{2,3},{3,2},{4,5},{5,4},{6,7},{7,6},{8,9},{9,8},{10,11... | collective-permute-start | bytes 196616 | tf_op jit(solution)/shard_map/ppermute | solution.py:576
  42.6 0.8 %collective-permute-start.10 = (bf16[128,256]{1,0:T(8,128)(2,1)S(1)}, bf16[128,256]{1,0:T(8,128)(2,1)S(1)}, u32[]{:S(2)}, u32[]{:S(2)}) collective-permute-start(bf16[128,256]{1,0:T(8,128)(2,1)S(1)} %get-tuple-element.51), channel_id=1, source_target_pairs={{1,2},{2,1},{3,4},{4,3},{5,6},{6,5},{7,8},{8,7},{9,10},{10,9},{11,... | collective-permute-start | bytes 196616 | tf_op jit(solution)/shard_map/ppermute | solution.py:576
  43.5 0.7 %shard_map.102 = (f32[128,1792]{1,0:T(8,128)S(1)}, f32[8,1792]{1,0:T(8,128)S(1)}, f32[40,128]{1,0:T(8,128)S(1)}) custom-call(f32[128,1792]{1,0:T(8,128)S(1)} %get-tuple-element.41.s_ref, f32[128,1792]{1,0:T(8,128)S(1)} %get-tuple-element.46.y_ref, f32[144,2048]{1,0:T(8,128)S(1)} %get-tuple-element.42.y_ref.coarse_rows, ...), custom_call_target="tpu_custom_call" | custom-call | flops 1000000000 | tf_op jit(solution)/shard_map/pallas_call | solution.py:668
  44.2 3.1 %shard_map.103 = (f32[128,2048]{1,0:T(8,128)S(1)}, f32[128,128]{1,0:T(8,128)S(1)}) custom-call(f32[128,2048]{1,0:T(8,128)S(1)} %get-tuple-element.49.u_ref, bf16[1792,2048]{1,0:T(8,128)(2,1)S(1)} %get-tuple-element.39.o_ref, f32[128,1792]{1,0:T(8,128)S(1)} %copy-done.1, f32[128,1792]{1,0:T(8,128)S(1)} %get-tuple-element.46.y_ref, ...), custom_call_target="tpu_custom_call" | custom-call | flops 2000000000 | tf_op jit(solution)/shard_map/pallas_call | solution.py:676
  47.3 1.2 %shard_map.104 = (f32[128,1792]{1,0:T(8,128)S(1)}, f32[128,1792]{1,0:T(8,128)S(1)}, f32[184,128]{1,0:T(8,128)S(1)}, f32[128,128]{1,0:T(8,128)S(1)}, f32[56,128]{1,0:T(8,128)S(1)}) custom-call(f32[128,2048]{1,0:T(8,128)S(1)} %get-tuple-element.49.u_ref, bf16[128,256]{1,0:T(8,128)(2,1)S(1)} %collective-permute-done.9.even_got, ...), custom_call_target="tpu_custom_call" | custom-call | flops 1000000000 | tf_op jit(solution)/shard_map/pallas_call | solution.py:680
  48.6 3.3 %collective-permute-start.11 = (f32[184,128]{1,0:T(8,128)S(1)}, f32[184,128]{1,0:T(8,128)S(1)}, u32[]{:S(2)}, u32[]{:S(2)}) collective-permute-start(f32[184,128]{1,0:T(8,128)S(1)} %get-tuple-element.59), channel_id=1, source_target_pairs={{0,1},{1,0},{2,3},{3,2},{4,5},{5,4},{6,7},{7,6},{8,9},{9,8},{10,11... | collective-permute-start | bytes 282632 | tf_op jit(solution)/shard_map/ppermute | solution.py:576
  51.9 0.9 %collective-permute-done.11.even_got = f32[184,128]{1,0:T(8,128)S(1)} collective-permute-done((f32[184,128]{1,0:T(8,128)S(1)}, f32[184,128]{1,0:T(8,128)S(1)}, u32[]{:S(2)}, u32[]{:S(2)}) %collective-permute-start.11) | collective-permute-done | bytes 94240 | tf_op jit(solution)/shard_map/ppermute | solution.py:576
  52.8 1.6 %collective-permute-start.13 = (f32[56,128]{1,0:T(8,128)S(1)}, f32[56,128]{1,0:T(8,128)S(1)}, u32[]{:S(2)}, u32[]{:S(2)}) collective-permute-start(f32[56,128]{1,0:T(8,128)S(1)} %slice_add_fusion), channel_id=1, source_target_pairs={{0,2},{1,3},{2,0},{3,1},{4,6},{5,7},{6,4},{7,5},{8,10},{9,11},{10,... | collective-permute-start | bytes 86024 | tf_op jit(solution)/shard_map/ppermute | solution.py:584
  54.4 0.7 collective-permute-start.12
  55.1 1.6 %collective-permute-done.13 = f32[56,128]{1,0:T(8,128)S(1)} collective-permute-done((f32[56,128]{1,0:T(8,128)S(1)}, f32[56,128]{1,0:T(8,128)S(1)}, u32[]{:S(2)}, u32[]{:S(2)}) %collective-permute-start.13) | collective-permute-done | bytes 28704 | tf_op jit(solution)/shard_map/ppermute | solution.py:584
  56.7 1.3 %collective-permute-start.14 = (f32[56,128]{1,0:T(8,128)S(1)}, f32[56,128]{1,0:T(8,128)S(1)}, u32[]{:S(2)}, u32[]{:S(2)}) collective-permute-start(f32[56,128]{1,0:T(8,128)S(1)} %add.19), channel_id=1, source_target_pairs={{0,4},{1,5},{2,6},{3,7},{4,0},{5,1},{6,2},{7,3},{8,12},{9,13},{10,... | collective-permute-start | bytes 86024 | tf_op jit(solution)/shard_map/ppermute | solution.py:584
  58.0 2.7 %collective-permute-done.14 = f32[56,128]{1,0:T(8,128)S(1)} collective-permute-done((f32[56,128]{1,0:T(8,128)S(1)}, f32[56,128]{1,0:T(8,128)S(1)}, u32[]{:S(2)}, u32[]{:S(2)}) %collective-permute-start.14) | collective-permute-done | bytes 28704 | tf_op jit(solution)/shard_map/ppermute | solution.py:584
  60.8 1.7 %collective-permute-start.15 = (f32[56,128]{1,0:T(8,128)S(1)}, f32[56,128]{1,0:T(8,128)S(1)}, u32[]{:S(2)}, u32[]{:S(2)}) collective-permute-start(f32[56,128]{1,0:T(8,128)S(1)} %add.20.part_in), channel_id=1, source_target_pairs={{0,8},{1,9},{2,10},{3,11},{4,12},{5,13},{6,14},{7,15},{8,0},{9,1},... | collective-permute-start | bytes 86024 | tf_op jit(solution)/shard_map/ppermute | solution.py:584
  62.4 3.1 %collective-permute-done.15.more_ref = f32[56,128]{1,0:T(8,128)S(1)} collective-permute-done((f32[56,128]{1,0:T(8,128)S(1)}, f32[56,128]{1,0:T(8,128)S(1)}, u32[]{:S(2)}, u32[]{:S(2)}) %collective-permute-start.15) | collective-permute-done | bytes 28704 | tf_op jit(solution)/shard_map/ppermute | solution.py:584
  65.5 2.1 %shard_map.105 = (f32[128,1792]{1,0:T(8,128)}, f32[128,1792]{1,0:T(8,128)}) custom-call(f32[128,1792]{1,0:T(8,128)S(1)} %copy-done.1, f32[128,1792]{1,0:T(8,128)S(1)} %get-tuple-element.48.z_ref, f32[128,1792]{1,0:T(8,128)S(1)} %get-tuple-element.46.y_ref, f32[128,1792]{1,0:T(8,128)S(1)} %get-tuple-element.57.w_ref, ...), custom_call_target="tpu_custom_call" | custom-call | tf_op jit(solution)/shard_map/pallas_call | solution.py:691
  (34 shorter events, 1.0 us)
Async XLA Ops:
  0.6 1.2 %copy-start = (f32[128,1792]{1,0:T(8,128)S(1)}, f32[128,1792]{1,0:T(8,128)}, u32[]{:S(2)}) copy-start(f32[128,1792]{1,0:T(8,128)} %rhs_ref.9) | copy-start | bytes 2752516
  1.8 0.7 %copy-start.2 = (f32[1792]{0:T(1024)S(1)}, f32[1792]{0:T(1024)}, u32[]{:S(2)}) copy-start(f32[1792]{0:T(1024)} %param.14) | copy-start | bytes 21508
  3.0 2.8 %collective-permute-start = (f32[152,128]{1,0:T(8,128)S(1)}, f32[152,128]{1,0:T(8,128)S(1)}, u32[]{:S(2)}, u32[]{:S(2)}) collective-permute-start(f32[152,128]{1,0:T(8,128)S(1)} %get-tuple-element.32), channel_id=1, source_target_pairs={{0,1},{1,0},{2,3},{3,2},{4,5},{5,4},{6,7},{7,6},{8,9},{9,8},{10,11... | collective-permute-start | bytes 233480 | tf_op jit(solution)/shard_map/ppermute | solution.py:576
  3.5 17.5 %collective-permute-start.1 = (f32[152,128]{1,0:T(8,128)S(1)}, f32[152,128]{1,0:T(8,128)S(1)}, u32[]{:S(2)}, u32[]{:S(2)}) collective-permute-start(f32[152,128]{1,0:T(8,128)S(1)} %get-tuple-element.33), channel_id=1, source_target_pairs={{1,2},{2,1},{3,4},{4,3},{5,6},{6,5},{7,8},{8,7},{9,10},{10,9},{11,... | collective-permute-start | bytes 233480 | tf_op jit(solution)/shard_map/ppermute | solution.py:576
  5.7 15.3 %collective-permute-start.2 = (f32[16,128]{1,0:T(8,128)S(1)}, f32[16,128]{1,0:T(8,128)S(1)}, u32[]{:S(2)}, u32[]{:S(2)}) collective-permute-start(f32[16,128]{1,0:T(8,128)S(1)} %slice_add_fusion.1.sum_ref), channel_id=1, source_target_pairs={{0,2},{1,3},{2,0},{3,1},{4,6},{5,7},{6,4},{7,5},{8,10},{9,11},{10,... | collective-permute-start | bytes 24584 | tf_op jit(solution)/shard_map/ppermute | solution.py:584
  9.6 11.5 %slice-start = ((s8[8388608]{0:T(1024)(128)(4,1)}), s8[4194304]{0:T(1024)(128)(4,1)S(1)}, s32[]{:S(2)}) async-start(s8[8388608]{0:T(1024)(128)(4,1)} %bitcast.8), calls=%async_computation | async-start | bytes 8388608
  9.6 11.5 %slice-start.1 = ((s8[8388608]{0:T(1024)(128)(4,1)}), s8[4194304]{0:T(1024)(128)(4,1)S(1)}, s32[]{:S(2)}) async-start(s8[8388608]{0:T(1024)(128)(4,1)} %bitcast.8), calls=%async_computation.1 | async-start | bytes 8388608
  9.6 11.5 %copy-start.1 = (f32[128,1792]{1,0:T(8,128)S(1)}, f32[128,1792]{1,0:T(8,128)}, u32[]{:S(2)}) copy-start(f32[128,1792]{1,0:T(8,128)} %rhs_ref.9) | copy-start | bytes 2752516
  21.1 4.7 %copy-start.3 = (f32[1792]{0:T(1024)S(1)}, f32[1792]{0:T(1024)}, u32[]{:S(2)}) copy-start(f32[1792]{0:T(1024)} %param.14) | copy-start | bytes 21508
  22.4 6.3 %collective-permute-start.5 = (f32[16,128]{1,0:T(8,128)S(1)}, f32[16,128]{1,0:T(8,128)S(1)}, u32[]{:S(2)}, u32[]{:S(2)}) collective-permute-start(f32[16,128]{1,0:T(8,128)S(1)} %get-tuple-element.40.sum_ref), channel_id=1, source_target_pairs={{0,4},{1,5},{2,6},{3,7},{4,0},{5,1},{6,2},{7,3},{8,12},{9,13},{10,... | collective-permute-start | bytes 24584 | tf_op jit(solution)/shard_map/ppermute | solution.py:584
  24.6 4.1 %collective-permute-start.3 = (bf16[128,256]{1,0:T(8,128)(2,1)S(1)}, bf16[128,256]{1,0:T(8,128)(2,1)S(1)}, u32[]{:S(2)}, u32[]{:S(2)}) collective-permute-start(bf16[128,256]{1,0:T(8,128)(2,1)S(1)} %get-tuple-element.37), channel_id=1, source_target_pairs={{0,1},{1,0},{2,3},{3,2},{4,5},{5,4},{6,7},{7,6},{8,9},{9,8},{10,11... | collective-permute-start | bytes 196616 | tf_op jit(solution)/shard_map/ppermute | solution.py:576
  25.1 3.6 %collective-permute-start.4 = (bf16[128,256]{1,0:T(8,128)(2,1)S(1)}, bf16[128,256]{1,0:T(8,128)(2,1)S(1)}, u32[]{:S(2)}, u32[]{:S(2)}) collective-permute-start(bf16[128,256]{1,0:T(8,128)(2,1)S(1)} %get-tuple-element.38), channel_id=1, source_target_pairs={{1,2},{2,1},{3,4},{4,3},{5,6},{6,5},{7,8},{8,7},{9,10},{10,9},{11,... | collective-permute-start | bytes 196616 | tf_op jit(solution)/shard_map/ppermute | solution.py:576
  25.8 2.9 %copy-start.5 = (f32[1792]{0:T(1024)S(1)}, f32[1792]{0:T(1024)}, u32[]{:S(2)}) copy-start(f32[1792]{0:T(1024)} %param.9) | copy-start | bytes 21508
  29.9 7.0 %collective-permute-start.8 = (f32[16,128]{1,0:T(8,128)S(1)}, f32[16,128]{1,0:T(8,128)S(1)}, u32[]{:S(2)}, u32[]{:S(2)}) collective-permute-start(f32[16,128]{1,0:T(8,128)S(1)} %get-tuple-element.45.sum_ref), channel_id=1, source_target_pairs={{0,8},{1,9},{2,10},{3,11},{4,12},{5,13},{6,14},{7,15},{8,0},{9,1},... | collective-permute-start | bytes 24584 | tf_op jit(solution)/shard_map/ppermute | solution.py:584
  35.0 1.8 %collective-permute-start.6 = (bf16[144,256]{1,0:T(8,128)(2,1)S(1)}, bf16[144,256]{1,0:T(8,128)(2,1)S(1)}, u32[]{:S(2)}, u32[]{:S(2)}) collective-permute-start(bf16[144,256]{1,0:T(8,128)(2,1)S(1)} %get-tuple-element.43), channel_id=1, source_target_pairs={{0,1},{1,0},{2,3},{3,2},{4,5},{5,4},{6,7},{7,6},{8,9},{9,8},{10,11... | collective-permute-start | bytes 221192 | tf_op jit(solution)/shard_map/ppermute | solution.py:576
  35.0 1.8 %collective-permute-start.7 = (bf16[144,256]{1,0:T(8,128)(2,1)S(1)}, bf16[144,256]{1,0:T(8,128)(2,1)S(1)}, u32[]{:S(2)}, u32[]{:S(2)}) collective-permute-start(bf16[144,256]{1,0:T(8,128)(2,1)S(1)} %get-tuple-element.44), channel_id=1, source_target_pairs={{1,2},{2,1},{3,4},{4,3},{5,6},{6,5},{7,8},{8,7},{9,10},{10,9},{11,... | collective-permute-start | bytes 221192 | tf_op jit(solution)/shard_map/ppermute | solution.py:576
  35.7 1.2 %copy-start.4 = (f32[16,16]{1,0:T(8,128)S(1)}, f32[16,16]{1,0:T(8,128)}, u32[]{:S(2)}) copy-start(f32[16,16]{1,0:T(8,128)} %cinv_ref.5) | copy-start | bytes 3076
  38.3 9.1 %collective-permute-start.9 = (bf16[128,256]{1,0:T(8,128)(2,1)S(1)}, bf16[128,256]{1,0:T(8,128)(2,1)S(1)}, u32[]{:S(2)}, u32[]{:S(2)}) collective-permute-start(bf16[128,256]{1,0:T(8,128)(2,1)S(1)} %get-tuple-element.50), channel_id=1, source_target_pairs={{0,1},{1,0},{2,3},{3,2},{4,5},{5,4},{6,7},{7,6},{8,9},{9,8},{10,11... | collective-permute-start | bytes 196616 | tf_op jit(solution)/shard_map/ppermute | solution.py:576
  42.6 4.7 %collective-permute-start.10 = (bf16[128,256]{1,0:T(8,128)(2,1)S(1)}, bf16[128,256]{1,0:T(8,128)(2,1)S(1)}, u32[]{:S(2)}, u32[]{:S(2)}) collective-permute-start(bf16[128,256]{1,0:T(8,128)(2,1)S(1)} %get-tuple-element.51), channel_id=1, source_target_pairs={{1,2},{2,1},{3,4},{4,3},{5,6},{6,5},{7,8},{8,7},{9,10},{10,9},{11,... | collective-permute-start | bytes 196616 | tf_op jit(solution)/shard_map/ppermute | solution.py:576
  48.6 4.3 %collective-permute-start.11 = (f32[184,128]{1,0:T(8,128)S(1)}, f32[184,128]{1,0:T(8,128)S(1)}, u32[]{:S(2)}, u32[]{:S(2)}) collective-permute-start(f32[184,128]{1,0:T(8,128)S(1)} %get-tuple-element.59), channel_id=1, source_target_pairs={{0,1},{1,0},{2,3},{3,2},{4,5},{5,4},{6,7},{7,6},{8,9},{9,8},{10,11... | collective-permute-start | bytes 282632 | tf_op jit(solution)/shard_map/ppermute | solution.py:576
  52.8 3.9 %collective-permute-start.13 = (f32[56,128]{1,0:T(8,128)S(1)}, f32[56,128]{1,0:T(8,128)S(1)}, u32[]{:S(2)}, u32[]{:S(2)}) collective-permute-start(f32[56,128]{1,0:T(8,128)S(1)} %slice_add_fusion), channel_id=1, source_target_pairs={{0,2},{1,3},{2,0},{3,1},{4,6},{5,7},{6,4},{7,5},{8,10},{9,11},{10,... | collective-permute-start | bytes 86024 | tf_op jit(solution)/shard_map/ppermute | solution.py:584
  54.4 8.0 %collective-permute-start.12 = (f32[128,128]{1,0:T(8,128)S(1)}, f32[128,128]{1,0:T(8,128)S(1)}, u32[]{:S(2)}, u32[]{:S(2)}) collective-permute-start(f32[128,128]{1,0:T(8,128)S(1)} %get-tuple-element.60), channel_id=1, source_target_pairs={{1,2},{2,1},{3,4},{4,3},{5,6},{6,5},{7,8},{8,7},{9,10},{10,9},{11,... | collective-permute-start | bytes 196616 | tf_op jit(solution)/shard_map/ppermute | solution.py:576
  56.7 4.0 %collective-permute-start.14 = (f32[56,128]{1,0:T(8,128)S(1)}, f32[56,128]{1,0:T(8,128)S(1)}, u32[]{:S(2)}, u32[]{:S(2)}) collective-permute-start(f32[56,128]{1,0:T(8,128)S(1)} %add.19), channel_id=1, source_target_pairs={{0,4},{1,5},{2,6},{3,7},{4,0},{5,1},{6,2},{7,3},{8,12},{9,13},{10,... | collective-permute-start | bytes 86024 | tf_op jit(solution)/shard_map/ppermute | solution.py:584
  60.8 4.8 %collective-permute-start.15 = (f32[56,128]{1,0:T(8,128)S(1)}, f32[56,128]{1,0:T(8,128)S(1)}, u32[]{:S(2)}, u32[]{:S(2)}) collective-permute-start(f32[56,128]{1,0:T(8,128)S(1)} %add.20.part_in), channel_id=1, source_target_pairs={{0,8},{1,9},{2,10},{3,11},{4,12},{5,13},{6,14},{7,15},{8,0},{9,1},... | collective-permute-start | bytes 86024 | tf_op jit(solution)/shard_map/ppermute | solution.py:584
